TPU v7x, 32 devices: a whole 2x2x4 slice. The times are simulated.
32 devices in a mesh: lat: 4 (over z), lon: 8 (over y, x, core).
Axes of the slice: x: 2, y: 2, z: 4, core: 2. Of those that a mesh axis runs over, the one named last changes fastest.
Arguments:
- obs_pert: bfloat16 [2048, 64, 128], P(('lat', 'lon')), may hold values from -6 to 6
- obs_dep: bfloat16 [2048, 64], P(('lat', 'lon')), may hold values from -6 to 6
- obs_prec: bfloat16 [2048, 64], P(('lat', 'lon')), may hold values from 0.25 to 4
- obs_count: int32 [2048], P(('lat', 'lon')), may hold values from 16 to 64
- owner_point: int32 [2048], P(('lat', 'lon')), may hold values from 0 to 2047, as said below
- anomalies: bfloat16 [1, 800, 1600, 128], P(None, 'lat', 'lon'), may hold values from -6 to 6
- flux_mean: float32 [1, 800, 1600], P(None, 'lat', 'lon'), may hold values from -6 to 6
Outputs:
- analysis_anomalies: bfloat16 [1, 800, 1600, 128], P(None, 'lat', 'lon')
- analysis_mean: float32 [1, 800, 1600], P(None, 'lat', 'lon')
Inputs may be any that keep to these rules, and one draw needn't show every extreme that they name: owner_point is a permutation of the 2048 coarse point numbers. Of the 64 blocks held by one device, at most 2 belong to points of the tiles of any one device, and exactly 2 for some; every device's tiles get the blocks of all their points.
All inputs are finite; a program needn't handle non-finite values.
Results may differ from a plain program's by a relative error of at most 0.0032.
Values may be sent and summed in bfloat16 or wider, within the bound.
No kernel may reach another device: no remote copies, remote signals or barrier semaphores. Data moves between devices by JAX's collectives and lax.ppermute only.
A program may use at most 256 MiB of HBM per device.

v0:
```python
import math

import jax
import jax.numpy as jnp
from jax import lax
from jax.sharding import PartitionSpec as P

FINE = 25
TILES_LAT = 8
TILES_LON = 8


def passed_along(value, axis, steps):
    count = lax.axis_size(axis)
    pairs = [(source, (source + steps) % count) for source in range(count)]
    return lax.ppermute(value, axis, pairs)


def shifted_2(shard, axis, by):
    count = lax.axis_size(axis)
    pairs = [(i, i + by) for i in range(count) if 0 <= i + by < count]
    return lax.ppermute(shard, axis, pairs)


def solve_blocks(perturbed, departures, weighting):
    members = perturbed.shape[-1]
    values = perturbed.astype(jnp.float32)
    scaled = values * weighting[:, :, None]
    gram_matrix = jnp.einsum("pik,pim->pkm", scaled, values, precision=lax.Precision.HIGHEST)
    right_side = jnp.einsum(
        "pik,pi->pk", scaled, departures.astype(jnp.float32), precision=lax.Precision.HIGHEST
    )
    identity = jnp.eye(members, dtype=jnp.float32)
    system = gram_matrix + (members - 1.0) * identity
    lower_factor = jnp.linalg.cholesky(system)
    inverse = lax.linalg.triangular_solve(
        lower_factor, jnp.broadcast_to(identity, system.shape), left_side=True, lower=True
    )
    transform = (math.sqrt(members - 1.0) * jnp.swapaxes(inverse, 1, 2)).astype(jnp.bfloat16)
    forward = lax.linalg.triangular_solve(
        lower_factor, right_side[:, :, None], left_side=True, lower=True
    )
    backward = lax.linalg.triangular_solve(
        lower_factor, forward, left_side=True, lower=True, transpose_a=True
    )
    return (transform, backward[:, :, 0].astype(jnp.bfloat16))


def plan_routes(point_ids, devices, capacity, columns, lon_devices):
    point_row = point_ids // columns
    point_col = point_ids % columns
    target_dev = point_row // TILES_LAT * lon_devices + point_col // TILES_LON
    within = point_row % TILES_LAT * TILES_LON + point_col % TILES_LON
    ordinal = jnp.arange(point_ids.shape[0], dtype=jnp.int32)
    earlier = (target_dev[:, None] == target_dev[None, :]) & (ordinal[None, :] < ordinal[:, None])
    slot_rank = jnp.sum(earlier.astype(jnp.int32), axis=1)
    position = target_dev * capacity + slot_rank
    places = jnp.arange(devices * capacity, dtype=jnp.int32)
    matches = position[None, :] == places[:, None]
    source_slot = jnp.sum(jnp.where(matches, ordinal[None, :], 0), axis=1)
    filled_slot = jnp.any(matches, axis=1)
    labels = jnp.where(filled_slot, jnp.take(within, source_slot), -1)
    return (source_slot, filled_slot, labels)


def pack_rows(array, source_slot, filled_slot):
    picked = jnp.take(array, source_slot, axis=0)
    keep_mask = filled_slot.reshape((-1,) + (1,) * (array.ndim - 1))
    return jnp.where(keep_mask, picked, jnp.zeros_like(picked))


def unpack_rows(array, labels, wanted):
    ordinal = jnp.arange(labels.shape[0], dtype=jnp.int32)
    targets = jnp.arange(wanted, dtype=jnp.int32)
    chosen = jnp.sum(jnp.where(labels[None, :] == targets[:, None], ordinal[None, :], 0), axis=1)
    return jnp.take(array, chosen, axis=0)


def shards(obs_pert, obs_dep, obs_prec, obs_count, owner_point, anomalies, flux_mean):
    lat_devices = lax.axis_size("lat")
    lon_devices = lax.axis_size("lon")
    devices = lat_devices * lon_devices
    holding = owner_point.shape[0]
    capacity = max(1, (holding + devices - 1) // devices)
    tiles_here = TILES_LAT * TILES_LON
    columns = TILES_LON * lon_devices
    slot_total = obs_dep.shape[1]
    live_slot = jnp.arange(slot_total, dtype=jnp.int32)[None, :] < obs_count[:, None]
    source_slot, filled_slot, labels = plan_routes(
        owner_point, devices, capacity, columns, lon_devices
    )
    weighting = jnp.where(live_slot, obs_prec.astype(jnp.float32), jnp.zeros((), jnp.float32))
    transform, mean_weight = solve_blocks(obs_pert, obs_dep, weighting)
    arrived = (
        lax.all_to_all(
            pack_rows(transform, source_slot, filled_slot),
            ("lat", "lon"),
            split_axis=0,
            concat_axis=0,
            tiled=True,
        ),
        lax.all_to_all(
            pack_rows(mean_weight, source_slot, filled_slot),
            ("lat", "lon"),
            split_axis=0,
            concat_axis=0,
            tiled=True,
        ),
        lax.all_to_all(labels, ("lat", "lon"), split_axis=0, concat_axis=0, tiled=True),
    )
    tile_transform = unpack_rows(arrived[0], arrived[2], tiles_here)
    tile_mean = unpack_rows(arrived[1], arrived[2], tiles_here)
    members = tile_transform.shape[-1]
    grid_transform = tile_transform.reshape(TILES_LAT, TILES_LON, members, members)
    grid_mean = tile_mean.reshape(TILES_LAT, TILES_LON, members)
    east_edge = passed_along((grid_transform[:, :1], grid_mean[:, :1]), "lon", -1)
    wide_transform = jnp.concatenate([grid_transform, east_edge[0]], axis=1)
    wide_mean = jnp.concatenate([grid_mean, east_edge[1]], axis=1)
    north_edge = shifted_2((wide_transform[:1], wide_mean[:1]), "lat", -1)
    is_top = lax.axis_index("lat") == lat_devices - 1
    full_transform = jnp.concatenate(
        [wide_transform, jnp.where(is_top, wide_transform[-1:], north_edge[0])], axis=0
    )
    full_mean = jnp.concatenate(
        [wide_mean, jnp.where(is_top, wide_mean[-1:], north_edge[1])], axis=0
    )
    lag_total, rows_here, cols_here, member_total = anomalies.shape
    anomaly_field = anomalies.reshape(lag_total, TILES_LAT, FINE, TILES_LON, FINE, member_total)
    fraction = jnp.arange(FINE, dtype=jnp.float32) / FINE
    corner_sets = [
        (full_transform[:-1, :-1], full_mean[:-1, :-1], 1.0 - fraction, 1.0 - fraction),
        (full_transform[:-1, 1:], full_mean[:-1, 1:], 1.0 - fraction, fraction),
        (full_transform[1:, :-1], full_mean[1:, :-1], fraction, 1.0 - fraction),
        (full_transform[1:, 1:], full_mean[1:, 1:], fraction, fraction),
    ]
    summed = jnp.zeros(anomaly_field.shape, jnp.float32)
    shifted = jnp.zeros((lag_total, TILES_LAT, FINE, TILES_LON, FINE), jnp.float32)
    for corner_transform, corner_mean, lat_weight, lon_weight in corner_sets:
        bilinear = lat_weight[None, None, :, None, None] * lon_weight[None, None, None, None, :]
        mixed_part = jnp.einsum(
            "laibjk,abkm->laibjm",
            anomaly_field,
            corner_transform,
            preferred_element_type=jnp.float32,
        )
        summed = summed + bilinear[..., None] * mixed_part
        mean_part = jnp.einsum(
            "laibjk,abk->laibj", anomaly_field, corner_mean, preferred_element_type=jnp.float32
        )
        shifted = shifted + bilinear * mean_part
    analysis = summed.reshape(lag_total, rows_here, cols_here, member_total).astype(jnp.bfloat16)
    return (analysis, flux_mean + shifted.reshape(lag_total, rows_here, cols_here))


def solution(mesh):
    placed = (
        P(("lat", "lon"), None, None),
        P(("lat", "lon"), None),
        P(("lat", "lon"), None),
        P(("lat", "lon")),
        P(("lat", "lon")),
        P(None, "lat", "lon", None),
        P(None, "lat", "lon"),
    )
    return jax.shard_map(
        shards,
        mesh=mesh,
        in_specs=placed,
        out_specs=(P(None, "lat", "lon", None), P(None, "lat", "lon")),
        check_vma=False,
    )
```

profile of v0, /device:TPU:1, one launch (start us, length us, event | category | flops | bytes accessed | tf_op | source)
XLA Modules:
  0.0 1689.2 jit_solution(16332894532987827688)
XLA Ops:
  0.6 0.0 copy-start
  0.6 0.0 copy-start.4
  0.7 0.8 fusion.65
  1.4 0.2 convert_reduce_fusion
  1.6 0.1 select_reduce_fusion.2
  1.7 0.1 fusion.56
  1.9 0.1 reduce_sum.37
  2.0 0.1 reduce_or.12
  2.1 0.8 gather_fusion
  2.9 0.1 gather.13
  3.0 0.6 select_select_fusion.2
  3.6 7.1 all-to-all-start.1
  10.8 0.8 convert_select_fusion
  11.6 7.7 fusion.34
  19.3 1.3 fusion.36
  20.7 0.1 copy.34
  20.8 5.6 copy.35
  26.4 6.8 fusion.12
  33.2 751.8 %custom-call.11 = f32[64,128,128]{2,1,0:T(8,128)} custom-call(f32[64,128,128]{2,1,0:T(8,128)} %fusion.12), custom_call_target="Cholesky" | custom-call | tf_op jit(solution)/shard_map/jit(cholesky)/cholesky | solution.py:35
  785.0 2.9 select_reduce_fusion
  787.9 0.1 compare_reduce_fusion
  788.0 0.4 copy-done.3
  788.5 2.5 select_bitcast_fusion
  791.0 630.5 %custom-call.12 = f32[64,1,128,128]{2,3,1,0:T(8,128)} custom-call(f32[64,1,128,128]{3,2,1,0:T(8,128)} %select_bitcast_fusion), custom_call_target="InvertDiagBlocksLowerTriangular" | custom-call | tf_op jit(solution)/shard_map/triangular_solve | solution.py:36
  1421.6 5.5 fusion.37
  1427.1 6.6 fusion.5
  1433.7 4.1 multiply_convert_fusion
  1437.8 2.1 gather_fusion.1
  1440.0 0.6 gather_fusion.3
  1440.6 3.2 select_select_fusion
  1443.8 0.7 select_select_fusion.1
  1444.5 5.8 all-to-all-start.2
  1450.4 0.5 broadcast.452
  1450.9 0.7 reduce.9
  1451.6 0.1 eq.72
  1451.7 0.1 select_reduce_fusion.1
  1451.8 5.3 all-to-all-done.2
  1457.2 3.0 all-to-all-start
  1460.2 0.6 gather_fusion.4
  1460.8 0.1 fusion.61
  1460.9 0.5 collective-permute-start.2
  1461.3 0.1 broadcast_multiply_fusion.2
  1461.4 17.5 %reshape.426 = bf16[8,25,8,25,128]{4,3,2,1,0:T(8,128)(2,1)} reshape(bf16[1,200,200,128]{3,2,1,0:T(8,128)(2,1)} %param.16) | data formatting | bytes 20480000 | tf_op jit(solution)/shard_map/reshape.27
  1478.9 1.5 collective-permute-start.3
  1480.4 22.2 %fusion.24 = f32[8,8,1,25,25]{4,2,3,1,0:T(1,128)} fusion(bf16[8,25,8,25,128]{4,3,2,1,0:T(8,128)(2,1)} %reshape.426, bf16[8,8,128,1,1]{2,1,0,3,4:T(8,128)(2,1)S(1)} %get-tuple-element.11), kind=kOutput, calls=%fused_computation.40 | convolution fusion | flops 10240000 | bytes 10416384 | tf_op jit(solution)/shard_map/laibjk,abk->laibj/dot_general | solution.py:147
  1502.6 22.4 %fusion.22 = f32[8,8,1,25,25]{4,2,3,1,0:T(1,128)} fusion(bf16[8,25,8,25,128]{4,3,2,1,0:T(8,128)(2,1)} %reshape.426, bf16[8,8,128,1,1]{2,1,0,3,4:T(8,128)(2,1)S(1)} %get-tuple-element.10), kind=kOutput, calls=%fused_computation.38 | convolution fusion | flops 10240000 | bytes 10416384 | tf_op jit(solution)/shard_map/laibjk,abk->laibj/dot_general | solution.py:147
  1525.0 22.2 %fusion.20 = f32[8,8,1,25,25]{4,2,3,1,0:T(1,128)} fusion(bf16[8,25,8,25,128]{4,3,2,1,0:T(8,128)(2,1)} %reshape.426, bf16[8,8,128,1,1]{2,1,0,3,4:T(8,128)(2,1)S(1)} %get-tuple-element.8), kind=kOutput, calls=%fused_computation.36 | convolution fusion | flops 10240000 | bytes 10416384 | tf_op jit(solution)/shard_map/laibjk,abk->laibj/dot_general | solution.py:147
  1547.1 22.6 %fusion.18 = f32[8,8,1,25,25]{4,2,3,1,0:T(1,128)} fusion(bf16[8,25,8,25,128]{4,3,2,1,0:T(8,128)(2,1)} %reshape.426, bf16[8,8,128,1,1]{2,1,0,3,4:T(8,128)(2,1)S(1)} %get-tuple-element.9), kind=kOutput, calls=%fused_computation.34 | convolution fusion | flops 10240000 | bytes 10416384 | tf_op jit(solution)/shard_map/laibjk,abk->laibj/dot_general | solution.py:147
  1569.7 2.1 gather_fusion.2
  1571.8 1.9 broadcast_select_fusion
  1573.8 0.7 slice.76
  1574.5 2.3 collective-permute-start
  1576.8 1.9 fusion.43
  1578.7 0.3 reshape.428
  1579.0 1.6 add.142
  1580.6 1.5 collective-permute-start.1
  1582.1 13.4 fusion.26
  1595.5 0.7 collective-permute-done.1
  1596.3 1.8 pad_maximum_fusion
  1598.1 14.1 fusion.15
  1612.2 14.1 fusion.13
  1626.2 34.5 %fusion.4 = bf16[1,8,25,8,25,128]{5,4,2,3,1,0:T(8,128)(2,1)} fusion(f32[8,8,128,25,25]{2,4,3,1,0:T(8,128)} %fusion.13, f32[8,8,128,25,25]{2,4,3,1,0:T(8,128)} %fusion.15, f32[8,8,128,25,25]{2,4,3,1,0:T(8,128)} %fusion.26, f32[25,25]{1,0:T(8,128)S(1)} %get-tuple-element.16, f32[25,25]{1,0:T(8,128)S(1)} %get-tuple-element.14, ...), kind=kOutput, calls=%fused_computation.13 | convolution fusion | flops 1355874304 | bytes 84289296 | tf_op jit(solution)/shard_map/laibjk,abkm->laibjm/dot_general | solution.py:140
  1660.7 10.6 copy.41
  1671.3 17.7 %convert_element_type.36 = bf16[1,200,200,128]{3,2,1,0:T(8,128)(2,1)} reshape(bf16[1,8,25,8,25,128]{5,4,3,2,1,0:T(8,128)(2,1)} %copy.41) | data formatting | bytes 20480000 | tf_op jit(solution)/shard_map/convert_element_type | solution.py:151
  (36 shorter events, 0.3 us)
Async XLA Ops:
  0.6 18.7 %copy-start = (bf16[64,64]{1,0:T(8,128)(2,1)S(1)}, bf16[64,64]{1,0:T(8,128)(2,1)}, u32[]{:S(2)}) copy-start(bf16[64,64]{1,0:T(8,128)(2,1)} %param.12) | copy-start | bytes 24580
  0.6 18.7 %copy-start.4 = (bf16[64,64,128]{2,1,0:T(8,128)(2,1)S(1)}, bf16[64,64,128]{2,1,0:T(8,128)(2,1)}, u32[]{:S(2)}) copy-start(bf16[64,64,128]{2,1,0:T(8,128)(2,1)} %param.11) | copy-start | bytes 3145732
  3.6 1440.9 %all-to-all-start.1 = ((s32[32,2,1]{1,2,0:T(1,128)}), s32[32,2,1]{1,2,0:T(1,128)S(1)}, u32[]{:S(2)}, u32[]{:S(2)}) async-start(s32[32,2,1]{1,2,0:T(1,128)} %bitcast.2), calls=%async_computation.1 | async-start | bytes 32768 | tf_op jit(solution)/shard_map/all_to_all | solution.py:109
  785.0 3.4 copy-start.3
  1421.6 5.6 copy-start.2
  1444.5 12.6 all-to-all-start.2
  1457.2 112.5 %all-to-all-start = ((bf16[64,128,128]{2,1,0:T(8,128)(2,1)}), bf16[64,128,128]{2,1,0:T(8,128)(2,1)S(1)}, u32[]{:S(2)}, u32[]{:S(2)}) async-start(bf16[64,128,128]{2,1,0:T(8,128)(2,1)} %select_select_fusion), calls=%async_computation | async-start | bytes 4194304 | tf_op jit(solution)/shard_map/all_to_all | solution.py:95
  1460.9 18.0 %collective-permute-start.2 = (bf16[8,1,128]{2,1,0:T(2,128)(2,1)S(1)}, bf16[8,1,128]{2,1,0:T(2,128)(2,1)S(1)}, u32[]{:S(2)}, u32[]{:S(2)}) collective-permute-start(bf16[8,1,128]{2,1,0:T(2,128)(2,1)S(1)} %slice.83), channel_id=1, source_target_pairs={{0,7},{1,0},{2,1},{3,2},{4,3},{5,4},{6,5},{7,6},{8,15},{9,8},{10,9... | collective-permute-start | bytes 6152 | tf_op jit(solution)/shard_map/ppermute | solution.py:16
  1478.9 23.6 %collective-permute-start.3 = (bf16[1,9,128]{2,1,0:T(8,128)(2,1)S(1)}, bf16[1,9,128]{2,1,0:T(8,128)(2,1)S(1)}, u32[]{:S(2)}, u32[]{:S(2)}) collective-permute-start(bf16[1,9,128]{2,1,0:T(8,128)(2,1)S(1)} %pad_maximum_fusion.4), channel_id=1, source_target_pairs={{8,0},{16,8},{24,16},{9,1},{17,9},{25,17},{10,2},{18,10},{26,18},{... | collective-permute-start | bytes 6920 | tf_op jit(solution)/shard_map/ppermute | solution.py:22
  1571.8 4.9 copy-start.5
  1574.5 6.1 collective-permute-start
  1580.6 15.6 collective-permute-start.1
  1671.3 17.7 %copy-start.1 = (bf16[64,64]{1,0:T(8,128)(2,1)S(1)}, bf16[64,64]{1,0:T(8,128)(2,1)}, u32[]{:S(2)}) copy-start(bf16[64,64]{1,0:T(8,128)(2,1)} %param.12) | copy-start | bytes 24580
where the time goes:
time: 1700 us; the launch traced here: 1690 us
  other arithmetic  1410 us (83%)
  matrix products  191 us (11%)
  local copies, waits for them, and re-layouts  60.1 us (4%)
  starting transfers between devices  21.6 us (1%)
    another operation x3, other arithmetic, solve_blocks(): lower_factor = jnp.linalg.cholesky(system)  755 us
    another operation x3, other arithmetic, solve_blocks(): lax.linalg.triangular_solve(lower_factor, jnp.broadcast_to(identity, syst...  633 us
    dot_general x4, matrix products, shards(): jnp.einsum('laibjk,abk->laibj', anomaly_field, corner_mean, preferred_ele...  89.3 us
    dot_general x4, matrix products, shards(): jnp.einsum('laibjk,abkm->laibjm', anomaly_field, corner_transform, prefer...  76 us
  transfers between devices with their start and end apart: 7, of which 2 were waited for; matrix products, arithmetic and copies ran while one was open for 92% of the time, Pallas kernels for 0%

commit v1 on v0

v1 whole, which is shorter than its diff:
```python
import functools
import math

import jax
import jax.numpy as jnp
from jax import lax
from jax.experimental import pallas as pl
from jax.experimental.pallas import tpu as pltpu
from jax.sharding import PartitionSpec as P

FINE = 25
TILES_LAT = 8
TILES_LON = 8
BLOCK = 16
META = 16
F32 = jnp.float32
BF16 = jnp.bfloat16
NT = (((1,), (1,)), ((), ()))
NN = (((1,), (0,)), ((), ()))


def split(value):
    high = value.astype(BF16)
    return high, (value - high.astype(F32)).astype(BF16)


def dot(left, right, dims=NN):
    return lax.dot_general(left, right, dims, preferred_element_type=F32)


def pack_kernel(columns, lon_devices, capacity, owner, pert, meta, out, ranks):
    slots = out.shape[0]
    holding, locn, _ = pert.shape

    @pl.loop(0, slots // capacity)
    def _(device):
        ranks[device] = 0

    if slots > holding:

        @pl.loop(0, slots)
        def _(slot):
            out[slot, locn:, :] = jnp.full(meta.shape[1:], -1, out.dtype)

    @pl.loop(0, holding)
    def _(block):
        point = owner[block]
        row = point // columns
        col = point % columns
        device = row // TILES_LAT * lon_devices + col // TILES_LON
        rank = ranks[device]
        ranks[device] = rank + 1
        slot = device * capacity + jnp.minimum(rank, capacity - 1)
        out[slot, 0:locn, :] = pert[block]
        out[slot, locn:, :] = meta[block]


def pack(owner, pert, meta, columns, lon_devices, devices, capacity):
    holding, locn, members = pert.shape
    slots = devices * capacity
    return pl.pallas_call(
        functools.partial(pack_kernel, columns, lon_devices, capacity),
        out_shape=jax.ShapeDtypeStruct((slots, locn + META, members), BF16),
        in_specs=[
            pl.BlockSpec(memory_space=pltpu.SMEM),
            pl.BlockSpec(memory_space=pltpu.VMEM),
            pl.BlockSpec(memory_space=pltpu.VMEM),
        ],
        out_specs=pl.BlockSpec(memory_space=pltpu.VMEM),
        scratch_shapes=[pltpu.SMEM((devices,), jnp.int32)],
        name="pack",
    )(owner, pert, meta)


def load_systems(labels, arrived, systems, rights):
    slots, rows, members = arrived.shape
    locn = rows - META
    points = rights.shape[0]
    lane = lax.broadcasted_iota(jnp.int32, (members + META, members), 1)
    eye = lax.broadcasted_iota(jnp.int32, (members, members), 0) == lax.broadcasted_iota(
        jnp.int32, (members, members), 1
    )
    ridge = jnp.where(eye, members - 1.0, 0.0)

    def one(slot):
        label = labels[slot]
        pert = arrived[slot, 0:locn, :]
        meta = arrived[slot, locn:, :].astype(F32)
        weight = meta[0:1]
        depart = meta[1:2]
        twice = jnp.concatenate([pert, pert], axis=0)
        scaled = twice.T.astype(F32) * weight
        line = jnp.broadcast_to(weight * depart, (META, members))
        left = jnp.concatenate([scaled, line], axis=0)
        high = left.astype(BF16).astype(F32)
        both = jnp.where(lane < locn, high, left - high).astype(BF16)
        gram = dot(both, twice)

        def put():
            systems[label] = gram[0:members] + ridge
            rights[pl.ds(label, 1), :] = gram[members : members + 1]

        if slots > points:
            pl.when(label >= 0)(put)
        else:
            put()

    def several(step, carry):
        for part in range(4):
            one(step * 4 + part)
        return carry

    lax.fori_loop(0, slots // 4, several, 0)


def diagonal_inverses(step, systems2d, factors, points, members):
    size = BLOCK
    per = members // size
    lane_block = lax.broadcasted_iota(jnp.int32, (points, members), 1) // size
    rows = []
    for half in range(size // per):
        packed = jnp.zeros((points, members), F32)
        for inner in range(per):
            line = systems2d[pl.ds(size * step + per * half + inner, points, stride=members), :]
            line = pltpu.roll(line, (size * (inner - step)) % members, 1)
            packed = jnp.where(lane_block == inner, line, packed)
        turned = packed.T
        for inner in range(per):
            rows.append(turned[size * inner : size * (inner + 1)])
    sub = lax.broadcasted_iota(jnp.int32, (size, points), 0)
    roots = []
    for k in range(size):
        pivot = jnp.broadcast_to(rows[k][k : k + 1], (size, points))
        root = lax.rsqrt(pivot)
        inverse = root * root
        roots.append(root)
        line = jnp.where(sub == k, 1.0, rows[k])
        scaled = line * inverse
        for i in range(k + 1, size):
            factor = jnp.broadcast_to(rows[i][k : k + 1], (size, points))
            rows[i] = jnp.where(sub == k, 0.0, rows[i]) - factor * scaled
    lower = []
    for i in range(size):
        line = jnp.where(sub < i, rows[i], jnp.where(sub == i, 1.0, 0.0))
        lower.append(line * roots[i])
    whole = []
    for i in range(size):
        total = jnp.zeros((size, points), F32)
        for l in range(i, size):
            total += jnp.broadcast_to(lower[l][i : i + 1], (size, points)) * lower[l]
        whole.append(total)
    for group in range(size // per):
        part = slice(group * per, (group + 1) * per)
        factors[group] = jnp.concatenate(whole[part], axis=0).T
        factors[size // per + group] = jnp.concatenate(lower[part], axis=0).T


def solve_kernel(labels, arrived, own, east, north, corner, systems2d, rights, factors, slabs):
    points = own.shape[0]
    members = own.shape[2]
    systems = systems2d.reshape(points, members, members)
    size = BLOCK
    per = members // size
    groups = 2 * size // per
    load_systems(labels, arrived, systems, rights)
    row8 = lax.broadcasted_iota(jnp.int32, (per, members), 0)
    lane8 = lax.broadcasted_iota(jnp.int32, (per, members), 1)
    own_block = row8 == lane8 // size
    row = lax.broadcasted_iota(jnp.int32, (size, members), 0)
    lane = lax.broadcasted_iota(jnp.int32, (size, members), 1)
    many = 8
    for step in range(members // size):
        diagonal_inverses(step, systems2d, factors, points, members)
        first = step * size
        after = first + size
        here = (lane >= first) & (lane < after)
        unit = jnp.where(lane - first == row, 1.0, 0.0)

        def small(point):
            parts = []
            for group in range(groups):
                line = factors[group, pl.ds(point, 1), :]
                parts.append(jnp.where(own_block, jnp.broadcast_to(line, (per, members)), 0.0))
            left_high, left_low = split(jnp.concatenate(parts, axis=0))
            slab = jnp.where(here, unit, systems[point, first:after, :])
            high, low = split(slab)
            highs = jnp.concatenate([high] * per, axis=0)
            lows = jnp.concatenate([low] * per, axis=0)
            both = dot(
                jnp.concatenate([left_high, left_low], axis=1),
                jnp.concatenate([highs, highs], axis=0),
            ) + dot(left_high, lows)
            systems[point, first:after, :] = jnp.where(lane < after, both[size:], 0.0)
            slabs[point] = both[:size]

        def small_many(index, carry):
            for part in range(many):
                small(index * many + part)
            return carry

        lax.fori_loop(0, points // many, small_many, 0)
        if after == members:
            continue
        rest = members - after
        lane_rest = lax.broadcasted_iota(jnp.int32, (rest, members), 1)
        here_rest = (lane_rest >= first) & (lane_rest < after)
        before_zeros = [jnp.zeros((first, members), BF16)] if first else []
        after_zeros = [jnp.zeros((rest, members), BF16)]

        def trail(point):
            high, low = split(slabs[point])
            wide_high = jnp.concatenate(before_zeros + [high] + after_zeros, axis=0)
            wide_low = jnp.concatenate(before_zeros + [low] + after_zeros, axis=0)
            old = systems[point, after:, :]
            old_high, old_low = split(old)
            change = dot(
                jnp.concatenate([old_high, old_low], axis=1),
                jnp.concatenate([wide_high, wide_high], axis=0),
            ) + dot(old_high, wide_low)
            systems[point, after:, :] = jnp.where(here_rest, 0.0, old) - change

        def trail_many(index, carry):
            for part in range(many):
                trail(index * many + part)
            return carry

        lax.fori_loop(0, points // many, trail_many, 0)

    def finish(point):
        inverse = systems[point]
        right = rights[pl.ds(point, 1), :]
        forward = jnp.sum(inverse * right, axis=1, keepdims=True)
        mean = jnp.sum(inverse * forward, axis=0, keepdims=True)
        own[point, 0:members, :] = (math.sqrt(members - 1.0) * inverse).astype(BF16)
        own[point, members:, :] = jnp.broadcast_to(mean, (META, members)).astype(BF16)

    def finish_many(index, carry):
        for part in range(4):
            finish(index * 4 + part)
        return carry

    lax.fori_loop(0, points // 4, finish_many, 0)
    for index in range(TILES_LON):
        north[index] = own[index]
    for index in range(TILES_LAT):
        east[index] = own[index * TILES_LON]
    corner[0] = own[0]


def solve(labels, arrived):
    slots, rows, members = arrived.shape
    points = TILES_LAT * TILES_LON
    shape = lambda count: jax.ShapeDtypeStruct((count, members + META, members), BF16)
    vmem = pl.BlockSpec(memory_space=pltpu.VMEM)
    return pl.pallas_call(
        solve_kernel,
        out_shape=(shape(points), shape(TILES_LAT), shape(TILES_LON), shape(1)),
        in_specs=[pl.BlockSpec(memory_space=pltpu.SMEM), vmem],
        out_specs=(vmem, vmem, vmem, vmem),
        scratch_shapes=[
            pltpu.VMEM((points * members, members), F32),
            pltpu.VMEM((points, members), F32),
            pltpu.VMEM((2 * BLOCK * BLOCK // members, points, members), F32),
            pltpu.VMEM((points, BLOCK, members), F32),
        ],
        compiler_params=pltpu.CompilerParams(vmem_limit_bytes=48 << 20),
        name="solve",
    )(labels, arrived)


def apply_kernel(
    top, own, east, north, corner, anomalies, flux, out, mean, weights, means, hats
):
    members = anomalies.shape[3]
    cols = anomalies.shape[2]
    tile_row = pl.program_id(1)
    is_top = top[0] == 1
    last = tile_row == TILES_LAT - 1
    half = (FINE + 1) // 2

    def here(col):
        if col < TILES_LON:
            return own[tile_row * TILES_LON + col]
        return east[tile_row]

    def above(col):
        ahead = jnp.minimum(tile_row + 1, TILES_LAT - 1)
        inner = own[ahead * TILES_LON + col] if col < TILES_LON else east[ahead]
        outer = north[col] if col < TILES_LON else corner[0]
        return jnp.where(last & jnp.logical_not(is_top), outer, inner)

    for col in range(TILES_LON + 1):
        low = here(col)
        high = above(col)
        change = (high[:members].astype(F32) - low[:members].astype(F32)).astype(BF16)
        place = slice(col * members, (col + 1) * members)
        weights[0, place, 0:members] = low[:members]
        weights[0, place, members:] = change
        weights[1, place, 0:members] = high[:members]
        weights[1, place, members:] = change
        means[col : col + 1, :] = low[members:].astype(F32)[0:1]
        means[16 + col : 17 + col, :] = high[members:].astype(F32)[0:1]

    width = 32
    offset = lax.broadcasted_iota(jnp.int32, (width, members), 0)
    for part, (start, stop) in enumerate(((0, half), (half, FINE))):
        count = stop - start
        fraction = (
            lax.broadcasted_iota(jnp.int32, (count, width, members), 0) + start
        ).astype(F32) / FINE - part
        carry = None
        for col in range(TILES_LON):
            begin = col * (FINE - 1)
            field = anomalies[0, start:stop, begin : begin + width, :]
            scaled = (field.astype(F32) * fraction).astype(BF16)
            left = jnp.concatenate([field, scaled], axis=2).reshape(count * width, 2 * members)
            place = slice(col * members, (col + 2) * members)
            both = dot(left, weights[part, place, :], NT).reshape(count, width, 2 * members)
            cell = offset - col
            inside = (cell >= 0) & (cell < FINE)
            right_weight = jnp.where(inside, cell.astype(F32) / FINE, 0.0)
            left_weight = jnp.where(inside, 1.0 - cell.astype(F32) / FINE, 0.0)
            result = left_weight * both[:, :, :members] + right_weight * both[:, :, members:]
            head = result[:, 0:8]
            if carry is not None:
                head = head + carry
            carry = result[:, width - 8 :]
            out[0, start:stop, begin : begin + width - 8, :] = jnp.concatenate(
                [head, result[:, 8 : width - 8]], axis=1
            ).astype(BF16)
        out[0, start:stop, cols - 8 :, :] = carry.astype(BF16)

    corner_index = lax.broadcasted_iota(jnp.int32, (16, cols), 0)
    cell = lax.broadcasted_iota(jnp.int32, (16, cols), 1)
    tile = cell // FINE
    part = (cell - tile * FINE).astype(F32) / FINE
    hat = jnp.where(
        tile == corner_index, 1.0 - part, jnp.where(tile + 1 == corner_index, part, 0.0)
    )
    keep = lax.broadcasted_iota(jnp.int32, (16, members), 0) <= TILES_LON
    left = jnp.concatenate(
        [jnp.where(keep, means[0:16, :], 0.0), jnp.where(keep, means[16:32, :], 0.0)], axis=0
    ).astype(BF16)
    for line in range(FINE):
        product = dot(left, anomalies[0, line], NT)
        up = line / FINE
        mixed = (1.0 - up) * product[0:16] + up * product[16:32]
        shift = jnp.sum(mixed * hat, axis=0, keepdims=True)
        place = pl.ds(tile_row * FINE + line, 1)
        mean[0, place, :] = flux[0, place, :] + shift


def apply(top, own, east, north, corner, anomalies, flux):
    lags, rows, cols, members = anomalies.shape
    whole = lambda array: pl.BlockSpec(array.shape, lambda l, r: (0,) * array.ndim)
    strip = pl.BlockSpec((1, FINE, cols, members), lambda l, r: (l, r, 0, 0))
    plane = pl.BlockSpec((1, rows, cols), lambda l, r: (l, 0, 0))
    return pl.pallas_call(
        apply_kernel,
        grid=(lags, TILES_LAT),
        out_shape=(
            jax.ShapeDtypeStruct(anomalies.shape, BF16),
            jax.ShapeDtypeStruct(flux.shape, F32),
        ),
        in_specs=[
            pl.BlockSpec(memory_space=pltpu.SMEM),
            whole(own),
            whole(east),
            whole(north),
            whole(corner),
            strip,
            plane,
        ],
        out_specs=(strip, plane),
        scratch_shapes=[
            pltpu.VMEM((2, (TILES_LON + 1) * members, 2 * members), BF16),
            pltpu.VMEM((32, members), F32),
            pltpu.VMEM((16, cols), F32),
        ],
        compiler_params=pltpu.CompilerParams(vmem_limit_bytes=48 << 20),
        name="apply",
    )(top, own, east, north, corner, anomalies, flux)


def shards(obs_pert, obs_dep, obs_prec, obs_count, owner_point, anomalies, flux_mean):
    lat_devices = lax.axis_size("lat")
    lon_devices = lax.axis_size("lon")
    devices = lat_devices * lon_devices
    holding, locn, members = obs_pert.shape
    capacity = max(1, (holding + devices - 1) // devices)
    columns = TILES_LON * lon_devices
    live = jnp.arange(locn, dtype=jnp.int32)[None, :] < obs_count[:, None]
    weight = jnp.where(live, obs_prec, jnp.zeros((), BF16))
    within = owner_point // columns % TILES_LAT * TILES_LON + owner_point % TILES_LON
    line = lax.broadcasted_iota(jnp.int32, (holding, META, members), 1)
    meta = jnp.where(
        line == 0,
        jnp.concatenate([weight, weight], axis=1)[:, None, :],
        jnp.where(
            line == 1,
            jnp.concatenate([obs_dep, obs_dep], axis=1)[:, None, :],
            within.astype(BF16)[:, None, None],
        ),
    )
    packed = pack(owner_point, obs_pert, meta, columns, lon_devices, devices, capacity)
    arrived = lax.all_to_all(packed, ("lat", "lon"), split_axis=0, concat_axis=0, tiled=True)
    labels = arrived[:, locn + 2, 0].astype(jnp.int32)
    own, east, north, corner = solve(labels, arrived)
    lat_pairs = [(i, i - 1) for i in range(1, lat_devices)]
    lon_pairs = [(i, (i - 1) % lon_devices) for i in range(lon_devices)]
    both_pairs = [
        (a * lon_devices + c, b * lon_devices + d) for a, b in lat_pairs for c, d in lon_pairs
    ]
    east = lax.ppermute(east, "lon", lon_pairs)
    north = lax.ppermute(north, "lat", lat_pairs)
    corner = lax.ppermute(corner, ("lat", "lon"), both_pairs)
    top = (lax.axis_index("lat") == lat_devices - 1).astype(jnp.int32).reshape(1)
    return apply(top, own, east, north, corner, anomalies, flux_mean)


def solution(mesh):
    placed = (
        P(("lat", "lon"), None, None),
        P(("lat", "lon"), None),
        P(("lat", "lon"), None),
        P(("lat", "lon")),
        P(("lat", "lon")),
        P(None, "lat", "lon", None),
        P(None, "lat", "lon"),
    )
    return jax.shard_map(
        shards,
        mesh=mesh,
        in_specs=placed,
        out_specs=(P(None, "lat", "lon", None), P(None, "lat", "lon")),
        check_vma=False,
    )
```

time: 1700 us -> 129 us (0.08)
  other arithmetic: 1410 us -> 4.42 us
  matrix products: 191 us -> 0 us
  Pallas kernels: 0 us -> 70.8 us
  local copies, waits for them, and re-layouts: 60.1 us -> 0.01 us
  blocking collectives: 0 us -> 39.1 us
  starting transfers between devices: 21.6 us -> 4 us
    another operation x6 -> x0, other arithmetic: 1390 us -> none  [the longest x3 755 us: solve_blocks(): lower_factor = jnp.linalg.cholesky(system)]
    dot_general x10 -> x0, matrix products: 174 us -> none  [the longest x4 89.3 us: shards(): jnp.einsum('laibjk,abk->laibj', anomaly_field, corner_mean, preferred_ele...]
    pallas_call x0 -> x3, Pallas kernels: none -> 70.8 us  [the longest x1 48.4 us: solve(): pl.pallas_call(solve_kernel, out_shape=(shape(points), shape(TILES_LAT),...]
    all_to_all x0 -> x1, blocking collectives: none -> 39.1 us  [shards(): lax.all_to_all(packed, ('lat', 'lon'), split_axis=0, concat_axis=0, tiled...]
    convert_element_type x2 -> x0, local copies, waits for them, and re-layouts: 17.8 us -> none  [the longest x1 17.7 us: shards(): summed.reshape(lag_total, rows_here, cols_here, member_total)]
    another operation x1 -> x0, local copies, waits for them, and re-layouts: 17.5 us -> none
  transfers between devices with their start and end apart: 7 -> 3, of which waited for: 2 -> 1; matrix products, arithmetic and copies ran while one was open for 92% -> 0% of each run, Pallas kernels for 0% -> 0%
where the time goes in v1:
time: 129 us; the launch traced here: 127 us
  Pallas kernels  70.8 us (55%)
  blocking collectives  39.1 us (30%)
  waiting for transfers between devices  8.4 us (7%)
  other arithmetic  4.42 us (3%)
  starting transfers between devices  4 us (3%)
    pallas_call x1, Pallas kernels, solve(): pl.pallas_call(solve_kernel, out_shape=(shape(points), shape(TILES_LAT),...  48.4 us
    all_to_all x1, blocking collectives, shards(): lax.all_to_all(packed, ('lat', 'lon'), split_axis=0, concat_axis=0, tiled...  39.1 us
    pallas_call x1, Pallas kernels, apply(): pl.pallas_call(apply_kernel, grid=(lags, TILES_LAT), out_shape=(jax.Shape...  18.1 us
    ppermute x1, waiting for transfers between devices, shards(): corner = lax.ppermute(corner, ('lat', 'lon'), both_pairs)  8.39 us
    pallas_call x1, Pallas kernels, pack(): pl.pallas_call(functools.partial(pack_kernel, columns, lon_devices, capac...  4.35 us
  transfers between devices with their start and end apart: 3, of which 1 were waited for; matrix products, arithmetic and copies ran while one was open for 0% of the time, Pallas kernels for 0%

profile of v1, /device:TPU:1, one launch (start us, length us, event | category | flops | bytes accessed | tf_op | source)
XLA Modules:
  0.0 127.4 jit_solution(8162927066307370927)
XLA Ops:
  0.6 0.7 fusion.5
  1.3 0.8 fusion.1
  2.1 0.9 pad_maximum_fusion
  3.0 0.8 select_select_fusion.meta
  3.8 4.3 %pack.1 = bf16[64,80,128]{2,1,0:T(8,128)(2,1)} custom-call(s32[64]{0:T(128)} %owner.1, bf16[64,64,128]{2,1,0:T(8,128)(2,1)} %pert.1, bf16[64,16,128]{2,1,0:T(8,128)(2,1)} %select_select_fusion.meta), custom_call_target="tpu_custom_call" | custom-call | tf_op jit(solution)/shard_map/pack/pallas_call | solution.py:61
  8.2 0.0 copy-start
  8.2 39.1 %all_to_all.5.arrived = bf16[64,80,128]{2,1,0:T(8,128)(2,1)S(1)} all-to-all(bf16[64,80,128]{2,1,0:T(8,128)(2,1)} %pack.1), channel_id=1, replica_groups=mesh['lat'=4,'lon'=8] {'lat','lon'}, dimensions={0} | all-to-all | bytes 2621440 | tf_op jit(solution)/shard_map/all_to_all | solution.py:406
  47.3 1.2 fusion.labels
  48.6 48.4 %solve.1 = (bf16[64,144,128]{2,1,0:T(8,128)(2,1)S(1)}, bf16[8,144,128]{2,1,0:T(8,128)(2,1)}, bf16[8,144,128]{2,1,0:T(8,128)(2,1)S(1)}, bf16[1,144,128]{2,1,0:T(8,128)(2,1)S(1)}) custom-call(s32[64]{0:T(128)S(1)} %fusion.labels, bf16[64,80,128]{2,1,0:T(8,128)(2,1)S(1)} %all_to_all.5.arrived), custom_call_target="tpu_custom_call" | custom-call | tf_op jit(solution)/shard_map/solve/pallas_call | solution.py:255
  96.9 1.4 %collective-permute-start = (bf16[8,144,128]{2,1,0:T(8,128)(2,1)}, bf16[8,144,128]{2,1,0:T(8,128)(2,1)S(1)}, u32[]{:S(2)}, u32[]{:S(2)}) collective-permute-start(bf16[8,144,128]{2,1,0:T(8,128)(2,1)} %get-tuple-element.7), channel_id=1, source_target_pairs={{0,7},{1,0},{2,1},{3,2},{4,3},{5,4},{6,5},{7,6},{8,15},{9,8},{10,9... | collective-permute-start | bytes 884744 | tf_op jit(solution)/shard_map/ppermute | solution.py:414
  98.4 1.3 %collective-permute-start.1 = (bf16[8,144,128]{2,1,0:T(8,128)(2,1)S(1)}, bf16[8,144,128]{2,1,0:T(8,128)(2,1)S(1)}, u32[]{:S(2)}, u32[]{:S(2)}) collective-permute-start(bf16[8,144,128]{2,1,0:T(8,128)(2,1)S(1)} %get-tuple-element.8), channel_id=1, source_target_pairs={{8,0},{16,8},{24,16},{9,1},{17,9},{25,17},{10,2},{18,10},{26,18},{... | collective-permute-start | bytes 884744 | tf_op jit(solution)/shard_map/ppermute | solution.py:415
  99.7 1.3 %collective-permute-start.2 = (bf16[1,144,128]{2,1,0:T(8,128)(2,1)S(1)}, bf16[1,144,128]{2,1,0:T(8,128)(2,1)S(1)}, u32[]{:S(2)}, u32[]{:S(2)}) collective-permute-start(bf16[1,144,128]{2,1,0:T(8,128)(2,1)S(1)} %get-tuple-element.9), channel_id=1, source_target_pairs={{8,7},{9,0},{10,1},{11,2},{12,3},{13,4},{14,5},{15,6},{16,15},{17,... | collective-permute-start | bytes 110600 | tf_op jit(solution)/shard_map/ppermute | solution.py:416
  101.0 8.4 %collective-permute-done.2.corner = bf16[1,144,128]{2,1,0:T(8,128)(2,1)S(1)} collective-permute-done((bf16[1,144,128]{2,1,0:T(8,128)(2,1)S(1)}, bf16[1,144,128]{2,1,0:T(8,128)(2,1)S(1)}, u32[]{:S(2)}, u32[]{:S(2)}) %collective-permute-start.2) | collective-permute-done | bytes 36896 | tf_op jit(solution)/shard_map/ppermute | solution.py:416
  109.4 0.0 collective-permute-done.east
  109.4 0.0 collective-permute-done.1.north
  109.4 0.0 copy-done
  109.4 18.1 %apply.1 = (bf16[1,200,200,128]{3,2,1,0:T(8,128)(2,1)}, f32[1,200,200]{2,1,0:T(8,128)}) custom-call(s32[1]{0:T(128)} %bitcast.top, bf16[64,144,128]{2,1,0:T(8,128)(2,1)S(1)} %get-tuple-element.6.own, bf16[8,144,128]{2,1,0:T(8,128)(2,1)S(1)} %collective-permute-done.east, bf16[8,144,128]{2,1,0:T(8,128)(2,1)S(1)} %collective-permute-done.1.north, ...), custom_call_target="tpu_custom_call" | custom-call | tf_op jit(solution)/shard_map/apply/pallas_call | solution.py:358
  (1 shorter events, 0.0 us)
Async XLA Ops:
  8.2 101.2 %copy-start = (f32[1,200,200]{2,1,0:T(8,128)S(1)}, f32[1,200,200]{2,1,0:T(8,128)}, u32[]{:S(2)}) copy-start(f32[1,200,200]{2,1,0:T(8,128)} %flux.1) | copy-start | bytes 480004
  96.9 12.4 %collective-permute-start = (bf16[8,144,128]{2,1,0:T(8,128)(2,1)}, bf16[8,144,128]{2,1,0:T(8,128)(2,1)S(1)}, u32[]{:S(2)}, u32[]{:S(2)}) collective-permute-start(bf16[8,144,128]{2,1,0:T(8,128)(2,1)} %get-tuple-element.7), channel_id=1, source_target_pairs={{0,7},{1,0},{2,1},{3,2},{4,3},{5,4},{6,5},{7,6},{8,15},{9,8},{10,9... | collective-permute-start | bytes 884744 | tf_op jit(solution)/shard_map/ppermute | solution.py:414
  98.4 11.0 %collective-permute-start.1 = (bf16[8,144,128]{2,1,0:T(8,128)(2,1)S(1)}, bf16[8,144,128]{2,1,0:T(8,128)(2,1)S(1)}, u32[]{:S(2)}, u32[]{:S(2)}) collective-permute-start(bf16[8,144,128]{2,1,0:T(8,128)(2,1)S(1)} %get-tuple-element.8), channel_id=1, source_target_pairs={{8,0},{16,8},{24,16},{9,1},{17,9},{25,17},{10,2},{18,10},{26,18},{... | collective-permute-start | bytes 884744 | tf_op jit(solution)/shard_map/ppermute | solution.py:415
  99.7 9.7 %collective-permute-start.2 = (bf16[1,144,128]{2,1,0:T(8,128)(2,1)S(1)}, bf16[1,144,128]{2,1,0:T(8,128)(2,1)S(1)}, u32[]{:S(2)}, u32[]{:S(2)}) collective-permute-start(bf16[1,144,128]{2,1,0:T(8,128)(2,1)S(1)} %get-tuple-element.9), channel_id=1, source_target_pairs={{8,7},{9,0},{10,1},{11,2},{12,3},{13,4},{14,5},{15,6},{16,15},{17,... | collective-permute-start | bytes 110600 | tf_op jit(solution)/shard_map/ppermute | solution.py:416

commit v2 on v1

--- a/solution.py
+++ b/solution.py
@@ -12,7 +12,7 @@
 TILES_LAT = 8
 TILES_LON = 8
 BLOCK = 16
-META = 16
+META = 8
 F32 = jnp.float32
 BF16 = jnp.bfloat16
 NT = (((1,), (1,)), ((), ()))
@@ -28,51 +28,97 @@
     return lax.dot_general(left, right, dims, preferred_element_type=F32)
 
 
-def pack_kernel(columns, lon_devices, capacity, owner, pert, meta, out, ranks):
-    slots = out.shape[0]
-    holding, locn, _ = pert.shape
-
-    @pl.loop(0, slots // capacity)
+def pack_kernel(
+    columns, lon_devices, sent, owner, count, pert, prec, dep, first, second, ranks, weights, departs
+):
+    holding, locn, members = pert.shape
+    devices = first.shape[0] // sent
+
+    @pl.loop(0, devices)
     def _(device):
         ranks[device] = 0
 
+    weights[...] = jnp.concatenate([prec[...], prec[...]], axis=1).astype(F32)
+    departs[...] = jnp.concatenate([dep[...], dep[...]], axis=1).astype(F32)
+    slots = first.shape[0] + (0 if second is None else second.shape[0])
     if slots > holding:
 
-        @pl.loop(0, slots)
+        @pl.loop(0, first.shape[0])
         def _(slot):
-            out[slot, locn:, :] = jnp.full(meta.shape[1:], -1, out.dtype)
+            first[slot, locn:, :] = jnp.full((META, members), -1, BF16)
+
+        if second is not None:
+
+            @pl.loop(0, second.shape[0])
+            def _(slot):
+                second[slot, locn:, :] = jnp.full((META, members), -1, BF16)
+
+    row = lax.broadcasted_iota(jnp.int32, (META, members), 0)
+    slot_of_lane = lax.broadcasted_iota(jnp.int32, (META, members), 1) % locn
 
     @pl.loop(0, holding)
     def _(block):
         point = owner[block]
-        row = point // columns
-        col = point % columns
-        device = row // TILES_LAT * lon_devices + col // TILES_LON
+        point_row = point // columns
+        point_col = point % columns
+        device = point_row // TILES_LAT * lon_devices + point_col // TILES_LON
+        within = point_row % TILES_LAT * TILES_LON + point_col % TILES_LON
         rank = ranks[device]
         ranks[device] = rank + 1
-        slot = device * capacity + jnp.minimum(rank, capacity - 1)
-        out[slot, 0:locn, :] = pert[block]
-        out[slot, locn:, :] = meta[block]
-
-
-def pack(owner, pert, meta, columns, lon_devices, devices, capacity):
+        weight = jnp.broadcast_to(weights[pl.ds(block, 1), :], (META, members))
+        depart = jnp.broadcast_to(departs[pl.ds(block, 1), :], (META, members))
+        meta = jnp.where(
+            row == 0,
+            jnp.where(slot_of_lane < count[block], weight, 0.0),
+            jnp.where(row == 1, depart, within.astype(F32)),
+        ).astype(BF16)
+
+        def put(out, place):
+            out[place, 0:locn, :] = pert[block]
+            out[place, locn:, :] = meta
+
+        if second is None:
+            put(first, device * sent + jnp.minimum(rank, sent - 1))
+        else:
+            kept = second.shape[0] // devices
+
+            @pl.when(rank < sent)
+            def _():
+                put(first, device * sent + rank)
+
+            @pl.when(rank >= sent)
+            def _():
+                put(second, device * kept + jnp.minimum(rank - sent, kept - 1))
+
+
+def pack(owner, count, pert, prec, dep, columns, lon_devices, devices, sent, kept):
     holding, locn, members = pert.shape
-    slots = devices * capacity
+    shape = lambda each: jax.ShapeDtypeStruct((devices * each, locn + META, members), BF16)
+    vmem = pl.BlockSpec(memory_space=pltpu.VMEM)
+    smem = pl.BlockSpec(memory_space=pltpu.SMEM)
+    kernel = functools.partial(pack_kernel, columns, lon_devices, sent)
+    if not kept:
+        both = kernel
+        kernel = lambda *refs: both(*refs[:6], None, *refs[6:])
     return pl.pallas_call(
-        functools.partial(pack_kernel, columns, lon_devices, capacity),
-        out_shape=jax.ShapeDtypeStruct((slots, locn + META, members), BF16),
-        in_specs=[
-            pl.BlockSpec(memory_space=pltpu.SMEM),
-            pl.BlockSpec(memory_space=pltpu.VMEM),
-            pl.BlockSpec(memory_space=pltpu.VMEM),
+        kernel,
+        out_shape=(shape(sent), shape(kept)) if kept else (shape(sent),),
+        in_specs=[smem, smem, vmem, vmem, vmem],
+        out_specs=(vmem, vmem) if kept else (vmem,),
+        scratch_shapes=[
+            pltpu.SMEM((devices,), jnp.int32),
+            pltpu.VMEM((holding, members), F32),
+            pltpu.VMEM((holding, members), F32),
         ],
-        out_specs=pl.BlockSpec(memory_space=pltpu.VMEM),
-        scratch_shapes=[pltpu.SMEM((devices,), jnp.int32)],
         name="pack",
-    )(owner, pert, meta)
-
-
-def load_systems(labels, arrived, systems, rights):
+    )(owner, count, pert, prec, dep)
+
+
+def label_of(meta):
+    return jnp.max(meta.astype(F32)[2:3]).astype(jnp.int32)
+
+
+def load_systems(arrived, systems, rights):
     slots, rows, members = arrived.shape
     locn = rows - META
     points = rights.shape[0]
@@ -83,7 +129,6 @@
     ridge = jnp.where(eye, members - 1.0, 0.0)
 
     def one(slot):
-        label = labels[slot]
         pert = arrived[slot, 0:locn, :]
         meta = arrived[slot, locn:, :].astype(F32)
         weight = meta[0:1]
@@ -96,14 +141,15 @@
         both = jnp.where(lane < locn, high, left - high).astype(BF16)
         gram = dot(both, twice)
 
-        def put():
-            systems[label] = gram[0:members] + ridge
-            rights[pl.ds(label, 1), :] = gram[members : members + 1]
+        def put(place):
+            systems[place] = gram[0:members] + ridge
+            rights[pl.ds(place, 1), :] = gram[members : members + 1]
 
         if slots > points:
-            pl.when(label >= 0)(put)
+            label = label_of(arrived[slot, locn:, :])
+            pl.when(label >= 0)(lambda: put(label))
         else:
-            put()
+            put(slot)
 
     def several(step, carry):
         for part in range(4):
@@ -151,24 +197,38 @@
         whole.append(total)
     for group in range(size // per):
         part = slice(group * per, (group + 1) * per)
-        factors[group] = jnp.concatenate(whole[part], axis=0).T
-        factors[size // per + group] = jnp.concatenate(lower[part], axis=0).T
-
-
-def solve_kernel(labels, arrived, own, east, north, corner, systems2d, rights, factors, slabs):
-    points = own.shape[0]
-    members = own.shape[2]
+        factors[group] = jnp.concatenate(whole[part][::-1], axis=0).T
+        factors[size // per + group] = jnp.concatenate(lower[part][::-1], axis=0).T
+
+
+def solve_kernel(folded, arrived, out, systems2d, rights, factors, slabs):
+    points = out.shape[0]
+    members = out.shape[2]
+    locn = arrived.shape[1] - META
     systems = systems2d.reshape(points, members, members)
     size = BLOCK
     per = members // size
     groups = 2 * size // per
-    load_systems(labels, arrived, systems, rights)
-    row8 = lax.broadcasted_iota(jnp.int32, (per, members), 0)
+    load_systems(arrived, systems, rights)
     lane8 = lax.broadcasted_iota(jnp.int32, (per, members), 1)
-    own_block = row8 == lane8 // size
-    row = lax.broadcasted_iota(jnp.int32, (size, members), 0)
-    lane = lax.broadcasted_iota(jnp.int32, (size, members), 1)
-    many = 8
+    row = lax.broadcasted_iota(jnp.int32, (members, members), 0) % size
+    lane = lax.broadcasted_iota(jnp.int32, (members, members), 1)
+    empty = jnp.zeros((members, members), BF16)
+
+    def halves(value):
+        high, low = split(value)
+        return jnp.concatenate(
+            [
+                jnp.concatenate([high, low], axis=1),
+                jnp.concatenate([high, empty], axis=1),
+            ],
+            axis=0,
+        )
+
+    def product(left, right):
+        both = dot(jnp.concatenate(split(left), axis=1), right)
+        return both[:, :members] + both[:, members:]
+
     for step in range(members // size):
         diagonal_inverses(step, systems2d, factors, points, members)
         first = step * size
@@ -176,63 +236,90 @@
         here = (lane >= first) & (lane < after)
         unit = jnp.where(lane - first == row, 1.0, 0.0)
 
-        def small(point):
+        def small(index):
+            start = pl.multiple_of(index * per, per)
             parts = []
-            for group in range(groups):
-                line = factors[group, pl.ds(point, 1), :]
-                parts.append(jnp.where(own_block, jnp.broadcast_to(line, (per, members)), 0.0))
-            left_high, left_low = split(jnp.concatenate(parts, axis=0))
-            slab = jnp.where(here, unit, systems[point, first:after, :])
-            high, low = split(slab)
-            highs = jnp.concatenate([high] * per, axis=0)
-            lows = jnp.concatenate([low] * per, axis=0)
-            both = dot(
-                jnp.concatenate([left_high, left_low], axis=1),
-                jnp.concatenate([highs, highs], axis=0),
-            ) + dot(left_high, lows)
-            systems[point, first:after, :] = jnp.where(lane < after, both[size:], 0.0)
-            slabs[point] = both[:size]
+            for inner in range(per):
+                for group in range(groups):
+                    lines = jnp.broadcast_to(
+                        factors[group, pl.ds(start + inner, 1), :], (per, members)
+                    )
+                    lines = pltpu.roll(lines, 0, 1, stride=size, stride_axis=0)
+                    lines = pltpu.roll(lines, (size * (inner - per + 1)) % members, 1)
+                    parts.append(jnp.where(lane8 // size == inner, lines, 0.0))
+            slab = systems[pl.ds(start, per), first:after, :].reshape(members, members)
+            right = halves(jnp.where(here, unit, slab))
+            both = product(jnp.concatenate(parts, axis=0), right)
+            for inner in range(per):
+                begin = 2 * size * inner
+                slabs[start + inner] = both[begin : begin + size]
+                systems[start + inner, first:after, :] = jnp.where(
+                    lane[:size] < after, both[begin + size : begin + 2 * size], 0.0
+                )
 
         def small_many(index, carry):
-            for part in range(many):
-                small(index * many + part)
+            small(index * 2)
+            small(index * 2 + 1)
             return carry
 
-        lax.fori_loop(0, points // many, small_many, 0)
+        lax.fori_loop(0, points // per // 2, small_many, 0)
         if after == members:
             continue
         rest = members - after
         lane_rest = lax.broadcasted_iota(jnp.int32, (rest, members), 1)
         here_rest = (lane_rest >= first) & (lane_rest < after)
-        before_zeros = [jnp.zeros((first, members), BF16)] if first else []
-        after_zeros = [jnp.zeros((rest, members), BF16)]
-
-        def trail(point):
-            high, low = split(slabs[point])
-            wide_high = jnp.concatenate(before_zeros + [high] + after_zeros, axis=0)
-            wide_low = jnp.concatenate(before_zeros + [low] + after_zeros, axis=0)
-            old = systems[point, after:, :]
-            old_high, old_low = split(old)
-            change = dot(
-                jnp.concatenate([old_high, old_low], axis=1),
-                jnp.concatenate([wide_high, wide_high], axis=0),
-            ) + dot(old_high, wide_low)
-            systems[point, after:, :] = jnp.where(here_rest, 0.0, old) - change
+
+        def trail(index):
+            start = pl.multiple_of(index * per, per)
+            right = halves(slabs[pl.ds(start, per)].reshape(members, members))
+            parts = []
+            for inner in range(per):
+                old = systems[start + inner, after:, :]
+                moved = pltpu.roll(old, (size * (inner - step)) % members, 1)
+                parts.append(jnp.where(lane_rest // size == inner, moved, 0.0))
+            change = product(jnp.concatenate(parts, axis=0), right)
+            for inner in range(per):
+                old = systems[start + inner, after:, :]
+                systems[start + inner, after:, :] = (
+                    jnp.where(here_rest, 0.0, old) - change[inner * rest : (inner + 1) * rest]
+                )
 
         def trail_many(index, carry):
-            for part in range(many):
-                trail(index * many + part)
+            trail(index * 2)
+            trail(index * 2 + 1)
             return carry
 
-        lax.fori_loop(0, points // many, trail_many, 0)
+        lax.fori_loop(0, points // per // 2, trail_many, 0)
 
     def finish(point):
         inverse = systems[point]
         right = rights[pl.ds(point, 1), :]
         forward = jnp.sum(inverse * right, axis=1, keepdims=True)
         mean = jnp.sum(inverse * forward, axis=0, keepdims=True)
-        own[point, 0:members, :] = (math.sqrt(members - 1.0) * inverse).astype(BF16)
-        own[point, members:, :] = jnp.broadcast_to(mean, (META, members)).astype(BF16)
+        scaled = (math.sqrt(members - 1.0) * inverse).astype(BF16)
+        line = jnp.broadcast_to(mean, (META, members))
+        if not folded:
+            out[point, 0:members, :] = scaled
+            out[point, members:, :] = line.astype(BF16)
+            return
+        upper = scaled[:half]
+        turned = jnp.concatenate([upper, upper], axis=0).T.astype(F32)[:half]
+        ready = jnp.where(spare, turned, scaled[half:].astype(F32))
+        diagonal = jnp.sum(jnp.where(on_diagonal, upper.astype(F32), 0.0), axis=0, keepdims=True)
+        label = arrived[point, locn:, :].astype(F32)
+        out[point, 0:half, :] = ready.astype(BF16)
+        out[point, half:, :] = jnp.where(
+            lane8 < 0,
+            0.0,
+            jnp.where(row8 == 0, line, jnp.where(row8 == 1, diagonal, label)),
+        ).astype(BF16)
+
+    half = members // 2
+    row_half = lax.broadcasted_iota(jnp.int32, (half, members), 0)
+    lane_half = lax.broadcasted_iota(jnp.int32, (half, members), 1)
+    spare = lane_half - half > row_half
+    on_diagonal = lane_half == row_half
+    row8 = lax.broadcasted_iota(jnp.int32, (META, members), 0)
 
     def finish_many(index, carry):
         for part in range(4):
@@ -240,32 +327,95 @@
         return carry
 
     lax.fori_loop(0, points // 4, finish_many, 0)
-    for index in range(TILES_LON):
-        north[index] = own[index]
-    for index in range(TILES_LAT):
-        east[index] = own[index * TILES_LON]
-    corner[0] = own[0]
-
-
-def solve(labels, arrived):
+
+
+def solve(arrived, points, folded):
     slots, rows, members = arrived.shape
-    points = TILES_LAT * TILES_LON
-    shape = lambda count: jax.ShapeDtypeStruct((count, members + META, members), BF16)
+    height = (members // 2 if folded else members) + META
     vmem = pl.BlockSpec(memory_space=pltpu.VMEM)
     return pl.pallas_call(
-        solve_kernel,
-        out_shape=(shape(points), shape(TILES_LAT), shape(TILES_LON), shape(1)),
-        in_specs=[pl.BlockSpec(memory_space=pltpu.SMEM), vmem],
-        out_specs=(vmem, vmem, vmem, vmem),
+        functools.partial(solve_kernel, folded),
+        out_shape=jax.ShapeDtypeStruct((points, height, members), BF16),
+        in_specs=[vmem],
+        out_specs=vmem,
         scratch_shapes=[
             pltpu.VMEM((points * members, members), F32),
             pltpu.VMEM((points, members), F32),
             pltpu.VMEM((2 * BLOCK * BLOCK // members, points, members), F32),
             pltpu.VMEM((points, BLOCK, members), F32),
         ],
-        compiler_params=pltpu.CompilerParams(vmem_limit_bytes=48 << 20),
-        name="solve",
-    )(labels, arrived)
+        compiler_params=pltpu.CompilerParams(vmem_limit_bytes=32 << 20),
+        cost_estimate=pl.CostEstimate(
+            flops=points * 60_000_000, bytes_accessed=points * 60_000, transcendentals=0
+        ),
+        name="solve_folded" if folded else "solve",
+    )(arrived)
+
+
+def merge_kernel(kept, *refs):
+    if kept:
+        solved, origin, folded, own, east, north, corner = refs
+    else:
+        solved, own, east, north, corner = refs
+    members = own.shape[2]
+    half = members // 2
+    row = lax.broadcasted_iota(jnp.int32, (half, members), 0)
+    lane = lax.broadcasted_iota(jnp.int32, (half, members), 1)
+    below = lane - half <= row
+
+    def unfolded(step, carry):
+        for part in range(4):
+            slot = step * 4 + part
+            meta = folded[slot, half:, :]
+            label = label_of(meta)
+            lines = folded[slot, 0:half, :].astype(F32)
+            spare = jnp.where(below, 0.0, lines).astype(BF16)
+            turned = jnp.concatenate([spare, spare], axis=0).T.astype(F32)[half:]
+            upper = jnp.where(
+                lane == row,
+                jnp.broadcast_to(meta.astype(F32)[1:2], (half, members)),
+                jnp.where(lane < half, turned, 0.0),
+            )
+            own[label, 0:half, :] = upper.astype(BF16)
+            own[label, half:members, :] = jnp.where(below, lines, 0.0).astype(BF16)
+            own[label, members:, :] = meta
+        return carry
+
+    def direct(step, carry):
+        for part in range(4):
+            slot = step * 4 + part
+            label = label_of(origin[slot, origin.shape[1] - META :, :])
+            own[label] = solved[slot]
+        return carry
+
+    if kept:
+        lax.fori_loop(0, solved.shape[0] // 4, direct, 0)
+        lax.fori_loop(0, folded.shape[0] // 4, unfolded, 0)
+    else:
+
+        @pl.loop(0, own.shape[0])
+        def _(label):
+            own[label] = solved[label]
+
+    for index in range(TILES_LON):
+        north[index] = own[index]
+    for index in range(TILES_LAT):
+        east[index] = own[index * TILES_LON]
+    corner[0] = own[0]
+
+
+def merge(*arrays):
+    members = arrays[0].shape[2]
+    shape = lambda count: jax.ShapeDtypeStruct((count, members + META, members), BF16)
+    vmem = pl.BlockSpec(memory_space=pltpu.VMEM)
+    return pl.pallas_call(
+        functools.partial(merge_kernel, len(arrays) > 1),
+        out_shape=(shape(TILES_LAT * TILES_LON), shape(TILES_LAT), shape(TILES_LON), shape(1)),
+        in_specs=[vmem] * len(arrays),
+        out_specs=(vmem,) * 4,
+        compiler_params=pltpu.CompilerParams(vmem_limit_bytes=32 << 20),
+        name="merge",
+    )(*arrays)
 
 
 def apply_kernel(
@@ -389,23 +539,24 @@
     holding, locn, members = obs_pert.shape
     capacity = max(1, (holding + devices - 1) // devices)
     columns = TILES_LON * lon_devices
-    live = jnp.arange(locn, dtype=jnp.int32)[None, :] < obs_count[:, None]
-    weight = jnp.where(live, obs_prec, jnp.zeros((), BF16))
-    within = owner_point // columns % TILES_LAT * TILES_LON + owner_point % TILES_LON
-    line = lax.broadcasted_iota(jnp.int32, (holding, META, members), 1)
-    meta = jnp.where(
-        line == 0,
-        jnp.concatenate([weight, weight], axis=1)[:, None, :],
-        jnp.where(
-            line == 1,
-            jnp.concatenate([obs_dep, obs_dep], axis=1)[:, None, :],
-            within.astype(BF16)[:, None, None],
-        ),
+    points = TILES_LAT * TILES_LON
+    kept = capacity // 2
+    sent = capacity - kept
+    if devices * capacity > points:
+        kept, sent = 0, capacity
+    packed = pack(
+        owner_point, obs_count, obs_pert, obs_prec, obs_dep, columns, lon_devices, devices, sent, kept
     )
-    packed = pack(owner_point, obs_pert, meta, columns, lon_devices, devices, capacity)
-    arrived = lax.all_to_all(packed, ("lat", "lon"), split_axis=0, concat_axis=0, tiled=True)
-    labels = arrived[:, locn + 2, 0].astype(jnp.int32)
-    own, east, north, corner = solve(labels, arrived)
+    exchange = functools.partial(
+        lax.all_to_all, axis_name=("lat", "lon"), split_axis=0, concat_axis=0, tiled=True
+    )
+    arrived = exchange(packed[0])
+    if kept:
+        folded = exchange(solve(packed[1], devices * kept, True))
+        solved = solve(arrived, devices * sent, False)
+        own, east, north, corner = merge(solved, arrived, folded)
+    else:
+        own, east, north, corner = merge(solve(arrived, points, False))
     lat_pairs = [(i, i - 1) for i in range(1, lat_devices)]
     lon_pairs = [(i, (i - 1) % lon_devices) for i in range(lon_devices)]
     both_pairs = [

time: 129 us -> 95.5 us (0.74)
  blocking collectives: 39.1 us -> 0 us
  starting transfers between devices: 4 us -> 15.9 us
  Pallas kernels: 70.8 us -> 64.5 us
  other arithmetic: 4.42 us -> 0 us
  local copies, waits for them, and re-layouts: 0.01 us -> 4.22 us
    all_to_all x1 -> x0, blocking collectives: 39.1 us -> none  [shards(): lax.all_to_all(packed, ('lat', 'lon'), split_axis=0, concat_axis=0, tiled...]
    all_to_all x0 -> x2, starting transfers between devices: none -> 12.9 us  [the longest x1 7.08 us: shards(): arrived = exchange(packed[0])]
    pallas_call x2 -> x4, Pallas kernels: 52.7 us -> 46.5 us  [the longest x2 38.4 us: solve(): pl.pallas_call(functools.partial(solve_kernel, folded), out_shape=jax.Sha...]
    unnamed x2 -> x8, local copies, waits for them, and re-layouts: 0.01 us -> 4.22 us
    convert_element_type x2 -> x0, other arithmetic: 1.9 us -> none  [the longest x1 1.23 us: shards(): labels = arrived[:, locn + 2, 0].astype(jnp.int32)]
    select_n x2 -> x0, other arithmetic: 1.63 us -> none  [the longest x1 0.83 us: shards(): jnp.where(line == 0, jnp.concatenate([weight, weight], axis=1)[:, None, :...]
  transfers between devices with their start and end apart: 3 -> 5, of which waited for: 1 -> 1; matrix products, arithmetic and copies ran while one was open for 0% -> 0% of each run, Pallas kernels for 0% -> 40%
where the time goes in v2:
time: 95.5 us; the launch traced here: 95 us
  Pallas kernels  64.5 us (68%)
  starting transfers between devices  15.9 us (17%)
  waiting for transfers between devices  9.65 us (10%)
  local copies, waits for them, and re-layouts  4.22 us (4%)
    pallas_call x2, Pallas kernels, solve(): pl.pallas_call(functools.partial(solve_kernel, folded), out_shape=jax.Sha...  38.4 us
    pallas_call x1, Pallas kernels, apply(): pl.pallas_call(apply_kernel, grid=(lags, TILES_LAT), out_shape=(jax.Shape...  18 us
    ppermute x1, waiting for transfers between devices, shards(): corner = lax.ppermute(corner, ('lat', 'lon'), both_pairs)  9.64 us
    all_to_all x1, starting transfers between devices, shards(): arrived = exchange(packed[0])  7.08 us
    all_to_all x1, starting transfers between devices, shards(): folded = exchange(solve(packed[1], devices * kept, True))  5.83 us
    pallas_call x1, Pallas kernels, pack(): pl.pallas_call(kernel, out_shape=(shape(sent), shape(kept)) if kept else...  5.16 us
    unnamed x8, local copies, waits for them, and re-layouts  4.22 us
    pallas_call x1, Pallas kernels, merge(): pl.pallas_call(functools.partial(merge_kernel, len(arrays) > 1), out_shap...  2.97 us
  transfers between devices with their start and end apart: 5, of which 1 were waited for; matrix products, arithmetic and copies ran while one was open for 0% of the time, Pallas kernels for 40%

profile of v2, /device:TPU:1, one launch (start us, length us, event | category | flops | bytes accessed | tf_op | source)
XLA Modules:
  0.0 95.0 jit_solution(7408304161277597558)
XLA Ops:
  0.6 5.2 %pack.1 = (bf16[32,72,128]{2,1,0:T(8,128)(2,1)}, bf16[32,72,128]{2,1,0:T(8,128)(2,1)}) custom-call(s32[64]{0:T(128)} %owner.1, s32[64]{0:T(128)} %count.1, bf16[64,64,128]{2,1,0:T(8,128)(2,1)} %pert.1, bf16[64,64]{1,0:T(8,128)(2,1)} %prec.1, bf16[64,64]{1,0:T(8,128)(2,1)} %dep.1), custom_call_target="tpu_custom_call" | custom-call | tf_op jit(solution)/shard_map/pack/pallas_call | solution.py:103
  5.8 7.1 %all-to-all-start = ((bf16[32,72,128]{2,1,0:T(8,128)(2,1)}), bf16[32,72,128]{2,1,0:T(8,128)(2,1)S(1)}, u32[]{:S(2)}, u32[]{:S(2)}) async-start(bf16[32,72,128]{2,1,0:T(8,128)(2,1)} %get-tuple-element.8), calls=%async_computation | async-start | bytes 1179648 | tf_op jit(solution)/shard_map/all_to_all | solution.py:553
  12.9 0.0 copy-start.3
  12.9 1.1 %copy-done.3 = bf16[32,72,128]{2,1,0:T(8,128)(2,1)S(1)} copy-done((bf16[32,72,128]{2,1,0:T(8,128)(2,1)S(1)}, bf16[32,72,128]{2,1,0:T(8,128)(2,1)}, u32[]{:S(2)}) %copy-start.3) | copy-done | bytes 589848
  14.0 19.7 %solve_folded.1 = bf16[32,72,128]{2,1,0:T(8,128)(2,1)} custom-call(bf16[32,72,128]{2,1,0:T(8,128)(2,1)S(1)} %copy-done.3), custom_call_target="tpu_custom_call" | custom-call | flops 1920000000 | bytes 1920000 | tf_op jit(solution)/shard_map/solve_folded/pallas_call | solution.py:336
  33.6 0.0 all-to-all-done.arrived.refs_1_
  33.6 5.8 %all-to-all-start.1 = ((bf16[32,72,128]{2,1,0:T(8,128)(2,1)}), bf16[32,72,128]{2,1,0:T(8,128)(2,1)S(1)}, u32[]{:S(2)}, u32[]{:S(2)}) async-start(bf16[32,72,128]{2,1,0:T(8,128)(2,1)} %solve_folded.1), calls=%async_computation.1 | async-start | bytes 1179648 | tf_op jit(solution)/shard_map/all_to_all | solution.py:555
  39.5 18.7 %solve.1.refs_0_ = bf16[32,136,128]{2,1,0:T(8,128)(2,1)S(1)} custom-call(bf16[32,72,128]{2,1,0:T(8,128)(2,1)S(1)} %all-to-all-done.arrived.refs_1_), custom_call_target="tpu_custom_call" | custom-call | flops 1920000000 | bytes 1920000 | tf_op jit(solution)/shard_map/solve/pallas_call | solution.py:336
  58.2 0.0 copy-start
  58.2 1.0 %copy-done = bf16[32,136,128]{2,1,0:T(8,128)(2,1)} copy-done((bf16[32,136,128]{2,1,0:T(8,128)(2,1)}, bf16[32,136,128]{2,1,0:T(8,128)(2,1)S(1)}, u32[]{:S(2)}) %copy-start) | copy-done | bytes 1114136
  59.2 0.0 all-to-all-done.1.refs_2_
  59.2 0.0 copy-start.1
  59.2 1.2 %copy-done.1 = bf16[32,136,128]{2,1,0:T(8,128)(2,1)S(1)} copy-done((bf16[32,136,128]{2,1,0:T(8,128)(2,1)S(1)}, bf16[32,136,128]{2,1,0:T(8,128)(2,1)}, u32[]{:S(2)}) %copy-start.1) | copy-done | bytes 1114136
  60.4 3.0 %merge.1 = (bf16[64,136,128]{2,1,0:T(8,128)(2,1)S(1)}, bf16[8,136,128]{2,1,0:T(8,128)(2,1)}, bf16[8,136,128]{2,1,0:T(8,128)(2,1)}, bf16[1,136,128]{2,1,0:T(8,128)(2,1)S(1)}) custom-call(bf16[32,136,128]{2,1,0:T(8,128)(2,1)S(1)} %copy-done.1, bf16[32,72,128]{2,1,0:T(8,128)(2,1)S(1)} %all-to-all-done.arrived.refs_1_, ...), custom_call_target="tpu_custom_call" | custom-call | tf_op jit(solution)/shard_map/merge/pallas_call | solution.py:411
  63.4 0.4 collective-permute-start
  63.8 1.3 %collective-permute-start.1 = (bf16[8,136,128]{2,1,0:T(8,128)(2,1)}, bf16[8,136,128]{2,1,0:T(8,128)(2,1)S(1)}, u32[]{:S(2)}, u32[]{:S(2)}) collective-permute-start(bf16[8,136,128]{2,1,0:T(8,128)(2,1)} %get-tuple-element.12), channel_id=1, source_target_pairs={{8,0},{16,8},{24,16},{9,1},{17,9},{25,17},{10,2},{18,10},{26,18},{... | collective-permute-start | bytes 835592 | tf_op jit(solution)/shard_map/ppermute | solution.py:566
  65.1 1.3 %collective-permute-start.2 = (bf16[1,136,128]{2,1,0:T(8,128)(2,1)S(1)}, bf16[1,136,128]{2,1,0:T(8,128)(2,1)S(1)}, u32[]{:S(2)}, u32[]{:S(2)}) collective-permute-start(bf16[1,136,128]{2,1,0:T(8,128)(2,1)S(1)} %get-tuple-element.13), channel_id=1, source_target_pairs={{8,7},{9,0},{10,1},{11,2},{12,3},{13,4},{14,5},{15,6},{16,15},{17,... | collective-permute-start | bytes 104456 | tf_op jit(solution)/shard_map/ppermute | solution.py:567
  66.4 9.6 %collective-permute-done.2.corner = bf16[1,136,128]{2,1,0:T(8,128)(2,1)S(1)} collective-permute-done((bf16[1,136,128]{2,1,0:T(8,128)(2,1)S(1)}, bf16[1,136,128]{2,1,0:T(8,128)(2,1)S(1)}, u32[]{:S(2)}, u32[]{:S(2)}) %collective-permute-start.2) | collective-permute-done | bytes 34848 | tf_op jit(solution)/shard_map/ppermute | solution.py:567
  76.1 0.0 collective-permute-done.east
  76.1 0.0 collective-permute-done.1.north
  76.1 0.0 copy-start.2
  76.1 0.9 copy-done.2
  77.0 18.0 %apply.1 = (bf16[1,200,200,128]{3,2,1,0:T(8,128)(2,1)}, f32[1,200,200]{2,1,0:T(8,128)}) custom-call(s32[1]{0:T(128)} %bitcast.top, bf16[64,136,128]{2,1,0:T(8,128)(2,1)S(1)} %get-tuple-element.10.own, bf16[8,136,128]{2,1,0:T(8,128)(2,1)S(1)} %collective-permute-done.east, bf16[8,136,128]{2,1,0:T(8,128)(2,1)S(1)} %collective-permute-done.1.north, ...), custom_call_target="tpu_custom_call" | custom-call | tf_op jit(solution)/shard_map/apply/pallas_call | solution.py:508
Async XLA Ops:
  5.8 27.8 %all-to-all-start = ((bf16[32,72,128]{2,1,0:T(8,128)(2,1)}), bf16[32,72,128]{2,1,0:T(8,128)(2,1)S(1)}, u32[]{:S(2)}, u32[]{:S(2)}) async-start(bf16[32,72,128]{2,1,0:T(8,128)(2,1)} %get-tuple-element.8), calls=%async_computation | async-start | bytes 1179648 | tf_op jit(solution)/shard_map/all_to_all | solution.py:553
  12.9 1.1 %copy-start.3 = (bf16[32,72,128]{2,1,0:T(8,128)(2,1)S(1)}, bf16[32,72,128]{2,1,0:T(8,128)(2,1)}, u32[]{:S(2)}) copy-start(bf16[32,72,128]{2,1,0:T(8,128)(2,1)} %get-tuple-element.9.arrived) | copy-start | bytes 1769476
  33.6 25.6 %all-to-all-start.1 = ((bf16[32,72,128]{2,1,0:T(8,128)(2,1)}), bf16[32,72,128]{2,1,0:T(8,128)(2,1)S(1)}, u32[]{:S(2)}, u32[]{:S(2)}) async-start(bf16[32,72,128]{2,1,0:T(8,128)(2,1)} %solve_folded.1), calls=%async_computation.1 | async-start | bytes 1179648 | tf_op jit(solution)/shard_map/all_to_all | solution.py:555
  58.2 1.0 %copy-start = (bf16[32,136,128]{2,1,0:T(8,128)(2,1)}, bf16[32,136,128]{2,1,0:T(8,128)(2,1)S(1)}, u32[]{:S(2)}) copy-start(bf16[32,136,128]{2,1,0:T(8,128)(2,1)S(1)} %solve.1.refs_0_) | copy-start | bytes 3342340
  59.2 1.2 %copy-start.1 = (bf16[32,136,128]{2,1,0:T(8,128)(2,1)S(1)}, bf16[32,136,128]{2,1,0:T(8,128)(2,1)}, u32[]{:S(2)}) copy-start(bf16[32,136,128]{2,1,0:T(8,128)(2,1)} %copy-done) | copy-start | bytes 3342340
  63.4 12.7 %collective-permute-start = (bf16[8,136,128]{2,1,0:T(8,128)(2,1)}, bf16[8,136,128]{2,1,0:T(8,128)(2,1)S(1)}, u32[]{:S(2)}, u32[]{:S(2)}) collective-permute-start(bf16[8,136,128]{2,1,0:T(8,128)(2,1)} %get-tuple-element.11), channel_id=1, source_target_pairs={{0,7},{1,0},{2,1},{3,2},{4,3},{5,4},{6,5},{7,6},{8,15},{9,8},{10,9... | collective-permute-start | bytes 835592 | tf_op jit(solution)/shard_map/ppermute | solution.py:565
  63.8 12.2 %collective-permute-start.1 = (bf16[8,136,128]{2,1,0:T(8,128)(2,1)}, bf16[8,136,128]{2,1,0:T(8,128)(2,1)S(1)}, u32[]{:S(2)}, u32[]{:S(2)}) collective-permute-start(bf16[8,136,128]{2,1,0:T(8,128)(2,1)} %get-tuple-element.12), channel_id=1, source_target_pairs={{8,0},{16,8},{24,16},{9,1},{17,9},{25,17},{10,2},{18,10},{26,18},{... | collective-permute-start | bytes 835592 | tf_op jit(solution)/shard_map/ppermute | solution.py:566
  65.1 11.0 %collective-permute-start.2 = (bf16[1,136,128]{2,1,0:T(8,128)(2,1)S(1)}, bf16[1,136,128]{2,1,0:T(8,128)(2,1)S(1)}, u32[]{:S(2)}, u32[]{:S(2)}) collective-permute-start(bf16[1,136,128]{2,1,0:T(8,128)(2,1)S(1)} %get-tuple-element.13), channel_id=1, source_target_pairs={{8,7},{9,0},{10,1},{11,2},{12,3},{13,4},{14,5},{15,6},{16,15},{17,... | collective-permute-start | bytes 104456 | tf_op jit(solution)/shard_map/ppermute | solution.py:567
  76.1 0.9 copy-start.2

commit v3 on v2

--- a/solution.py
+++ b/solution.py
@@ -28,88 +28,85 @@
     return lax.dot_general(left, right, dims, preferred_element_type=F32)
 
 
-def pack_kernel(
-    columns, lon_devices, sent, owner, count, pert, prec, dep, first, second, ranks, weights, departs
-):
+def quotient(value, by):
+    if by & (by - 1) == 0:
+        return value >> (by.bit_length() - 1), value & (by - 1)
+    return lax.div(value, jnp.int32(by)), lax.rem(value, jnp.int32(by))
+
+
+def place_of(point, columns, lon_devices):
+    point_row, point_col = quotient(point, columns)
+    device_row, tile_row = quotient(point_row, TILES_LAT)
+    device_col, tile_col = quotient(point_col, TILES_LON)
+    return device_row * lon_devices + device_col, tile_row * TILES_LON + tile_col
+
+
+def pack_kernel(columns, lon_devices, capacity, owner, count, pert, prec, dep, *refs):
+    outs, (ranks, weights, departs) = refs[:-3], refs[-3:]
     holding, locn, members = pert.shape
-    devices = first.shape[0] // sent
-
-    @pl.loop(0, devices)
-    def _(device):
-        ranks[device] = 0
-
     weights[...] = jnp.concatenate([prec[...], prec[...]], axis=1).astype(F32)
     departs[...] = jnp.concatenate([dep[...], dep[...]], axis=1).astype(F32)
-    slots = first.shape[0] + (0 if second is None else second.shape[0])
-    if slots > holding:
-
-        @pl.loop(0, first.shape[0])
-        def _(slot):
-            first[slot, locn:, :] = jnp.full((META, members), -1, BF16)
-
-        if second is not None:
-
-            @pl.loop(0, second.shape[0])
-            def _(slot):
-                second[slot, locn:, :] = jnp.full((META, members), -1, BF16)
-
     row = lax.broadcasted_iota(jnp.int32, (META, members), 0)
     slot_of_lane = lax.broadcasted_iota(jnp.int32, (META, members), 1) % locn
 
-    @pl.loop(0, holding)
-    def _(block):
-        point = owner[block]
-        point_row = point // columns
-        point_col = point % columns
-        device = point_row // TILES_LAT * lon_devices + point_col // TILES_LON
-        within = point_row % TILES_LAT * TILES_LON + point_col % TILES_LON
-        rank = ranks[device]
-        ranks[device] = rank + 1
+    def put(out, place, block, within):
         weight = jnp.broadcast_to(weights[pl.ds(block, 1), :], (META, members))
         depart = jnp.broadcast_to(departs[pl.ds(block, 1), :], (META, members))
-        meta = jnp.where(
+        out[place, 0:locn, :] = pert[block]
+        out[place, locn:, :] = jnp.where(
             row == 0,
             jnp.where(slot_of_lane < count[block], weight, 0.0),
             jnp.where(row == 1, depart, within.astype(F32)),
         ).astype(BF16)
 
-        def put(out, place):
-            out[place, 0:locn, :] = pert[block]
-            out[place, locn:, :] = meta
-
-        if second is None:
-            put(first, device * sent + jnp.minimum(rank, sent - 1))
-        else:
-            kept = second.shape[0] // devices
-
-            @pl.when(rank < sent)
-            def _():
-                put(first, device * sent + rank)
-
-            @pl.when(rank >= sent)
-            def _():
-                put(second, device * kept + jnp.minimum(rank - sent, kept - 1))
-
-
-def pack(owner, count, pert, prec, dep, columns, lon_devices, devices, sent, kept):
+    if len(outs) == 2:
+        @pl.loop(0, holding, unroll=4)
+        def _(block):
+            device, within = place_of(owner[block], columns, lon_devices)
+            put(outs[1], device, block, within)
+            other = holding - 1 - block
+            device, within = place_of(owner[other], columns, lon_devices)
+            put(outs[0], device, other, within)
+
+        return
+
+    slots = outs[0].shape[0]
+
+    @pl.loop(0, slots // capacity)
+    def _(device):
+        ranks[device] = 0
+
+    if slots > holding:
+
+        @pl.loop(0, slots)
+        def _(slot):
+            outs[0][slot, locn:, :] = jnp.full((META, members), -1, BF16)
+
+    @pl.loop(0, holding)
+    def _(block):
+        device, within = place_of(owner[block], columns, lon_devices)
+        rank = ranks[device]
+        ranks[device] = rank + 1
+        put(outs[0], device * capacity + jnp.minimum(rank, capacity - 1), block, within)
+
+
+def pack(owner, count, pert, prec, dep, columns, lon_devices, devices, capacity, halved):
     holding, locn, members = pert.shape
-    shape = lambda each: jax.ShapeDtypeStruct((devices * each, locn + META, members), BF16)
+    parts = 2 if halved else 1
+    shape = jax.ShapeDtypeStruct((devices * capacity // parts, locn + META, members), BF16)
     vmem = pl.BlockSpec(memory_space=pltpu.VMEM)
     smem = pl.BlockSpec(memory_space=pltpu.SMEM)
-    kernel = functools.partial(pack_kernel, columns, lon_devices, sent)
-    if not kept:
-        both = kernel
-        kernel = lambda *refs: both(*refs[:6], None, *refs[6:])
     return pl.pallas_call(
-        kernel,
-        out_shape=(shape(sent), shape(kept)) if kept else (shape(sent),),
+        functools.partial(pack_kernel, columns, lon_devices, capacity),
+        out_shape=(shape,) * parts,
         in_specs=[smem, smem, vmem, vmem, vmem],
-        out_specs=(vmem, vmem) if kept else (vmem,),
+        out_specs=(vmem,) * parts,
         scratch_shapes=[
             pltpu.SMEM((devices,), jnp.int32),
             pltpu.VMEM((holding, members), F32),
             pltpu.VMEM((holding, members), F32),
         ],
+        compiler_params=pltpu.CompilerParams(vmem_limit_bytes=12 << 20),
         name="pack",
     )(owner, count, pert, prec, dep)
 
@@ -344,7 +341,7 @@
             pltpu.VMEM((2 * BLOCK * BLOCK // members, points, members), F32),
             pltpu.VMEM((points, BLOCK, members), F32),
         ],
-        compiler_params=pltpu.CompilerParams(vmem_limit_bytes=32 << 20),
+        compiler_params=pltpu.CompilerParams(vmem_limit_bytes=16 << 20),
         cost_estimate=pl.CostEstimate(
             flops=points * 60_000_000, bytes_accessed=points * 60_000, transcendentals=0
         ),
@@ -413,7 +410,7 @@
         out_shape=(shape(TILES_LAT * TILES_LON), shape(TILES_LAT), shape(TILES_LON), shape(1)),
         in_specs=[vmem] * len(arrays),
         out_specs=(vmem,) * 4,
-        compiler_params=pltpu.CompilerParams(vmem_limit_bytes=32 << 20),
+        compiler_params=pltpu.CompilerParams(vmem_limit_bytes=16 << 20),
         name="merge",
     )(*arrays)
 
@@ -442,7 +439,8 @@
     for col in range(TILES_LON + 1):
         low = here(col)
         high = above(col)
-        change = (high[:members].astype(F32) - low[:members].astype(F32)).astype(BF16)
+        change = high[:members].astype(F32) - low[:members].astype(F32)
+        change = (change * (1.0 / FINE)).astype(BF16)
         place = slice(col * members, (col + 1) * members)
         weights[0, place, 0:members] = low[:members]
         weights[0, place, members:] = change
@@ -455,14 +453,14 @@
     offset = lax.broadcasted_iota(jnp.int32, (width, members), 0)
     for part, (start, stop) in enumerate(((0, half), (half, FINE))):
         count = stop - start
-        fraction = (
-            lax.broadcasted_iota(jnp.int32, (count, width, members), 0) + start
-        ).astype(F32) / FINE - part
+        number = jnp.concatenate(
+            [jnp.full((1, width, members), line - part * FINE, BF16) for line in range(start, stop)]
+        )
         carry = None
         for col in range(TILES_LON):
             begin = col * (FINE - 1)
             field = anomalies[0, start:stop, begin : begin + width, :]
-            scaled = (field.astype(F32) * fraction).astype(BF16)
+            scaled = field * number
             left = jnp.concatenate([field, scaled], axis=2).reshape(count * width, 2 * members)
             place = slice(col * members, (col + 2) * members)
             both = dot(left, weights[part, place, :], NT).reshape(count, width, 2 * members)
@@ -527,7 +525,7 @@
             pltpu.VMEM((32, members), F32),
             pltpu.VMEM((16, cols), F32),
         ],
-        compiler_params=pltpu.CompilerParams(vmem_limit_bytes=48 << 20),
+        compiler_params=pltpu.CompilerParams(vmem_limit_bytes=32 << 20),
         name="apply",
     )(top, own, east, north, corner, anomalies, flux)
 
@@ -540,20 +538,18 @@
     capacity = max(1, (holding + devices - 1) // devices)
     columns = TILES_LON * lon_devices
     points = TILES_LAT * TILES_LON
-    kept = capacity // 2
-    sent = capacity - kept
-    if devices * capacity > points:
-        kept, sent = 0, capacity
+    halved = capacity == 2 and devices * capacity == holding == points
     packed = pack(
-        owner_point, obs_count, obs_pert, obs_prec, obs_dep, columns, lon_devices, devices, sent, kept
+        owner_point, obs_count, obs_pert, obs_prec, obs_dep,
+        columns, lon_devices, devices, capacity, halved,
     )
     exchange = functools.partial(
         lax.all_to_all, axis_name=("lat", "lon"), split_axis=0, concat_axis=0, tiled=True
     )
     arrived = exchange(packed[0])
-    if kept:
-        folded = exchange(solve(packed[1], devices * kept, True))
-        solved = solve(arrived, devices * sent, False)
+    if halved:
+        folded = exchange(solve(packed[1], points // 2, True))
+        solved = solve(arrived, points // 2, False)
         own, east, north, corner = merge(solved, arrived, folded)
     else:
         own, east, north, corner = merge(solve(arrived, points, False))

time: 95.5 us -> 98.2 us (1.028)
  local copies, waits for them, and re-layouts: 4.22 us -> 11 us
  Pallas kernels: 64.5 us -> 60.3 us
    unnamed x8 -> x18, local copies, waits for them, and re-layouts: 4.22 us -> 11 us
    pallas_call x1, Pallas kernels: 5.16 us -> 2.14 us  [pack(): pl.pallas_call(functools.partial(pack_kernel, columns, lon_devices, capac...]
    pallas_call x1, Pallas kernels: 18 us -> 16.7 us  [apply(): pl.pallas_call(apply_kernel, grid=(lags, TILES_LAT), out_shape=(jax.Shape...]
  transfers between devices with their start and end apart: 5 -> 5, of which waited for: 1 -> 1; matrix products, arithmetic and copies ran while one was open for 0% -> 0% of each run, Pallas kernels for 40% -> 39%
where the time goes in v3:
time: 98.2 us; the launch traced here: 97.6 us
  Pallas kernels  60.3 us (61%)
  starting transfers between devices  15.9 us (16%)
  local copies, waits for them, and re-layouts  11 us (11%)
  waiting for transfers between devices  9.67 us (10%)
    pallas_call x2, Pallas kernels, solve(): pl.pallas_call(functools.partial(solve_kernel, folded), out_shape=jax.Sha...  38.4 us
    pallas_call x1, Pallas kernels, apply(): pl.pallas_call(apply_kernel, grid=(lags, TILES_LAT), out_shape=(jax.Shape...  16.7 us
    unnamed x18, local copies, waits for them, and re-layouts  11 us
    ppermute x1, waiting for transfers between devices, shards(): corner = lax.ppermute(corner, ('lat', 'lon'), both_pairs)  9.66 us
    all_to_all x1, starting transfers between devices, shards(): arrived = exchange(packed[0])  7.08 us
    all_to_all x1, starting transfers between devices, shards(): folded = exchange(solve(packed[1], points // 2, True))  5.84 us
    pallas_call x1, Pallas kernels, merge(): pl.pallas_call(functools.partial(merge_kernel, len(arrays) > 1), out_shap...  2.98 us
    pallas_call x1, Pallas kernels, pack(): pl.pallas_call(functools.partial(pack_kernel, columns, lon_devices, capac...  2.14 us
  transfers between devices with their start and end apart: 5, of which 1 were waited for; matrix products, arithmetic and copies ran while one was open for 0% of the time, Pallas kernels for 39%

profile of v3, /device:TPU:1, one launch (start us, length us, event | category | flops | bytes accessed | tf_op | source)
XLA Modules:
  0.0 97.6 jit_solution(12556677317820029905)
XLA Ops:
  0.6 0.0 copy-start.3
  0.6 1.2 %copy-done.3 = bf16[64,64,128]{2,1,0:T(8,128)(2,1)S(1)} copy-done((bf16[64,64,128]{2,1,0:T(8,128)(2,1)S(1)}, bf16[64,64,128]{2,1,0:T(8,128)(2,1)}, u32[]{:S(2)}) %copy-start.3) | copy-done | bytes 1048600
  1.9 0.0 copy-start.5
  1.9 0.7 copy-done.5
  2.6 0.0 copy-start.6
  2.6 0.7 copy-done.6
  3.3 0.0 copy-start.7
  3.3 0.7 copy-done.7
  3.9 0.0 copy-start.8
  4.0 0.7 copy-done.8
  4.6 2.1 %pack.1 = (bf16[32,72,128]{2,1,0:T(8,128)(2,1)}, bf16[32,72,128]{2,1,0:T(8,128)(2,1)S(1)}) custom-call(s32[64]{0:T(128)S(1)} %copy-done.7, s32[64]{0:T(128)S(1)} %copy-done.8, bf16[64,64,128]{2,1,0:T(8,128)(2,1)S(1)} %copy-done.3, bf16[64,64]{1,0:T(8,128)(2,1)S(1)} %copy-done.5, bf16[64,64]{1,0:T(8,128)(2,1)S(1)} %copy-done.6), custom_call_target="tpu_custom_call" | custom-call | tf_op jit(solution)/shard_map/pack/pallas_call | solution.py:99
  6.7 7.1 %all-to-all-start = ((bf16[32,72,128]{2,1,0:T(8,128)(2,1)}), bf16[32,72,128]{2,1,0:T(8,128)(2,1)S(1)}, u32[]{:S(2)}, u32[]{:S(2)}) async-start(bf16[32,72,128]{2,1,0:T(8,128)(2,1)} %get-tuple-element.8), calls=%async_computation | async-start | bytes 1179648 | tf_op jit(solution)/shard_map/all_to_all | solution.py:549
  13.8 19.7 %solve_folded.1 = bf16[32,72,128]{2,1,0:T(8,128)(2,1)} custom-call(bf16[32,72,128]{2,1,0:T(8,128)(2,1)S(1)} %get-tuple-element.9.arrived), custom_call_target="tpu_custom_call" | custom-call | flops 1920000000 | bytes 1920000 | tf_op jit(solution)/shard_map/solve_folded/pallas_call | solution.py:333
  33.5 0.0 all-to-all-done.arrived.refs_1_
  33.5 5.8 %all-to-all-start.1 = ((bf16[32,72,128]{2,1,0:T(8,128)(2,1)}), bf16[32,72,128]{2,1,0:T(8,128)(2,1)S(1)}, u32[]{:S(2)}, u32[]{:S(2)}) async-start(bf16[32,72,128]{2,1,0:T(8,128)(2,1)} %solve_folded.1), calls=%async_computation.1 | async-start | bytes 1179648 | tf_op jit(solution)/shard_map/all_to_all | solution.py:551
  39.4 18.7 %solve.1.refs_0_ = bf16[32,136,128]{2,1,0:T(8,128)(2,1)S(1)} custom-call(bf16[32,72,128]{2,1,0:T(8,128)(2,1)S(1)} %all-to-all-done.arrived.refs_1_), custom_call_target="tpu_custom_call" | custom-call | flops 1920000000 | bytes 1920000 | tf_op jit(solution)/shard_map/solve/pallas_call | solution.py:333
  58.1 0.0 copy-start.1
  58.1 1.0 %copy-done.1 = bf16[32,136,128]{2,1,0:T(8,128)(2,1)} copy-done((bf16[32,136,128]{2,1,0:T(8,128)(2,1)}, bf16[32,136,128]{2,1,0:T(8,128)(2,1)S(1)}, u32[]{:S(2)}) %copy-start.1) | copy-done | bytes 1114136
  59.1 0.0 all-to-all-done.1.refs_2_
  59.1 0.0 copy-start.2
  59.1 1.2 %copy-done.2 = bf16[32,136,128]{2,1,0:T(8,128)(2,1)S(1)} copy-done((bf16[32,136,128]{2,1,0:T(8,128)(2,1)S(1)}, bf16[32,136,128]{2,1,0:T(8,128)(2,1)}, u32[]{:S(2)}) %copy-start.2) | copy-done | bytes 1114136
  60.3 3.0 %merge.1 = (bf16[64,136,128]{2,1,0:T(8,128)(2,1)S(1)}, bf16[8,136,128]{2,1,0:T(8,128)(2,1)}, bf16[8,136,128]{2,1,0:T(8,128)(2,1)}, bf16[1,136,128]{2,1,0:T(8,128)(2,1)S(1)}) custom-call(bf16[32,136,128]{2,1,0:T(8,128)(2,1)S(1)} %copy-done.2, bf16[32,72,128]{2,1,0:T(8,128)(2,1)S(1)} %all-to-all-done.arrived.refs_1_, ...), custom_call_target="tpu_custom_call" | custom-call | tf_op jit(solution)/shard_map/merge/pallas_call | solution.py:408
  63.3 0.4 collective-permute-start
  63.7 1.3 %collective-permute-start.1 = (bf16[8,136,128]{2,1,0:T(8,128)(2,1)}, bf16[8,136,128]{2,1,0:T(8,128)(2,1)S(1)}, u32[]{:S(2)}, u32[]{:S(2)}) collective-permute-start(bf16[8,136,128]{2,1,0:T(8,128)(2,1)} %get-tuple-element.12), channel_id=1, source_target_pairs={{8,0},{16,8},{24,16},{9,1},{17,9},{25,17},{10,2},{18,10},{26,18},{... | collective-permute-start | bytes 835592 | tf_op jit(solution)/shard_map/ppermute | solution.py:562
  65.0 1.3 %collective-permute-start.2 = (bf16[1,136,128]{2,1,0:T(8,128)(2,1)S(1)}, bf16[1,136,128]{2,1,0:T(8,128)(2,1)S(1)}, u32[]{:S(2)}, u32[]{:S(2)}) collective-permute-start(bf16[1,136,128]{2,1,0:T(8,128)(2,1)S(1)} %get-tuple-element.13), channel_id=1, source_target_pairs={{8,7},{9,0},{10,1},{11,2},{12,3},{13,4},{14,5},{15,6},{16,15},{17,... | collective-permute-start | bytes 104456 | tf_op jit(solution)/shard_map/ppermute | solution.py:563
  66.3 9.7 %collective-permute-done.2.corner = bf16[1,136,128]{2,1,0:T(8,128)(2,1)S(1)} collective-permute-done((bf16[1,136,128]{2,1,0:T(8,128)(2,1)S(1)}, bf16[1,136,128]{2,1,0:T(8,128)(2,1)S(1)}, u32[]{:S(2)}, u32[]{:S(2)}) %collective-permute-start.2) | collective-permute-done | bytes 34848 | tf_op jit(solution)/shard_map/ppermute | solution.py:563
  76.0 0.0 collective-permute-done.east
  76.0 0.0 collective-permute-done.1.north
  76.0 0.0 copy-start
  76.0 3.9 %copy-done = bf16[1,200,200,128]{3,2,1,0:T(8,128)(2,1)S(1)} copy-done((bf16[1,200,200,128]{3,2,1,0:T(8,128)(2,1)S(1)}, bf16[1,200,200,128]{3,2,1,0:T(8,128)(2,1)}, u32[]{:S(2)}) %copy-start) | copy-done | bytes 10240024
  79.9 0.0 copy-start.4
  79.9 0.9 copy-done.4
  80.8 16.7 %apply.1 = (bf16[1,200,200,128]{3,2,1,0:T(8,128)(2,1)}, f32[1,200,200]{2,1,0:T(8,128)}) custom-call(s32[1]{0:T(128)} %bitcast.top, bf16[64,136,128]{2,1,0:T(8,128)(2,1)S(1)} %get-tuple-element.10.own, bf16[8,136,128]{2,1,0:T(8,128)(2,1)S(1)} %collective-permute-done.east, bf16[8,136,128]{2,1,0:T(8,128)(2,1)S(1)} %collective-permute-done.1.north, ...), custom_call_target="tpu_custom_call" | custom-call | tf_op jit(solution)/shard_map/apply/pallas_call | solution.py:506
Async XLA Ops:
  0.6 1.2 %copy-start.3 = (bf16[64,64,128]{2,1,0:T(8,128)(2,1)S(1)}, bf16[64,64,128]{2,1,0:T(8,128)(2,1)}, u32[]{:S(2)}) copy-start(bf16[64,64,128]{2,1,0:T(8,128)(2,1)} %pert.1) | copy-start | bytes 3145732
  1.9 0.7 copy-start.5
  2.6 0.7 copy-start.6
  3.3 0.7 copy-start.7
  3.9 0.7 copy-start.8
  6.7 26.8 %all-to-all-start = ((bf16[32,72,128]{2,1,0:T(8,128)(2,1)}), bf16[32,72,128]{2,1,0:T(8,128)(2,1)S(1)}, u32[]{:S(2)}, u32[]{:S(2)}) async-start(bf16[32,72,128]{2,1,0:T(8,128)(2,1)} %get-tuple-element.8), calls=%async_computation | async-start | bytes 1179648 | tf_op jit(solution)/shard_map/all_to_all | solution.py:549
  33.5 25.6 %all-to-all-start.1 = ((bf16[32,72,128]{2,1,0:T(8,128)(2,1)}), bf16[32,72,128]{2,1,0:T(8,128)(2,1)S(1)}, u32[]{:S(2)}, u32[]{:S(2)}) async-start(bf16[32,72,128]{2,1,0:T(8,128)(2,1)} %solve_folded.1), calls=%async_computation.1 | async-start | bytes 1179648 | tf_op jit(solution)/shard_map/all_to_all | solution.py:551
  58.1 1.0 %copy-start.1 = (bf16[32,136,128]{2,1,0:T(8,128)(2,1)}, bf16[32,136,128]{2,1,0:T(8,128)(2,1)S(1)}, u32[]{:S(2)}) copy-start(bf16[32,136,128]{2,1,0:T(8,128)(2,1)S(1)} %solve.1.refs_0_) | copy-start | bytes 3342340
  59.1 1.2 %copy-start.2 = (bf16[32,136,128]{2,1,0:T(8,128)(2,1)S(1)}, bf16[32,136,128]{2,1,0:T(8,128)(2,1)}, u32[]{:S(2)}) copy-start(bf16[32,136,128]{2,1,0:T(8,128)(2,1)} %copy-done.1) | copy-start | bytes 3342340
  63.3 12.7 %collective-permute-start = (bf16[8,136,128]{2,1,0:T(8,128)(2,1)}, bf16[8,136,128]{2,1,0:T(8,128)(2,1)S(1)}, u32[]{:S(2)}, u32[]{:S(2)}) collective-permute-start(bf16[8,136,128]{2,1,0:T(8,128)(2,1)} %get-tuple-element.11), channel_id=1, source_target_pairs={{0,7},{1,0},{2,1},{3,2},{4,3},{5,4},{6,5},{7,6},{8,15},{9,8},{10,9... | collective-permute-start | bytes 835592 | tf_op jit(solution)/shard_map/ppermute | solution.py:561
  63.7 12.3 %collective-permute-start.1 = (bf16[8,136,128]{2,1,0:T(8,128)(2,1)}, bf16[8,136,128]{2,1,0:T(8,128)(2,1)S(1)}, u32[]{:S(2)}, u32[]{:S(2)}) collective-permute-start(bf16[8,136,128]{2,1,0:T(8,128)(2,1)} %get-tuple-element.12), channel_id=1, source_target_pairs={{8,0},{16,8},{24,16},{9,1},{17,9},{25,17},{10,2},{18,10},{26,18},{... | collective-permute-start | bytes 835592 | tf_op jit(solution)/shard_map/ppermute | solution.py:562
  65.0 11.0 %collective-permute-start.2 = (bf16[1,136,128]{2,1,0:T(8,128)(2,1)S(1)}, bf16[1,136,128]{2,1,0:T(8,128)(2,1)S(1)}, u32[]{:S(2)}, u32[]{:S(2)}) collective-permute-start(bf16[1,136,128]{2,1,0:T(8,128)(2,1)S(1)} %get-tuple-element.13), channel_id=1, source_target_pairs={{8,7},{9,0},{10,1},{11,2},{12,3},{13,4},{14,5},{15,6},{16,15},{17,... | collective-permute-start | bytes 104456 | tf_op jit(solution)/shard_map/ppermute | solution.py:563
  76.0 3.9 %copy-start = (bf16[1,200,200,128]{3,2,1,0:T(8,128)(2,1)S(1)}, bf16[1,200,200,128]{3,2,1,0:T(8,128)(2,1)}, u32[]{:S(2)}) copy-start(bf16[1,200,200,128]{3,2,1,0:T(8,128)(2,1)} %anomalies.1) | copy-start | bytes 30720004
  79.9 0.9 copy-start.4

commit v4 on v3

--- a/solution.py
+++ b/solution.py
@@ -106,7 +106,6 @@
             pltpu.VMEM((holding, members), F32),
             pltpu.VMEM((holding, members), F32),
         ],
-        compiler_params=pltpu.CompilerParams(vmem_limit_bytes=12 << 20),
         name="pack",
     )(owner, count, pert, prec, dep)
 
@@ -149,11 +148,11 @@
             put(slot)
 
     def several(step, carry):
-        for part in range(4):
-            one(step * 4 + part)
+        for part in range(8):
+            one(step * 8 + part)
         return carry
 
-    lax.fori_loop(0, slots // 4, several, 0)
+    lax.fori_loop(0, slots // 8, several, 0)
 
 
 def diagonal_inverses(step, systems2d, factors, points, members):
@@ -170,28 +169,44 @@
         turned = packed.T
         for inner in range(per):
             rows.append(turned[size * inner : size * (inner + 1)])
-    sub = lax.broadcasted_iota(jnp.int32, (size, points), 0)
+    half = size // 2
+    sub = lax.broadcasted_iota(jnp.int32, (half, points), 0)
+    rows = [[line[:half], line[half:]] for line in rows]
+    spread = lambda line, k: jnp.broadcast_to(
+        line[k // half][k % half : k % half + 1], (half, points)
+    )
     roots = []
     for k in range(size):
-        pivot = jnp.broadcast_to(rows[k][k : k + 1], (size, points))
-        root = lax.rsqrt(pivot)
+        part = k // half
+        root = lax.rsqrt(spread(rows[k], k))
         inverse = root * root
         roots.append(root)
-        line = jnp.where(sub == k, 1.0, rows[k])
-        scaled = line * inverse
+        factors_k = [spread(rows[k], i) for i in range(k + 1, size)]
+        line = list(rows[k])
+        line[part] = jnp.where(sub == k % half, 1.0, line[part])
+        line = [piece * inverse for piece in line]
         for i in range(k + 1, size):
-            factor = jnp.broadcast_to(rows[i][k : k + 1], (size, points))
-            rows[i] = jnp.where(sub == k, 0.0, rows[i]) - factor * scaled
+            rows[i][part] = jnp.where(sub == k % half, 0.0, rows[i][part])
+            rows[i] = [old - factors_k[i - k - 1] * piece for old, piece in zip(rows[i], line)]
     lower = []
     for i in range(size):
-        line = jnp.where(sub < i, rows[i], jnp.where(sub == i, 1.0, 0.0))
-        lower.append(line * roots[i])
+        part = i // half
+        line = [piece * roots[i] for piece in rows[i][: part + 1]]
+        line[part] = jnp.where(
+            sub < i % half, line[part], jnp.where(sub == i % half, roots[i], 0.0)
+        )
+        lower.append(line)
+    nothing = jnp.zeros((half, points), F32)
     whole = []
     for i in range(size):
-        total = jnp.zeros((size, points), F32)
+        total = [nothing, nothing]
         for l in range(i, size):
-            total += jnp.broadcast_to(lower[l][i : i + 1], (size, points)) * lower[l]
-        whole.append(total)
+            factor = spread(lower[l], i)
+            for piece in range(l // half + 1):
+                term = factor * lower[l][piece]
+                total[piece] = term if l == i or (piece and l == half) else total[piece] + term
+        whole.append(jnp.concatenate(total, axis=0))
+    lower = [jnp.concatenate((line + [nothing])[:2], axis=0) for line in lower]
     for group in range(size // per):
         part = slice(group * per, (group + 1) * per)
         factors[group] = jnp.concatenate(whole[part][::-1], axis=0).T
@@ -226,23 +241,26 @@
         both = dot(jnp.concatenate(split(left), axis=1), right)
         return both[:, :members] + both[:, members:]
 
+    diagonal_inverses(0, systems2d, factors, points, members)
     for step in range(members // size):
-        diagonal_inverses(step, systems2d, factors, points, members)
         first = step * size
         after = first + size
         here = (lane >= first) & (lane < after)
         unit = jnp.where(lane - first == row, 1.0, 0.0)
 
         def small(index):
-            start = pl.multiple_of(index * per, per)
+            start = index * per
             parts = []
             for inner in range(per):
                 for group in range(groups):
                     lines = jnp.broadcast_to(
                         factors[group, pl.ds(start + inner, 1), :], (per, members)
                     )
-                    lines = pltpu.roll(lines, 0, 1, stride=size, stride_axis=0)
-                    lines = pltpu.roll(lines, (size * (inner - per + 1)) % members, 1)
+                    move = (size * (inner - per + 1)) % members
+                    direct = move if move <= size else 0
+                    lines = pltpu.roll(lines, direct, 1, stride=size, stride_axis=0)
+                    if move != direct:
+                        lines = pltpu.roll(lines, move, 1)
                     parts.append(jnp.where(lane8 // size == inner, lines, 0.0))
             slab = systems[pl.ds(start, per), first:after, :].reshape(members, members)
             right = halves(jnp.where(here, unit, slab))
@@ -254,39 +272,34 @@
                     lane[:size] < after, both[begin + size : begin + 2 * size], 0.0
                 )
 
-        def small_many(index, carry):
-            small(index * 2)
-            small(index * 2 + 1)
-            return carry
-
-        lax.fori_loop(0, points // per // 2, small_many, 0)
+        for index in range(points // per):
+            small(index)
         if after == members:
             continue
-        rest = members - after
-        lane_rest = lax.broadcasted_iota(jnp.int32, (rest, members), 1)
-        here_rest = (lane_rest >= first) & (lane_rest < after)
-
-        def trail(index):
-            start = pl.multiple_of(index * per, per)
+        def trail(index, begin, stop):
+            start = index * per
+            rest = stop - begin
+            lane_rest = lax.broadcasted_iota(jnp.int32, (rest, members), 1)
+            here_rest = (lane_rest >= first) & (lane_rest < after)
             right = halves(slabs[pl.ds(start, per)].reshape(members, members))
             parts = []
             for inner in range(per):
-                old = systems[start + inner, after:, :]
+                old = systems[start + inner, begin:stop, :]
                 moved = pltpu.roll(old, (size * (inner - step)) % members, 1)
                 parts.append(jnp.where(lane_rest // size == inner, moved, 0.0))
             change = product(jnp.concatenate(parts, axis=0), right)
             for inner in range(per):
-                old = systems[start + inner, after:, :]
-                systems[start + inner, after:, :] = (
+                old = systems[start + inner, begin:stop, :]
+                systems[start + inner, begin:stop, :] = (
                     jnp.where(here_rest, 0.0, old) - change[inner * rest : (inner + 1) * rest]
                 )
 
-        def trail_many(index, carry):
-            trail(index * 2)
-            trail(index * 2 + 1)
-            return carry
-
-        lax.fori_loop(0, points // per // 2, trail_many, 0)
+        for index in range(points // per):
+            trail(index, after, after + size)
+        diagonal_inverses(step + 1, systems2d, factors, points, members)
+        if after + size < members:
+            for index in range(points // per):
+                trail(index, after + size, members)
 
     def finish(point):
         inverse = systems[point]
@@ -319,11 +332,11 @@
     row8 = lax.broadcasted_iota(jnp.int32, (META, members), 0)
 
     def finish_many(index, carry):
-        for part in range(4):
-            finish(index * 4 + part)
+        for part in range(8):
+            finish(index * 8 + part)
         return carry
 
-    lax.fori_loop(0, points // 4, finish_many, 0)
+    lax.fori_loop(0, points // 8, finish_many, 0)
 
 
 def solve(arrived, points, folded):
@@ -341,7 +354,6 @@
             pltpu.VMEM((2 * BLOCK * BLOCK // members, points, members), F32),
             pltpu.VMEM((points, BLOCK, members), F32),
         ],
-        compiler_params=pltpu.CompilerParams(vmem_limit_bytes=16 << 20),
         cost_estimate=pl.CostEstimate(
             flops=points * 60_000_000, bytes_accessed=points * 60_000, transcendentals=0
         ),
@@ -410,31 +422,36 @@
         out_shape=(shape(TILES_LAT * TILES_LON), shape(TILES_LAT), shape(TILES_LON), shape(1)),
         in_specs=[vmem] * len(arrays),
         out_specs=(vmem,) * 4,
-        compiler_params=pltpu.CompilerParams(vmem_limit_bytes=16 << 20),
         name="merge",
     )(*arrays)
 
 
-def apply_kernel(
-    top, own, east, north, corner, anomalies, flux, out, mean, weights, means, hats
-):
+def apply_kernel(first, *refs):
+    last = first == TILES_LAT - 1
+    if last:
+        top, own, east, north, corner, anomalies, flux, _, before, *refs = refs
+    else:
+        own, east, anomalies, flux, *refs = refs
+    out, mean, weights, means = refs
     members = anomalies.shape[3]
     cols = anomalies.shape[2]
-    tile_row = pl.program_id(1)
-    is_top = top[0] == 1
-    last = tile_row == TILES_LAT - 1
+    tile_row = pl.program_id(1) + first
+    if last:
+        mean[...] = before[...]
+
+    def inner(row, col):
+        return own[row * TILES_LON + col] if col < TILES_LON else east[row]
+
+    def here(col):
+        return inner(tile_row, col)
+
+    def above(col):
+        if not last:
+            return inner(tile_row + 1, col)
+        outer = north[col] if col < TILES_LON else corner[0]
+        return jnp.where(top[0] == 1, inner(TILES_LAT - 1, col), outer)
+
     half = (FINE + 1) // 2
-
-    def here(col):
-        if col < TILES_LON:
-            return own[tile_row * TILES_LON + col]
-        return east[tile_row]
-
-    def above(col):
-        ahead = jnp.minimum(tile_row + 1, TILES_LAT - 1)
-        inner = own[ahead * TILES_LON + col] if col < TILES_LON else east[ahead]
-        outer = north[col] if col < TILES_LON else corner[0]
-        return jnp.where(last & jnp.logical_not(is_top), outer, inner)
 
     for col in range(TILES_LON + 1):
         low = here(col)
@@ -498,36 +515,41 @@
         mean[0, place, :] = flux[0, place, :] + shift
 
 
-def apply(top, own, east, north, corner, anomalies, flux):
+def apply(first, count, operands, anomalies, flux, earlier=()):
     lags, rows, cols, members = anomalies.shape
     whole = lambda array: pl.BlockSpec(array.shape, lambda l, r: (0,) * array.ndim)
-    strip = pl.BlockSpec((1, FINE, cols, members), lambda l, r: (l, r, 0, 0))
+    strip = pl.BlockSpec((1, FINE, cols, members), lambda l, r: (l, r + first, 0, 0))
     plane = pl.BlockSpec((1, rows, cols), lambda l, r: (l, 0, 0))
+    specs = [
+        pl.BlockSpec(memory_space=pltpu.SMEM) if array.ndim == 1 else whole(array)
+        for array in operands
+    ] + [strip, plane]
+    aliases = {}
+    if earlier:
+        aliases = {len(specs): 0, len(specs) + 1: 1}
+        specs += [pl.BlockSpec(memory_space=pl.ANY), plane]
+    cells = count * FINE * cols * lags
     return pl.pallas_call(
-        apply_kernel,
-        grid=(lags, TILES_LAT),
+        functools.partial(apply_kernel, first),
+        grid=(lags, count),
         out_shape=(
             jax.ShapeDtypeStruct(anomalies.shape, BF16),
             jax.ShapeDtypeStruct(flux.shape, F32),
         ),
-        in_specs=[
-            pl.BlockSpec(memory_space=pltpu.SMEM),
-            whole(own),
-            whole(east),
-            whole(north),
-            whole(corner),
-            strip,
-            plane,
-        ],
+        in_specs=specs,
         out_specs=(strip, plane),
         scratch_shapes=[
             pltpu.VMEM((2, (TILES_LON + 1) * members, 2 * members), BF16),
             pltpu.VMEM((32, members), F32),
-            pltpu.VMEM((16, cols), F32),
         ],
-        compiler_params=pltpu.CompilerParams(vmem_limit_bytes=32 << 20),
-        name="apply",
-    )(top, own, east, north, corner, anomalies, flux)
+        input_output_aliases=aliases,
+        cost_estimate=pl.CostEstimate(
+            flops=cells * members * members * 8,
+            bytes_accessed=cells * members * 4,
+            transcendentals=0,
+        ),
+        name="apply_last" if earlier else "apply",
+    )(*operands, anomalies, flux, *earlier)
 
 
 def shards(obs_pert, obs_dep, obs_prec, obs_count, owner_point, anomalies, flux_mean):
@@ -562,7 +584,10 @@
     north = lax.ppermute(north, "lat", lat_pairs)
     corner = lax.ppermute(corner, ("lat", "lon"), both_pairs)
     top = (lax.axis_index("lat") == lat_devices - 1).astype(jnp.int32).reshape(1)
-    return apply(top, own, east, north, corner, anomalies, flux_mean)
+    inside = apply(0, TILES_LAT - 1, (own, east), anomalies, flux_mean)
+    return apply(
+        TILES_LAT - 1, 1, (top, own, east, north, corner), anomalies, flux_mean, inside
+    )
 
 
 def solution(mesh):

time: 98.2 us -> 83.8 us (0.85)
  local copies, waits for them, and re-layouts: 11 us -> 2.24 us
  waiting for transfers between devices: 9.67 us -> 6.89 us
  starting transfers between devices: 15.9 us -> 14.4 us
  Pallas kernels: 60.3 us -> 59.1 us
    ppermute x1, waiting for transfers between devices: 9.66 us -> 0.01 us  [shards(): corner = lax.ppermute(corner, ('lat', 'lon'), both_pairs)]
    pallas_call x2, Pallas kernels: 38.4 us -> 29.3 us  [solve(): pl.pallas_call(functools.partial(solve_kernel, folded), out_shape=jax.Sha...]
    unnamed x18 -> x10, local copies, waits for them, and re-layouts: 11 us -> 2.24 us
    pallas_call x1 -> x2, Pallas kernels: 16.7 us -> 21.4 us  [apply(): pl.pallas_call(functools.partial(apply_kernel, first), grid=(lags, count)...]
    ppermute x1, waiting for transfers between devices: 0.01 us -> 3.15 us  [shards(): east = lax.ppermute(east, 'lon', lon_pairs)]
    pallas_call x1, Pallas kernels: 2.98 us -> 5.25 us  [merge(): pl.pallas_call(functools.partial(merge_kernel, len(arrays) > 1), out_shap...]
    all_to_all x1, waiting for transfers between devices: 0.01 us -> 1.9 us  [shards(): folded = exchange(solve(packed[1], points // 2, True))]
    all_to_all x1, starting transfers between devices: 5.84 us -> 4 us  [shards(): folded = exchange(solve(packed[1], points // 2, True))]
  transfers between devices with their start and end apart: 5 -> 5, of which waited for: 1 -> 3; matrix products, arithmetic and copies ran while one was open for 0% -> 0% of each run, Pallas kernels for 39% -> 55%
where the time goes in v4:
time: 83.8 us; the launch traced here: 83.3 us
  Pallas kernels  59.1 us (71%)
  starting transfers between devices  14.4 us (17%)
  waiting for transfers between devices  6.89 us (8%)
  local copies, waits for them, and re-layouts  2.24 us (3%)
    pallas_call x2, Pallas kernels, solve(): pl.pallas_call(functools.partial(solve_kernel, folded), out_shape=jax.Sha...  29.3 us
    pallas_call x2, Pallas kernels, apply(): pl.pallas_call(functools.partial(apply_kernel, first), grid=(lags, count)...  21.4 us
    all_to_all x1, starting transfers between devices, shards(): arrived = exchange(packed[0])  7.08 us
    pallas_call x1, Pallas kernels, merge(): pl.pallas_call(functools.partial(merge_kernel, len(arrays) > 1), out_shap...  5.25 us
    all_to_all x1, starting transfers between devices, shards(): folded = exchange(solve(packed[1], points // 2, True))  4 us
    ppermute x1, waiting for transfers between devices, shards(): east = lax.ppermute(east, 'lon', lon_pairs)  3.15 us
    pallas_call x1, Pallas kernels, pack(): pl.pallas_call(functools.partial(pack_kernel, columns, lon_devices, capac...  3.07 us
    unnamed x10, local copies, waits for them, and re-layouts  2.24 us
  transfers between devices with their start and end apart: 5, of which 3 were waited for; matrix products, arithmetic and copies ran while one was open for 0% of the time, Pallas kernels for 55%

profile of v4, /device:TPU:1, one launch (start us, length us, event | category | flops | bytes accessed | tf_op | source)
XLA Modules:
  0.0 83.3 jit_solution(10552887053087334221)
XLA Ops:
  0.6 3.1 %pack.1 = (bf16[32,72,128]{2,1,0:T(8,128)(2,1)}, bf16[32,72,128]{2,1,0:T(8,128)(2,1)}) custom-call(s32[64]{0:T(128)} %owner.1, s32[64]{0:T(128)} %count.1, bf16[64,64,128]{2,1,0:T(8,128)(2,1)} %pert.1, bf16[64,64]{1,0:T(8,128)(2,1)} %prec.1, bf16[64,64]{1,0:T(8,128)(2,1)} %dep.1), custom_call_target="tpu_custom_call" | custom-call | tf_op jit(solution)/shard_map/pack/pallas_call | solution.py:99
  3.7 7.1 %all-to-all-start = ((bf16[32,72,128]{2,1,0:T(8,128)(2,1)}), bf16[32,72,128]{2,1,0:T(8,128)(2,1)S(1)}, u32[]{:S(2)}, u32[]{:S(2)}) async-start(bf16[32,72,128]{2,1,0:T(8,128)(2,1)} %get-tuple-element.10), calls=%async_computation | async-start | bytes 1179648 | tf_op jit(solution)/shard_map/all_to_all | solution.py:571
  10.8 14.7 %solve_folded.1 = bf16[32,72,128]{2,1,0:T(8,128)(2,1)} custom-call(bf16[32,72,128]{2,1,0:T(8,128)(2,1)} %get-tuple-element.11.arrived), custom_call_target="tpu_custom_call" | custom-call | flops 1920000000 | bytes 1920000 | tf_op jit(solution)/shard_map/solve_folded/pallas_call | solution.py:346
  25.5 1.8 %all-to-all-done.arrived.refs_1_ = bf16[32,72,128]{2,1,0:T(8,128)(2,1)S(1)} async-done(((bf16[32,72,128]{2,1,0:T(8,128)(2,1)}), bf16[32,72,128]{2,1,0:T(8,128)(2,1)S(1)}, u32[]{:S(2)}, u32[]{:S(2)}) %all-to-all-start) | async-done | bytes 589856 | tf_op jit(solution)/shard_map/all_to_all | solution.py:571
  27.3 0.0 copy-start
  27.3 4.0 %all-to-all-start.1 = ((bf16[32,72,128]{2,1,0:T(8,128)(2,1)}), bf16[32,72,128]{2,1,0:T(8,128)(2,1)S(1)}, u32[]{:S(2)}, u32[]{:S(2)}) async-start(bf16[32,72,128]{2,1,0:T(8,128)(2,1)} %solve_folded.1), calls=%async_computation.1 | async-start | bytes 1179648 | tf_op jit(solution)/shard_map/all_to_all | solution.py:573
  31.3 0.0 copy-done
  31.4 14.6 %solve.1.refs_0_ = bf16[32,136,128]{2,1,0:T(8,128)(2,1)} custom-call(bf16[32,72,128]{2,1,0:T(8,128)(2,1)} %copy-done), custom_call_target="tpu_custom_call" | custom-call | flops 1920000000 | bytes 1920000 | tf_op jit(solution)/shard_map/solve/pallas_call | solution.py:346
  46.0 1.9 %all-to-all-done.1.refs_2_ = bf16[32,72,128]{2,1,0:T(8,128)(2,1)S(1)} async-done(((bf16[32,72,128]{2,1,0:T(8,128)(2,1)}), bf16[32,72,128]{2,1,0:T(8,128)(2,1)S(1)}, u32[]{:S(2)}, u32[]{:S(2)}) %all-to-all-start.1) | async-done | bytes 589856 | tf_op jit(solution)/shard_map/all_to_all | solution.py:573
  47.9 0.0 copy-start.1
  47.9 0.8 copy-done.1
  48.7 5.2 %merge.1 = (bf16[64,136,128]{2,1,0:T(8,128)(2,1)}, bf16[8,136,128]{2,1,0:T(8,128)(2,1)}, bf16[8,136,128]{2,1,0:T(8,128)(2,1)}, bf16[1,136,128]{2,1,0:T(8,128)(2,1)}) custom-call(bf16[32,136,128]{2,1,0:T(8,128)(2,1)} %solve.1.refs_0_, bf16[32,72,128]{2,1,0:T(8,128)(2,1)} %copy-done, bf16[32,72,128]{2,1,0:T(8,128)(2,1)} %copy-done.1), custom_call_target="tpu_custom_call" | custom-call | tf_op jit(solution)/shard_map/merge/pallas_call | solution.py:420
  53.9 0.5 collective-permute-start
  54.5 1.3 %collective-permute-start.2 = (bf16[1,136,128]{2,1,0:T(8,128)(2,1)}, bf16[1,136,128]{2,1,0:T(8,128)(2,1)S(1)}, u32[]{:S(2)}, u32[]{:S(2)}) collective-permute-start(bf16[1,136,128]{2,1,0:T(8,128)(2,1)} %get-tuple-element.15), channel_id=1, source_target_pairs={{8,7},{9,0},{10,1},{11,2},{12,3},{13,4},{14,5},{15,6},{16,15},{17,... | collective-permute-start | bytes 104456 | tf_op jit(solution)/shard_map/ppermute | solution.py:585
  55.8 1.5 %collective-permute-start.1 = (bf16[8,136,128]{2,1,0:T(8,128)(2,1)}, bf16[8,136,128]{2,1,0:T(8,128)(2,1)S(1)}, u32[]{:S(2)}, u32[]{:S(2)}) collective-permute-start(bf16[8,136,128]{2,1,0:T(8,128)(2,1)} %get-tuple-element.14), channel_id=1, source_target_pairs={{8,0},{16,8},{24,16},{9,1},{17,9},{25,17},{10,2},{18,10},{26,18},{... | collective-permute-start | bytes 835592 | tf_op jit(solution)/shard_map/ppermute | solution.py:584
  57.3 3.1 %collective-permute-done.refs_1_.refs_2_ = bf16[8,136,128]{2,1,0:T(8,128)(2,1)S(1)} collective-permute-done((bf16[8,136,128]{2,1,0:T(8,128)(2,1)}, bf16[8,136,128]{2,1,0:T(8,128)(2,1)S(1)}, u32[]{:S(2)}, u32[]{:S(2)}) %collective-permute-start) | collective-permute-done | bytes 278560 | tf_op jit(solution)/shard_map/ppermute | solution.py:583
  60.4 0.0 copy-start.2
  60.4 0.7 copy-done.2
  61.1 16.5 %apply.1 = (bf16[1,200,200,128]{3,2,1,0:T(8,128)(2,1)}, f32[1,200,200]{2,1,0:T(8,128)}) custom-call(bf16[64,136,128]{2,1,0:T(8,128)(2,1)} %get-tuple-element.12.refs_0_.refs_1_, bf16[8,136,128]{2,1,0:T(8,128)(2,1)} %copy-done.2, bf16[1,200,200,128]{3,2,1,0:T(8,128)(2,1)} %refs_5_.1, f32[1,200,200]{2,1,0:T(8,128)} %refs_6_.1), custom_call_target="tpu_custom_call" | custom-call | flops 4587520000 | bytes 17920000 | tf_op jit(solution)/shard_map/apply/pallas_call | solution.py:532
  77.7 0.0 collective-permute-done.2.refs_4_
  77.7 0.0 copy-start.4
  77.7 0.0 collective-permute-done.1.refs_3_
  77.7 0.0 copy-start.3
  77.7 0.6 copy-done.4
  78.3 0.1 copy-done.3
  78.4 4.9 %apply_last.1 = (bf16[1,200,200,128]{3,2,1,0:T(8,128)(2,1)}, f32[1,200,200]{2,1,0:T(8,128)}) custom-call(s32[1]{0:T(128)} %bitcast.refs_0_, bf16[64,136,128]{2,1,0:T(8,128)(2,1)} %get-tuple-element.12.refs_0_.refs_1_, bf16[8,136,128]{2,1,0:T(8,128)(2,1)} %copy-done.2, bf16[8,136,128]{2,1,0:T(8,128)(2,1)} %copy-done.3, ...), custom_call_target="tpu_custom_call", output_to_operand_aliasing={{0}: (7, {}), {1}: (8, {})} | custom-call | flops 655360000 | bytes 2560000 | tf_op jit(solution)/shard_map/apply_last/pallas_call | solution.py:532
Async XLA Ops:
  3.7 23.6 %all-to-all-start = ((bf16[32,72,128]{2,1,0:T(8,128)(2,1)}), bf16[32,72,128]{2,1,0:T(8,128)(2,1)S(1)}, u32[]{:S(2)}, u32[]{:S(2)}) async-start(bf16[32,72,128]{2,1,0:T(8,128)(2,1)} %get-tuple-element.10), calls=%async_computation | async-start | bytes 1179648 | tf_op jit(solution)/shard_map/all_to_all | solution.py:571
  27.3 4.0 %copy-start = (bf16[32,72,128]{2,1,0:T(8,128)(2,1)}, bf16[32,72,128]{2,1,0:T(8,128)(2,1)S(1)}, u32[]{:S(2)}) copy-start(bf16[32,72,128]{2,1,0:T(8,128)(2,1)S(1)} %all-to-all-done.arrived.refs_1_) | copy-start | bytes 1769476
  27.3 20.5 %all-to-all-start.1 = ((bf16[32,72,128]{2,1,0:T(8,128)(2,1)}), bf16[32,72,128]{2,1,0:T(8,128)(2,1)S(1)}, u32[]{:S(2)}, u32[]{:S(2)}) async-start(bf16[32,72,128]{2,1,0:T(8,128)(2,1)} %solve_folded.1), calls=%async_computation.1 | async-start | bytes 1179648 | tf_op jit(solution)/shard_map/all_to_all | solution.py:573
  47.9 0.8 copy-start.1
  53.9 6.5 %collective-permute-start = (bf16[8,136,128]{2,1,0:T(8,128)(2,1)}, bf16[8,136,128]{2,1,0:T(8,128)(2,1)S(1)}, u32[]{:S(2)}, u32[]{:S(2)}) collective-permute-start(bf16[8,136,128]{2,1,0:T(8,128)(2,1)} %get-tuple-element.13), channel_id=1, source_target_pairs={{0,7},{1,0},{2,1},{3,2},{4,3},{5,4},{6,5},{7,6},{8,15},{9,8},{10,9... | collective-permute-start | bytes 835592 | tf_op jit(solution)/shard_map/ppermute | solution.py:583
  54.5 23.2 %collective-permute-start.2 = (bf16[1,136,128]{2,1,0:T(8,128)(2,1)}, bf16[1,136,128]{2,1,0:T(8,128)(2,1)S(1)}, u32[]{:S(2)}, u32[]{:S(2)}) collective-permute-start(bf16[1,136,128]{2,1,0:T(8,128)(2,1)} %get-tuple-element.15), channel_id=1, source_target_pairs={{8,7},{9,0},{10,1},{11,2},{12,3},{13,4},{14,5},{15,6},{16,15},{17,... | collective-permute-start | bytes 104456 | tf_op jit(solution)/shard_map/ppermute | solution.py:585
  55.8 21.9 %collective-permute-start.1 = (bf16[8,136,128]{2,1,0:T(8,128)(2,1)}, bf16[8,136,128]{2,1,0:T(8,128)(2,1)S(1)}, u32[]{:S(2)}, u32[]{:S(2)}) collective-permute-start(bf16[8,136,128]{2,1,0:T(8,128)(2,1)} %get-tuple-element.14), channel_id=1, source_target_pairs={{8,0},{16,8},{24,16},{9,1},{17,9},{25,17},{10,2},{18,10},{26,18},{... | collective-permute-start | bytes 835592 | tf_op jit(solution)/shard_map/ppermute | solution.py:584
  60.4 0.7 copy-start.2
  77.7 0.6 copy-start.4
  77.7 0.7 copy-start.3

commit v5 on v4

--- a/solution.py
+++ b/solution.py
@@ -213,7 +213,7 @@
         factors[size // per + group] = jnp.concatenate(lower[part][::-1], axis=0).T
 
 
-def solve_kernel(folded, arrived, out, systems2d, rights, factors, slabs):
+def solve_kernel(arrived, out, systems2d, rights, factors, slabs):
     points = out.shape[0]
     members = out.shape[2]
     locn = arrived.shape[1] - META
@@ -308,10 +308,6 @@
         mean = jnp.sum(inverse * forward, axis=0, keepdims=True)
         scaled = (math.sqrt(members - 1.0) * inverse).astype(BF16)
         line = jnp.broadcast_to(mean, (META, members))
-        if not folded:
-            out[point, 0:members, :] = scaled
-            out[point, members:, :] = line.astype(BF16)
-            return
         upper = scaled[:half]
         turned = jnp.concatenate([upper, upper], axis=0).T.astype(F32)[:half]
         ready = jnp.where(spare, turned, scaled[half:].astype(F32))
@@ -319,9 +315,7 @@
         label = arrived[point, locn:, :].astype(F32)
         out[point, 0:half, :] = ready.astype(BF16)
         out[point, half:, :] = jnp.where(
-            lane8 < 0,
-            0.0,
-            jnp.where(row8 == 0, line, jnp.where(row8 == 1, diagonal, label)),
+            row8 == 0, line, jnp.where(row8 == 1, diagonal, label)
         ).astype(BF16)
 
     half = members // 2
@@ -339,12 +333,12 @@
     lax.fori_loop(0, points // 8, finish_many, 0)
 
 
-def solve(arrived, points, folded):
+def solve(arrived, points):
     slots, rows, members = arrived.shape
-    height = (members // 2 if folded else members) + META
+    height = members // 2 + META
     vmem = pl.BlockSpec(memory_space=pltpu.VMEM)
     return pl.pallas_call(
-        functools.partial(solve_kernel, folded),
+        solve_kernel,
         out_shape=jax.ShapeDtypeStruct((points, height, members), BF16),
         in_specs=[vmem],
         out_specs=vmem,
@@ -357,55 +351,25 @@
         cost_estimate=pl.CostEstimate(
             flops=points * 60_000_000, bytes_accessed=points * 60_000, transcendentals=0
         ),
-        name="solve_folded" if folded else "solve",
+        name="solve",
     )(arrived)
 
 
-def merge_kernel(kept, *refs):
-    if kept:
-        solved, origin, folded, own, east, north, corner = refs
-    else:
-        solved, own, east, north, corner = refs
-    members = own.shape[2]
-    half = members // 2
-    row = lax.broadcasted_iota(jnp.int32, (half, members), 0)
-    lane = lax.broadcasted_iota(jnp.int32, (half, members), 1)
-    below = lane - half <= row
-
-    def unfolded(step, carry):
-        for part in range(4):
-            slot = step * 4 + part
-            meta = folded[slot, half:, :]
-            label = label_of(meta)
-            lines = folded[slot, 0:half, :].astype(F32)
-            spare = jnp.where(below, 0.0, lines).astype(BF16)
-            turned = jnp.concatenate([spare, spare], axis=0).T.astype(F32)[half:]
-            upper = jnp.where(
-                lane == row,
-                jnp.broadcast_to(meta.astype(F32)[1:2], (half, members)),
-                jnp.where(lane < half, turned, 0.0),
-            )
-            own[label, 0:half, :] = upper.astype(BF16)
-            own[label, half:members, :] = jnp.where(below, lines, 0.0).astype(BF16)
-            own[label, members:, :] = meta
-        return carry
-
-    def direct(step, carry):
-        for part in range(4):
-            slot = step * 4 + part
-            label = label_of(origin[slot, origin.shape[1] - META :, :])
-            own[label] = solved[slot]
-        return carry
-
-    if kept:
-        lax.fori_loop(0, solved.shape[0] // 4, direct, 0)
-        lax.fori_loop(0, folded.shape[0] // 4, unfolded, 0)
-    else:
-
-        @pl.loop(0, own.shape[0])
-        def _(label):
-            own[label] = solved[label]
-
+def merge_kernel(*refs):
+    solved, (own, east, north, corner) = refs[:-4], refs[-4:]
+    many = 8
+    half = own.shape[1] - META
+
+    for array in solved:
+
+        def several(step, carry):
+            for part in range(many):
+                slot = step * many + part
+                place = slot if len(solved) == 1 else label_of(array[slot, half:, :])
+                own[place] = array[slot]
+            return carry
+
+        lax.fori_loop(0, array.shape[0] // many, several, 0)
     for index in range(TILES_LON):
         north[index] = own[index]
     for index in range(TILES_LAT):
@@ -414,11 +378,10 @@
 
 
 def merge(*arrays):
-    members = arrays[0].shape[2]
-    shape = lambda count: jax.ShapeDtypeStruct((count, members + META, members), BF16)
+    shape = lambda count: jax.ShapeDtypeStruct((count,) + arrays[0].shape[1:], BF16)
     vmem = pl.BlockSpec(memory_space=pltpu.VMEM)
     return pl.pallas_call(
-        functools.partial(merge_kernel, len(arrays) > 1),
+        merge_kernel,
         out_shape=(shape(TILES_LAT * TILES_LON), shape(TILES_LAT), shape(TILES_LON), shape(1)),
         in_specs=[vmem] * len(arrays),
         out_specs=(vmem,) * 4,
@@ -426,45 +389,64 @@
     )(*arrays)
 
 
+def unfolded(folded):
+    members = folded.shape[1]
+    half = members // 2
+    row = lax.broadcasted_iota(jnp.int32, (half, members), 0)
+    lane = lax.broadcasted_iota(jnp.int32, (half, members), 1)
+    below = lane - half <= row
+    lines = folded[:half].astype(F32)
+    meta = folded[half:].astype(F32)
+    spare = jnp.where(below, 0.0, lines).astype(BF16)
+    turned = jnp.concatenate([spare, spare], axis=0).T.astype(F32)[half:]
+    upper = jnp.where(
+        lane == row,
+        jnp.broadcast_to(meta[1:2], (half, members)),
+        jnp.where(lane < half, turned, 0.0),
+    )
+    lower = jnp.where(below, lines, 0.0)
+    return jnp.concatenate([upper, lower], axis=0), meta[0:1]
+
+
 def apply_kernel(first, *refs):
     last = first == TILES_LAT - 1
     if last:
         top, own, east, north, corner, anomalies, flux, _, before, *refs = refs
     else:
-        own, east, anomalies, flux, *refs = refs
+        own, east, north, corner, anomalies, flux, *refs = refs
     out, mean, weights, means = refs
     members = anomalies.shape[3]
     cols = anomalies.shape[2]
-    tile_row = pl.program_id(1) + first
+    step = pl.program_id(1)
+    tile_row = step + first
+    now = lax.rem(step, 2)
+    later = 1 - now
+    half = (FINE + 1) // 2
     if last:
         mean[...] = before[...]
 
-    def inner(row, col):
-        return own[row * TILES_LON + col] if col < TILES_LON else east[row]
-
-    def here(col):
-        return inner(tile_row, col)
-
-    def above(col):
-        if not last:
-            return inner(tile_row + 1, col)
-        outer = north[col] if col < TILES_LON else corner[0]
-        return jnp.where(top[0] == 1, inner(TILES_LAT - 1, col), outer)
-
-    half = (FINE + 1) // 2
+    def put(place, col, folded):
+        factor, line = unfolded(folded)
+        weights[place, col * members : (col + 1) * members, 0:members] = factor.astype(BF16)
+        means[place, col : col + 1, :] = line
+        return factor
+
+    @pl.when(step == 0)
+    def _():
+        for col in range(TILES_LON + 1):
+            put(now, col, own[col] if col < TILES_LON else east[0])
 
     for col in range(TILES_LON + 1):
-        low = here(col)
-        high = above(col)
-        change = high[:members].astype(F32) - low[:members].astype(F32)
-        change = (change * (1.0 / FINE)).astype(BF16)
+        ahead = north[col] if col < TILES_LON else corner[0]
+        if last:
+            inner = own[col] if col < TILES_LON else east[0]
+            ahead = jnp.where(top[0] == 1, inner, ahead)
+        high = put(later, col, ahead)
         place = slice(col * members, (col + 1) * members)
-        weights[0, place, 0:members] = low[:members]
+        low = weights[now, place, 0:members].astype(F32)
+        change = ((high - low) * (1.0 / FINE)).astype(BF16)
         weights[0, place, members:] = change
-        weights[1, place, 0:members] = high[:members]
         weights[1, place, members:] = change
-        means[col : col + 1, :] = low[members:].astype(F32)[0:1]
-        means[16 + col : 17 + col, :] = high[members:].astype(F32)[0:1]
 
     width = 32
     offset = lax.broadcasted_iota(jnp.int32, (width, members), 0)
@@ -480,7 +462,7 @@
             scaled = field * number
             left = jnp.concatenate([field, scaled], axis=2).reshape(count * width, 2 * members)
             place = slice(col * members, (col + 2) * members)
-            both = dot(left, weights[part, place, :], NT).reshape(count, width, 2 * members)
+            both = dot(left, weights[later if part else now, place, :], NT).reshape(count, width, 2 * members)
             cell = offset - col
             inside = (cell >= 0) & (cell < FINE)
             right_weight = jnp.where(inside, cell.astype(F32) / FINE, 0.0)
@@ -504,7 +486,7 @@
     )
     keep = lax.broadcasted_iota(jnp.int32, (16, members), 0) <= TILES_LON
     left = jnp.concatenate(
-        [jnp.where(keep, means[0:16, :], 0.0), jnp.where(keep, means[16:32, :], 0.0)], axis=0
+        [jnp.where(keep, means[now], 0.0), jnp.where(keep, means[later], 0.0)], axis=0
     ).astype(BF16)
     for line in range(FINE):
         product = dot(left, anomalies[0, line], NT)
@@ -515,19 +497,26 @@
         mean[0, place, :] = flux[0, place, :] + shift
 
 
-def apply(first, count, operands, anomalies, flux, earlier=()):
+def apply(first, count, top, own, east, north, corner, anomalies, flux, earlier=()):
     lags, rows, cols, members = anomalies.shape
-    whole = lambda array: pl.BlockSpec(array.shape, lambda l, r: (0,) * array.ndim)
+    height = own.shape[1]
+    line = lambda at: pl.BlockSpec((TILES_LON, height, members), lambda l, r: (at(r), 0, 0))
+    one = lambda at: pl.BlockSpec((1, height, members), lambda l, r: (at(r), 0, 0))
     strip = pl.BlockSpec((1, FINE, cols, members), lambda l, r: (l, r + first, 0, 0))
     plane = pl.BlockSpec((1, rows, cols), lambda l, r: (l, 0, 0))
-    specs = [
-        pl.BlockSpec(memory_space=pltpu.SMEM) if array.ndim == 1 else whole(array)
-        for array in operands
-    ] + [strip, plane]
+    specs = [line(lambda r: r + first), one(lambda r: r + first)]
+    operands = [own, east]
     aliases = {}
     if earlier:
+        specs = [pl.BlockSpec(memory_space=pltpu.SMEM)] + specs
+        specs += [line(lambda r: 0), one(lambda r: 0), strip, plane]
+        operands = [top, own, east, north, corner, anomalies, flux]
         aliases = {len(specs): 0, len(specs) + 1: 1}
         specs += [pl.BlockSpec(memory_space=pl.ANY), plane]
+        operands += earlier
+    else:
+        specs += [line(lambda r: r + first + 1), one(lambda r: r + first + 1), strip, plane]
+        operands = [own, east, own, east, anomalies, flux]
     cells = count * FINE * cols * lags
     return pl.pallas_call(
         functools.partial(apply_kernel, first),
@@ -540,7 +529,7 @@
         out_specs=(strip, plane),
         scratch_shapes=[
             pltpu.VMEM((2, (TILES_LON + 1) * members, 2 * members), BF16),
-            pltpu.VMEM((32, members), F32),
+            pltpu.VMEM((2, 16, members), F32),
         ],
         input_output_aliases=aliases,
         cost_estimate=pl.CostEstimate(
@@ -549,7 +538,7 @@
             transcendentals=0,
         ),
         name="apply_last" if earlier else "apply",
-    )(*operands, anomalies, flux, *earlier)
+    )(*operands)
 
 
 def shards(obs_pert, obs_dep, obs_prec, obs_count, owner_point, anomalies, flux_mean):
@@ -570,11 +559,10 @@
     )
     arrived = exchange(packed[0])
     if halved:
-        folded = exchange(solve(packed[1], points // 2, True))
-        solved = solve(arrived, points // 2, False)
-        own, east, north, corner = merge(solved, arrived, folded)
+        folded = exchange(solve(packed[1], points // 2))
+        own, east, north, corner = merge(solve(arrived, points // 2), folded)
     else:
-        own, east, north, corner = merge(solve(arrived, points, False))
+        own, east, north, corner = merge(solve(arrived, points))
     lat_pairs = [(i, i - 1) for i in range(1, lat_devices)]
     lon_pairs = [(i, (i - 1) % lon_devices) for i in range(lon_devices)]
     both_pairs = [
@@ -584,10 +572,9 @@
     north = lax.ppermute(north, "lat", lat_pairs)
     corner = lax.ppermute(corner, ("lat", "lon"), both_pairs)
     top = (lax.axis_index("lat") == lat_devices - 1).astype(jnp.int32).reshape(1)
-    inside = apply(0, TILES_LAT - 1, (own, east), anomalies, flux_mean)
-    return apply(
-        TILES_LAT - 1, 1, (top, own, east, north, corner), anomalies, flux_mean, inside
-    )
+    fields = (top, own, east, north, corner, anomalies, flux_mean)
+    inside = apply(0, TILES_LAT - 1, *fields)
+    return apply(TILES_LAT - 1, 1, *fields, inside)
 
 
 def solution(mesh):

time: 83.8 us -> 81.6 us (0.974)
  waiting for transfers between devices: 6.89 us -> 5.09 us
  Pallas kernels: 59.1 us -> 58 us
    pallas_call x3, Pallas kernels: 34.6 us -> 32.9 us  [the longest x2 29.4 us: solve(): pl.pallas_call(solve_kernel, out_shape=jax.ShapeDtypeStruct((points, heig...]
    ppermute x1, waiting for transfers between devices: 3.15 us -> 1.45 us  [shards(): east = lax.ppermute(east, 'lon', lon_pairs)]
  transfers between devices with their start and end apart: 5 -> 5, of which waited for: 3 -> 3; matrix products, arithmetic and copies ran while one was open for 0% -> 0% of each run, Pallas kernels for 55% -> 59%
where the time goes in v5:
time: 81.6 us; the launch traced here: 80.3 us
  Pallas kernels  58 us (71%)
  starting transfers between devices  14.4 us (18%)
  waiting for transfers between devices  5.09 us (6%)
  local copies, waits for them, and re-layouts  2.12 us (3%)
    pallas_call x2, Pallas kernels, solve(): pl.pallas_call(solve_kernel, out_shape=jax.ShapeDtypeStruct((points, heig...  29.4 us
    pallas_call x2, Pallas kernels, apply(): pl.pallas_call(functools.partial(apply_kernel, first), grid=(lags, count)...  22.1 us
    all_to_all x1, starting transfers between devices, shards(): arrived = exchange(packed[0])  7.08 us
    all_to_all x1, starting transfers between devices, shards(): folded = exchange(solve(packed[1], points // 2))  4 us
    pallas_call x1, Pallas kernels, merge(): pl.pallas_call(merge_kernel, out_shape=(shape(TILES_LAT * TILES_LON), sha...  3.45 us
    pallas_call x1, Pallas kernels, pack(): pl.pallas_call(functools.partial(pack_kernel, columns, lon_devices, capac...  3.07 us
    unnamed x10, local copies, waits for them, and re-layouts  2.12 us
    all_to_all x1, waiting for transfers between devices, shards(): arrived = exchange(packed[0])  1.83 us
  transfers between devices with their start and end apart: 5, of which 3 were waited for; matrix products, arithmetic and copies ran while one was open for 0% of the time, Pallas kernels for 59%

profile of v5, /device:TPU:1, one launch (start us, length us, event | category | flops | bytes accessed | tf_op | source)
XLA Modules:
  0.0 80.3 jit_solution(3541428401466955761)
XLA Ops:
  0.6 3.1 %pack.1 = (bf16[32,72,128]{2,1,0:T(8,128)(2,1)}, bf16[32,72,128]{2,1,0:T(8,128)(2,1)}) custom-call(s32[64]{0:T(128)} %owner.1, s32[64]{0:T(128)} %count.1, bf16[64,64,128]{2,1,0:T(8,128)(2,1)} %pert.1, bf16[64,64]{1,0:T(8,128)(2,1)} %prec.1, bf16[64,64]{1,0:T(8,128)(2,1)} %dep.1), custom_call_target="tpu_custom_call" | custom-call | tf_op jit(solution)/shard_map/pack/pallas_call | solution.py:99
  3.7 7.1 %all-to-all-start = ((bf16[32,72,128]{2,1,0:T(8,128)(2,1)}), bf16[32,72,128]{2,1,0:T(8,128)(2,1)S(1)}, u32[]{:S(2)}, u32[]{:S(2)}) async-start(bf16[32,72,128]{2,1,0:T(8,128)(2,1)} %get-tuple-element.10), calls=%async_computation | async-start | bytes 1179648 | tf_op jit(solution)/shard_map/all_to_all | solution.py:560
  10.8 14.7 %solve.3 = bf16[32,72,128]{2,1,0:T(8,128)(2,1)} custom-call(bf16[32,72,128]{2,1,0:T(8,128)(2,1)} %get-tuple-element.11.arrived), custom_call_target="tpu_custom_call" | custom-call | flops 1920000000 | bytes 1920000 | tf_op jit(solution)/shard_map/solve/pallas_call | solution.py:340
  25.5 1.8 %all-to-all-done.arrived = bf16[32,72,128]{2,1,0:T(8,128)(2,1)S(1)} async-done(((bf16[32,72,128]{2,1,0:T(8,128)(2,1)}), bf16[32,72,128]{2,1,0:T(8,128)(2,1)S(1)}, u32[]{:S(2)}, u32[]{:S(2)}) %all-to-all-start) | async-done | bytes 589856 | tf_op jit(solution)/shard_map/all_to_all | solution.py:560
  27.3 0.0 copy-start.1
  27.3 4.0 %all-to-all-start.1 = ((bf16[32,72,128]{2,1,0:T(8,128)(2,1)}), bf16[32,72,128]{2,1,0:T(8,128)(2,1)S(1)}, u32[]{:S(2)}, u32[]{:S(2)}) async-start(bf16[32,72,128]{2,1,0:T(8,128)(2,1)} %solve.3), calls=%async_computation.1 | async-start | bytes 1179648 | tf_op jit(solution)/shard_map/all_to_all | solution.py:562
  31.3 0.0 copy-done.1
  31.4 14.7 %solve.2.refs_0_ = bf16[32,72,128]{2,1,0:T(8,128)(2,1)} custom-call(bf16[32,72,128]{2,1,0:T(8,128)(2,1)} %copy-done.1), custom_call_target="tpu_custom_call" | custom-call | flops 1920000000 | bytes 1920000 | tf_op jit(solution)/shard_map/solve/pallas_call | solution.py:340
  46.1 1.8 %all-to-all-done.1.refs_1_ = bf16[32,72,128]{2,1,0:T(8,128)(2,1)S(1)} async-done(((bf16[32,72,128]{2,1,0:T(8,128)(2,1)}), bf16[32,72,128]{2,1,0:T(8,128)(2,1)S(1)}, u32[]{:S(2)}, u32[]{:S(2)}) %all-to-all-start.1) | async-done | bytes 589856 | tf_op jit(solution)/shard_map/all_to_all | solution.py:562
  47.9 0.0 copy-start
  47.9 0.8 %copy-done = bf16[32,72,128]{2,1,0:T(8,128)(2,1)} copy-done((bf16[32,72,128]{2,1,0:T(8,128)(2,1)}, bf16[32,72,128]{2,1,0:T(8,128)(2,1)S(1)}, u32[]{:S(2)}) %copy-start) | copy-done | bytes 589848
  48.7 3.5 %merge.1 = (bf16[64,72,128]{2,1,0:T(8,128)(2,1)}, bf16[8,72,128]{2,1,0:T(8,128)(2,1)}, bf16[8,72,128]{2,1,0:T(8,128)(2,1)}, bf16[1,72,128]{2,1,0:T(8,128)(2,1)}) custom-call(bf16[32,72,128]{2,1,0:T(8,128)(2,1)} %solve.2.refs_0_, bf16[32,72,128]{2,1,0:T(8,128)(2,1)} %copy-done), custom_call_target="tpu_custom_call" | custom-call | tf_op jit(solution)/shard_map/merge/pallas_call | solution.py:383
  52.1 0.5 collective-permute-start
  52.7 1.3 %collective-permute-start.2 = (bf16[1,72,128]{2,1,0:T(8,128)(2,1)}, bf16[1,72,128]{2,1,0:T(8,128)(2,1)S(1)}, u32[]{:S(2)}, u32[]{:S(2)}) collective-permute-start(bf16[1,72,128]{2,1,0:T(8,128)(2,1)} %get-tuple-element.15), channel_id=1, source_target_pairs={{8,7},{9,0},{10,1},{11,2},{12,3},{13,4},{14,5},{15,6},{16,15},{17,... | collective-permute-start | bytes 55304 | tf_op jit(solution)/shard_map/ppermute | solution.py:573
  54.0 1.5 %collective-permute-start.1 = (bf16[8,72,128]{2,1,0:T(8,128)(2,1)}, bf16[8,72,128]{2,1,0:T(8,128)(2,1)S(1)}, u32[]{:S(2)}, u32[]{:S(2)}) collective-permute-start(bf16[8,72,128]{2,1,0:T(8,128)(2,1)} %get-tuple-element.14), channel_id=1, source_target_pairs={{8,0},{16,8},{24,16},{9,1},{17,9},{25,17},{10,2},{18,10},{26,18},{... | collective-permute-start | bytes 442376 | tf_op jit(solution)/shard_map/ppermute | solution.py:572
  55.5 1.4 %collective-permute-done.refs_1_.refs_3_.refs_2_ = bf16[8,72,128]{2,1,0:T(8,128)(2,1)S(1)} collective-permute-done((bf16[8,72,128]{2,1,0:T(8,128)(2,1)}, bf16[8,72,128]{2,1,0:T(8,128)(2,1)S(1)}, u32[]{:S(2)}, u32[]{:S(2)}) %collective-permute-start) | collective-permute-done | bytes 147488 | tf_op jit(solution)/shard_map/ppermute | solution.py:571
  56.9 0.0 copy-start.2
  56.9 0.7 copy-done.2
  57.6 17.8 %apply.1 = (bf16[1,200,200,128]{3,2,1,0:T(8,128)(2,1)}, f32[1,200,200]{2,1,0:T(8,128)}) custom-call(bf16[64,72,128]{2,1,0:T(8,128)(2,1)} %get-tuple-element.12.refs_0_.refs_2_.refs_1_, bf16[8,72,128]{2,1,0:T(8,128)(2,1)} %copy-done.2, bf16[64,72,128]{2,1,0:T(8,128)(2,1)} %get-tuple-element.12.refs_0_.refs_2_.refs_1_, bf16[8,72,128]{2,1,0:T(8,128)(2,1)} %copy-done.2, ...), custom_call_target="tpu_custom_call" | custom-call | flops 4587520000 | bytes 17920000 | tf_op jit(solution)/shard_map/apply/pallas_call | solution.py:521
  75.4 0.0 collective-permute-done.2.refs_4_
  75.4 0.0 copy-start.4
  75.4 0.0 collective-permute-done.1.refs_3_
  75.4 0.0 copy-start.3
  75.4 0.6 copy-done.4
  76.0 0.1 copy-done.3
  76.1 4.3 %apply_last.1 = (bf16[1,200,200,128]{3,2,1,0:T(8,128)(2,1)}, f32[1,200,200]{2,1,0:T(8,128)}) custom-call(s32[1]{0:T(128)} %bitcast.refs_0_, bf16[64,72,128]{2,1,0:T(8,128)(2,1)} %get-tuple-element.12.refs_0_.refs_2_.refs_1_, bf16[8,72,128]{2,1,0:T(8,128)(2,1)} %copy-done.2, ...), custom_call_target="tpu_custom_call", output_to_operand_aliasing={{0}: (7, {}), {1}: (8, {})} | custom-call | flops 655360000 | bytes 2560000 | tf_op jit(solution)/shard_map/apply_last/pallas_call | solution.py:521
Async XLA Ops:
  3.7 23.6 %all-to-all-start = ((bf16[32,72,128]{2,1,0:T(8,128)(2,1)}), bf16[32,72,128]{2,1,0:T(8,128)(2,1)S(1)}, u32[]{:S(2)}, u32[]{:S(2)}) async-start(bf16[32,72,128]{2,1,0:T(8,128)(2,1)} %get-tuple-element.10), calls=%async_computation | async-start | bytes 1179648 | tf_op jit(solution)/shard_map/all_to_all | solution.py:560
  27.3 4.0 %copy-start.1 = (bf16[32,72,128]{2,1,0:T(8,128)(2,1)}, bf16[32,72,128]{2,1,0:T(8,128)(2,1)S(1)}, u32[]{:S(2)}) copy-start(bf16[32,72,128]{2,1,0:T(8,128)(2,1)S(1)} %all-to-all-done.arrived) | copy-start | bytes 1769476
  27.3 20.5 %all-to-all-start.1 = ((bf16[32,72,128]{2,1,0:T(8,128)(2,1)}), bf16[32,72,128]{2,1,0:T(8,128)(2,1)S(1)}, u32[]{:S(2)}, u32[]{:S(2)}) async-start(bf16[32,72,128]{2,1,0:T(8,128)(2,1)} %solve.3), calls=%async_computation.1 | async-start | bytes 1179648 | tf_op jit(solution)/shard_map/all_to_all | solution.py:562
  47.9 0.8 %copy-start = (bf16[32,72,128]{2,1,0:T(8,128)(2,1)}, bf16[32,72,128]{2,1,0:T(8,128)(2,1)S(1)}, u32[]{:S(2)}) copy-start(bf16[32,72,128]{2,1,0:T(8,128)(2,1)S(1)} %all-to-all-done.1.refs_1_) | copy-start | bytes 1769476
  52.1 4.8 %collective-permute-start = (bf16[8,72,128]{2,1,0:T(8,128)(2,1)}, bf16[8,72,128]{2,1,0:T(8,128)(2,1)S(1)}, u32[]{:S(2)}, u32[]{:S(2)}) collective-permute-start(bf16[8,72,128]{2,1,0:T(8,128)(2,1)} %get-tuple-element.13), channel_id=1, source_target_pairs={{0,7},{1,0},{2,1},{3,2},{4,3},{5,4},{6,5},{7,6},{8,15},{9,8},{10,9... | collective-permute-start | bytes 442376 | tf_op jit(solution)/shard_map/ppermute | solution.py:571
  52.7 22.7 %collective-permute-start.2 = (bf16[1,72,128]{2,1,0:T(8,128)(2,1)}, bf16[1,72,128]{2,1,0:T(8,128)(2,1)S(1)}, u32[]{:S(2)}, u32[]{:S(2)}) collective-permute-start(bf16[1,72,128]{2,1,0:T(8,128)(2,1)} %get-tuple-element.15), channel_id=1, source_target_pairs={{8,7},{9,0},{10,1},{11,2},{12,3},{13,4},{14,5},{15,6},{16,15},{17,... | collective-permute-start | bytes 55304 | tf_op jit(solution)/shard_map/ppermute | solution.py:573
  54.0 21.4 %collective-permute-start.1 = (bf16[8,72,128]{2,1,0:T(8,128)(2,1)}, bf16[8,72,128]{2,1,0:T(8,128)(2,1)S(1)}, u32[]{:S(2)}, u32[]{:S(2)}) collective-permute-start(bf16[8,72,128]{2,1,0:T(8,128)(2,1)} %get-tuple-element.14), channel_id=1, source_target_pairs={{8,0},{16,8},{24,16},{9,1},{17,9},{25,17},{10,2},{18,10},{26,18},{... | collective-permute-start | bytes 442376 | tf_op jit(solution)/shard_map/ppermute | solution.py:572
  56.9 0.7 copy-start.2
  75.4 0.6 copy-start.4
  75.4 0.7 copy-start.3

commit v6 on v5

--- a/solution.py
+++ b/solution.py
@@ -405,43 +405,76 @@
         jnp.where(lane < half, turned, 0.0),
     )
     lower = jnp.where(below, lines, 0.0)
-    return jnp.concatenate([upper, lower], axis=0), meta[0:1]
-
-
-def apply_kernel(first, *refs):
-    last = first == TILES_LAT - 1
-    if last:
-        top, own, east, north, corner, anomalies, flux, _, before, *refs = refs
-    else:
-        own, east, north, corner, anomalies, flux, *refs = refs
-    out, mean, weights, means = refs
+    return jnp.concatenate([upper, lower], axis=0)
+
+
+def apply_kernel(
+    top, own, east, next_own, next_east, north, corner, anomalies, flux, out, mean, weights
+):
     members = anomalies.shape[3]
     cols = anomalies.shape[2]
     step = pl.program_id(1)
-    tile_row = step + first
+    tile_row = step
     now = lax.rem(step, 2)
     later = 1 - now
+    from_north = (step == TILES_LAT - 1) & (top[0] == 0)
     half = (FINE + 1) // 2
-    if last:
-        mean[...] = before[...]
+    def here(col):
+        return own[col] if col < TILES_LON else east[0]
+
+    def above(col):
+        inner = next_own[col] if col < TILES_LON else next_east[0]
+        outer = north[col] if col < TILES_LON else corner[0]
+        return jnp.where(from_north, outer, inner)
+
+    def means_of(blocks):
+        lines = [block[members // 2 :].astype(F32)[0:1] for block in blocks]
+        return jnp.concatenate(lines + [jnp.zeros((16 - len(lines), members), F32)], axis=0)
+
+    columns = range(TILES_LON + 1)
+    left = jnp.concatenate(
+        [means_of([here(col) for col in columns]), means_of([above(col) for col in columns])],
+        axis=0,
+    ).astype(BF16)
 
     def put(place, col, folded):
-        factor, line = unfolded(folded)
+        factor = unfolded(folded)
         weights[place, col * members : (col + 1) * members, 0:members] = factor.astype(BF16)
-        means[place, col : col + 1, :] = line
         return factor
 
     @pl.when(step == 0)
     def _():
-        for col in range(TILES_LON + 1):
-            put(now, col, own[col] if col < TILES_LON else east[0])
-
-    for col in range(TILES_LON + 1):
-        ahead = north[col] if col < TILES_LON else corner[0]
-        if last:
-            inner = own[col] if col < TILES_LON else east[0]
-            ahead = jnp.where(top[0] == 1, inner, ahead)
-        high = put(later, col, ahead)
+        for col in columns:
+            put(now, col, here(col))
+
+    corner_index = lax.broadcasted_iota(jnp.int32, (16, cols), 0)
+    cell = lax.broadcasted_iota(jnp.int32, (16, cols), 1)
+    tile = cell // FINE
+    part = (cell - tile * FINE).astype(F32) / FINE
+    hat = jnp.where(
+        tile == corner_index, 1.0 - part, jnp.where(tile + 1 == corner_index, part, 0.0)
+    )
+    empty = jnp.zeros_like(left)
+    double = jnp.concatenate(
+        [jnp.concatenate([left, empty], axis=1), jnp.concatenate([empty, left], axis=1)], axis=0
+    )
+    for begin in range(0, FINE, 2):
+        lines = range(begin, min(begin + 2, FINE))
+        if len(lines) == 2:
+            pair = jnp.concatenate([anomalies[0, line] for line in lines], axis=1)
+            product = dot(double, pair, NT)
+        else:
+            product = dot(left, anomalies[0, begin], NT)
+        for line in lines:
+            at = (line - begin) * left.shape[0]
+            up = line / FINE
+            mixed = (1.0 - up) * product[at : at + 16] + up * product[at + 16 : at + 32]
+            shift = jnp.sum(mixed * hat, axis=0, keepdims=True)
+            place = pl.ds(tile_row * FINE + line, 1)
+            mean[0, place, :] = flux[0, place, :] + shift
+
+    for col in columns:
+        high = put(later, col, above(col))
         place = slice(col * members, (col + 1) * members)
         low = weights[now, place, 0:members].astype(F32)
         change = ((high - low) * (1.0 / FINE)).astype(BF16)
@@ -477,68 +510,41 @@
             ).astype(BF16)
         out[0, start:stop, cols - 8 :, :] = carry.astype(BF16)
 
-    corner_index = lax.broadcasted_iota(jnp.int32, (16, cols), 0)
-    cell = lax.broadcasted_iota(jnp.int32, (16, cols), 1)
-    tile = cell // FINE
-    part = (cell - tile * FINE).astype(F32) / FINE
-    hat = jnp.where(
-        tile == corner_index, 1.0 - part, jnp.where(tile + 1 == corner_index, part, 0.0)
-    )
-    keep = lax.broadcasted_iota(jnp.int32, (16, members), 0) <= TILES_LON
-    left = jnp.concatenate(
-        [jnp.where(keep, means[now], 0.0), jnp.where(keep, means[later], 0.0)], axis=0
-    ).astype(BF16)
-    for line in range(FINE):
-        product = dot(left, anomalies[0, line], NT)
-        up = line / FINE
-        mixed = (1.0 - up) * product[0:16] + up * product[16:32]
-        shift = jnp.sum(mixed * hat, axis=0, keepdims=True)
-        place = pl.ds(tile_row * FINE + line, 1)
-        mean[0, place, :] = flux[0, place, :] + shift
-
-
-def apply(first, count, top, own, east, north, corner, anomalies, flux, earlier=()):
+
+def apply(top, own, east, north, corner, anomalies, flux):
     lags, rows, cols, members = anomalies.shape
     height = own.shape[1]
     line = lambda at: pl.BlockSpec((TILES_LON, height, members), lambda l, r: (at(r), 0, 0))
     one = lambda at: pl.BlockSpec((1, height, members), lambda l, r: (at(r), 0, 0))
-    strip = pl.BlockSpec((1, FINE, cols, members), lambda l, r: (l, r + first, 0, 0))
+    same = lambda r: r
+    above = lambda r: jnp.minimum(r + 1, TILES_LAT - 1)
+    fixed = lambda r: 0
+    strip = pl.BlockSpec((1, FINE, cols, members), lambda l, r: (l, r, 0, 0))
     plane = pl.BlockSpec((1, rows, cols), lambda l, r: (l, 0, 0))
-    specs = [line(lambda r: r + first), one(lambda r: r + first)]
-    operands = [own, east]
-    aliases = {}
-    if earlier:
-        specs = [pl.BlockSpec(memory_space=pltpu.SMEM)] + specs
-        specs += [line(lambda r: 0), one(lambda r: 0), strip, plane]
-        operands = [top, own, east, north, corner, anomalies, flux]
-        aliases = {len(specs): 0, len(specs) + 1: 1}
-        specs += [pl.BlockSpec(memory_space=pl.ANY), plane]
-        operands += earlier
-    else:
-        specs += [line(lambda r: r + first + 1), one(lambda r: r + first + 1), strip, plane]
-        operands = [own, east, own, east, anomalies, flux]
-    cells = count * FINE * cols * lags
     return pl.pallas_call(
-        functools.partial(apply_kernel, first),
-        grid=(lags, count),
+        apply_kernel,
+        grid=(lags, TILES_LAT),
         out_shape=(
             jax.ShapeDtypeStruct(anomalies.shape, BF16),
             jax.ShapeDtypeStruct(flux.shape, F32),
         ),
-        in_specs=specs,
+        in_specs=[
+            pl.BlockSpec(memory_space=pltpu.SMEM),
+            line(same),
+            one(same),
+            line(above),
+            one(above),
+            line(fixed),
+            one(fixed),
+            strip,
+            plane,
+        ],
         out_specs=(strip, plane),
         scratch_shapes=[
             pltpu.VMEM((2, (TILES_LON + 1) * members, 2 * members), BF16),
-            pltpu.VMEM((2, 16, members), F32),
         ],
-        input_output_aliases=aliases,
-        cost_estimate=pl.CostEstimate(
-            flops=cells * members * members * 8,
-            bytes_accessed=cells * members * 4,
-            transcendentals=0,
-        ),
-        name="apply_last" if earlier else "apply",
-    )(*operands)
+        name="apply",
+    )(top, own, east, own, east, north, corner, anomalies, flux)
 
 
 def shards(obs_pert, obs_dep, obs_prec, obs_count, owner_point, anomalies, flux_mean):
@@ -572,9 +578,7 @@
     north = lax.ppermute(north, "lat", lat_pairs)
     corner = lax.ppermute(corner, ("lat", "lon"), both_pairs)
     top = (lax.axis_index("lat") == lat_devices - 1).astype(jnp.int32).reshape(1)
-    fields = (top, own, east, north, corner, anomalies, flux_mean)
-    inside = apply(0, TILES_LAT - 1, *fields)
-    return apply(TILES_LAT - 1, 1, *fields, inside)
+    return apply(top, own, east, north, corner, anomalies, flux_mean)
 
 
 def solution(mesh):

time: 81.6 us -> 79.5 us (0.974)
  Pallas kernels: 58 us -> 52.8 us
  waiting for transfers between devices: 5.09 us -> 9.6 us
    ppermute x1, waiting for transfers between devices: 0.01 us -> 5.94 us  [shards(): corner = lax.ppermute(corner, ('lat', 'lon'), both_pairs)]
    pallas_call x2 -> x1, Pallas kernels: 22.1 us -> 16.9 us  [apply(): pl.pallas_call(apply_kernel, grid=(lags, TILES_LAT), out_shape=(jax.Shape...]
    ppermute x1, waiting for transfers between devices: 1.45 us -> 0.01 us  [shards(): east = lax.ppermute(east, 'lon', lon_pairs)]
  transfers between devices with their start and end apart: 5 -> 5, of which waited for: 3 -> 3; matrix products, arithmetic and copies ran while one was open for 0% -> 0% of each run, Pallas kernels for 59% -> 37%
where the time goes in v6:
time: 79.5 us; the launch traced here: 78.8 us
  Pallas kernels  52.8 us (66%)
  starting transfers between devices  14.2 us (18%)
  waiting for transfers between devices  9.6 us (12%)
  local copies, waits for them, and re-layouts  1.52 us (2%)
    pallas_call x2, Pallas kernels, solve(): pl.pallas_call(solve_kernel, out_shape=jax.ShapeDtypeStruct((points, heig...  29.4 us
    pallas_call x1, Pallas kernels, apply(): pl.pallas_call(apply_kernel, grid=(lags, TILES_LAT), out_shape=(jax.Shape...  16.9 us
    all_to_all x1, starting transfers between devices, shards(): arrived = exchange(packed[0])  7.08 us
    ppermute x1, waiting for transfers between devices, shards(): corner = lax.ppermute(corner, ('lat', 'lon'), both_pairs)  5.94 us
    all_to_all x1, starting transfers between devices, shards(): folded = exchange(solve(packed[1], points // 2))  4 us
    pallas_call x1, Pallas kernels, merge(): pl.pallas_call(merge_kernel, out_shape=(shape(TILES_LAT * TILES_LON), sha...  3.45 us
    pallas_call x1, Pallas kernels, pack(): pl.pallas_call(functools.partial(pack_kernel, columns, lon_devices, capac...  3.06 us
    all_to_all x1, waiting for transfers between devices, shards(): arrived = exchange(packed[0])  1.84 us
  transfers between devices with their start and end apart: 5, of which 3 were waited for; matrix products, arithmetic and copies ran while one was open for 0% of the time, Pallas kernels for 37%

profile of v6, /device:TPU:1, one launch (start us, length us, event | category | flops | bytes accessed | tf_op | source)
XLA Modules:
  0.0 78.8 jit_solution(17865751806517543227)
XLA Ops:
  0.6 3.1 %pack.1 = (bf16[32,72,128]{2,1,0:T(8,128)(2,1)}, bf16[32,72,128]{2,1,0:T(8,128)(2,1)}) custom-call(s32[64]{0:T(128)} %owner.1, s32[64]{0:T(128)} %count.1, bf16[64,64,128]{2,1,0:T(8,128)(2,1)} %pert.1, bf16[64,64]{1,0:T(8,128)(2,1)} %prec.1, bf16[64,64]{1,0:T(8,128)(2,1)} %dep.1), custom_call_target="tpu_custom_call" | custom-call | tf_op jit(solution)/shard_map/pack/pallas_call | solution.py:99
  3.7 7.1 %all-to-all-start = ((bf16[32,72,128]{2,1,0:T(8,128)(2,1)}), bf16[32,72,128]{2,1,0:T(8,128)(2,1)S(1)}, u32[]{:S(2)}, u32[]{:S(2)}) async-start(bf16[32,72,128]{2,1,0:T(8,128)(2,1)} %get-tuple-element.8), calls=%async_computation | async-start | bytes 1179648 | tf_op jit(solution)/shard_map/all_to_all | solution.py:566
  10.8 14.7 %solve.3 = bf16[32,72,128]{2,1,0:T(8,128)(2,1)} custom-call(bf16[32,72,128]{2,1,0:T(8,128)(2,1)} %get-tuple-element.9.arrived), custom_call_target="tpu_custom_call" | custom-call | flops 1920000000 | bytes 1920000 | tf_op jit(solution)/shard_map/solve/pallas_call | solution.py:340
  25.5 1.8 %all-to-all-done.arrived = bf16[32,72,128]{2,1,0:T(8,128)(2,1)S(1)} async-done(((bf16[32,72,128]{2,1,0:T(8,128)(2,1)}), bf16[32,72,128]{2,1,0:T(8,128)(2,1)S(1)}, u32[]{:S(2)}, u32[]{:S(2)}) %all-to-all-start) | async-done | bytes 589856 | tf_op jit(solution)/shard_map/all_to_all | solution.py:566
  27.3 0.0 copy-start.1
  27.3 4.0 %all-to-all-start.1 = ((bf16[32,72,128]{2,1,0:T(8,128)(2,1)}), bf16[32,72,128]{2,1,0:T(8,128)(2,1)S(1)}, u32[]{:S(2)}, u32[]{:S(2)}) async-start(bf16[32,72,128]{2,1,0:T(8,128)(2,1)} %solve.3), calls=%async_computation.1 | async-start | bytes 1179648 | tf_op jit(solution)/shard_map/all_to_all | solution.py:568
  31.3 0.0 copy-done.1
  31.3 14.7 %solve.2.refs_0_ = bf16[32,72,128]{2,1,0:T(8,128)(2,1)} custom-call(bf16[32,72,128]{2,1,0:T(8,128)(2,1)} %copy-done.1), custom_call_target="tpu_custom_call" | custom-call | flops 1920000000 | bytes 1920000 | tf_op jit(solution)/shard_map/solve/pallas_call | solution.py:340
  46.0 1.8 %all-to-all-done.1.refs_1_ = bf16[32,72,128]{2,1,0:T(8,128)(2,1)S(1)} async-done(((bf16[32,72,128]{2,1,0:T(8,128)(2,1)}), bf16[32,72,128]{2,1,0:T(8,128)(2,1)S(1)}, u32[]{:S(2)}, u32[]{:S(2)}) %all-to-all-start.1) | async-done | bytes 589856 | tf_op jit(solution)/shard_map/all_to_all | solution.py:568
  47.9 0.0 copy-start
  47.9 0.8 %copy-done = bf16[32,72,128]{2,1,0:T(8,128)(2,1)} copy-done((bf16[32,72,128]{2,1,0:T(8,128)(2,1)}, bf16[32,72,128]{2,1,0:T(8,128)(2,1)S(1)}, u32[]{:S(2)}) %copy-start) | copy-done | bytes 589848
  48.7 3.4 %merge.1 = (bf16[64,72,128]{2,1,0:T(8,128)(2,1)}, bf16[8,72,128]{2,1,0:T(8,128)(2,1)}, bf16[8,72,128]{2,1,0:T(8,128)(2,1)}, bf16[1,72,128]{2,1,0:T(8,128)(2,1)}) custom-call(bf16[32,72,128]{2,1,0:T(8,128)(2,1)} %solve.2.refs_0_, bf16[32,72,128]{2,1,0:T(8,128)(2,1)} %copy-done), custom_call_target="tpu_custom_call" | custom-call | tf_op jit(solution)/shard_map/merge/pallas_call | solution.py:383
  52.1 0.5 collective-permute-start
  52.6 1.3 %collective-permute-start.1 = (bf16[8,72,128]{2,1,0:T(8,128)(2,1)}, bf16[8,72,128]{2,1,0:T(8,128)(2,1)S(1)}, u32[]{:S(2)}, u32[]{:S(2)}) collective-permute-start(bf16[8,72,128]{2,1,0:T(8,128)(2,1)} %get-tuple-element.12), channel_id=1, source_target_pairs={{8,0},{16,8},{24,16},{9,1},{17,9},{25,17},{10,2},{18,10},{26,18},{... | collective-permute-start | bytes 442376 | tf_op jit(solution)/shard_map/ppermute | solution.py:578
  53.9 1.3 %collective-permute-start.2 = (bf16[1,72,128]{2,1,0:T(8,128)(2,1)}, bf16[1,72,128]{2,1,0:T(8,128)(2,1)S(1)}, u32[]{:S(2)}, u32[]{:S(2)}) collective-permute-start(bf16[1,72,128]{2,1,0:T(8,128)(2,1)} %get-tuple-element.13), channel_id=1, source_target_pairs={{8,7},{9,0},{10,1},{11,2},{12,3},{13,4},{14,5},{15,6},{16,15},{17,... | collective-permute-start | bytes 55304 | tf_op jit(solution)/shard_map/ppermute | solution.py:579
  55.2 5.9 %collective-permute-done.2.corner = bf16[1,72,128]{2,1,0:T(8,128)(2,1)S(1)} collective-permute-done((bf16[1,72,128]{2,1,0:T(8,128)(2,1)}, bf16[1,72,128]{2,1,0:T(8,128)(2,1)S(1)}, u32[]{:S(2)}, u32[]{:S(2)}) %collective-permute-start.2) | collective-permute-done | bytes 18464 | tf_op jit(solution)/shard_map/ppermute | solution.py:579
  61.2 0.0 copy-start.4
  61.2 0.0 collective-permute-done.east.next_east
  61.2 0.0 copy-start.2
  61.2 0.0 collective-permute-done.1.north
  61.2 0.0 copy-start.3
  61.2 0.6 copy-done.4
  61.8 0.1 copy-done.2
  61.9 0.0 copy-done.3
  61.9 16.9 %apply.1 = (bf16[1,200,200,128]{3,2,1,0:T(8,128)(2,1)}, f32[1,200,200]{2,1,0:T(8,128)}) custom-call(s32[1]{0:T(128)} %bitcast.top, bf16[64,72,128]{2,1,0:T(8,128)(2,1)} %get-tuple-element.10.own.next_own, bf16[8,72,128]{2,1,0:T(8,128)(2,1)} %copy-done.2, bf16[64,72,128]{2,1,0:T(8,128)(2,1)} %get-tuple-element.10.own.next_own, bf16[8,72,128]{2,1,0:T(8,128)(2,1)} %copy-done.2, ...), custom_call_target="tpu_custom_call" | custom-call | tf_op jit(solution)/shard_map/apply/pallas_call | solution.py:524
Async XLA Ops:
  3.7 23.6 %all-to-all-start = ((bf16[32,72,128]{2,1,0:T(8,128)(2,1)}), bf16[32,72,128]{2,1,0:T(8,128)(2,1)S(1)}, u32[]{:S(2)}, u32[]{:S(2)}) async-start(bf16[32,72,128]{2,1,0:T(8,128)(2,1)} %get-tuple-element.8), calls=%async_computation | async-start | bytes 1179648 | tf_op jit(solution)/shard_map/all_to_all | solution.py:566
  27.3 4.0 %copy-start.1 = (bf16[32,72,128]{2,1,0:T(8,128)(2,1)}, bf16[32,72,128]{2,1,0:T(8,128)(2,1)S(1)}, u32[]{:S(2)}) copy-start(bf16[32,72,128]{2,1,0:T(8,128)(2,1)S(1)} %all-to-all-done.arrived) | copy-start | bytes 1769476
  27.3 20.5 %all-to-all-start.1 = ((bf16[32,72,128]{2,1,0:T(8,128)(2,1)}), bf16[32,72,128]{2,1,0:T(8,128)(2,1)S(1)}, u32[]{:S(2)}, u32[]{:S(2)}) async-start(bf16[32,72,128]{2,1,0:T(8,128)(2,1)} %solve.3), calls=%async_computation.1 | async-start | bytes 1179648 | tf_op jit(solution)/shard_map/all_to_all | solution.py:568
  47.9 0.8 %copy-start = (bf16[32,72,128]{2,1,0:T(8,128)(2,1)}, bf16[32,72,128]{2,1,0:T(8,128)(2,1)S(1)}, u32[]{:S(2)}) copy-start(bf16[32,72,128]{2,1,0:T(8,128)(2,1)S(1)} %all-to-all-done.1.refs_1_) | copy-start | bytes 1769476
  52.1 9.1 %collective-permute-start = (bf16[8,72,128]{2,1,0:T(8,128)(2,1)}, bf16[8,72,128]{2,1,0:T(8,128)(2,1)S(1)}, u32[]{:S(2)}, u32[]{:S(2)}) collective-permute-start(bf16[8,72,128]{2,1,0:T(8,128)(2,1)} %get-tuple-element.11), channel_id=1, source_target_pairs={{0,7},{1,0},{2,1},{3,2},{4,3},{5,4},{6,5},{7,6},{8,15},{9,8},{10,9... | collective-permute-start | bytes 442376 | tf_op jit(solution)/shard_map/ppermute | solution.py:577
  52.6 8.5 %collective-permute-start.1 = (bf16[8,72,128]{2,1,0:T(8,128)(2,1)}, bf16[8,72,128]{2,1,0:T(8,128)(2,1)S(1)}, u32[]{:S(2)}, u32[]{:S(2)}) collective-permute-start(bf16[8,72,128]{2,1,0:T(8,128)(2,1)} %get-tuple-element.12), channel_id=1, source_target_pairs={{8,0},{16,8},{24,16},{9,1},{17,9},{25,17},{10,2},{18,10},{26,18},{... | collective-permute-start | bytes 442376 | tf_op jit(solution)/shard_map/ppermute | solution.py:578
  53.9 7.3 %collective-permute-start.2 = (bf16[1,72,128]{2,1,0:T(8,128)(2,1)}, bf16[1,72,128]{2,1,0:T(8,128)(2,1)S(1)}, u32[]{:S(2)}, u32[]{:S(2)}) collective-permute-start(bf16[1,72,128]{2,1,0:T(8,128)(2,1)} %get-tuple-element.13), channel_id=1, source_target_pairs={{8,7},{9,0},{10,1},{11,2},{12,3},{13,4},{14,5},{15,6},{16,15},{17,... | collective-permute-start | bytes 55304 | tf_op jit(solution)/shard_map/ppermute | solution.py:579
  61.2 0.6 copy-start.4
  61.2 0.7 copy-start.2
  61.2 0.7 copy-start.3

commit v7 on v6

--- a/solution.py
+++ b/solution.py
@@ -7,6 +7,7 @@
 from jax.experimental import pallas as pl
 from jax.experimental.pallas import tpu as pltpu
 from jax.sharding import PartitionSpec as P
+
 
 FINE = 25
 TILES_LAT = 8
@@ -276,6 +277,7 @@
             small(index)
         if after == members:
             continue
+
         def trail(index, begin, stop):
             start = index * per
             rest = stop - begin
@@ -334,7 +336,7 @@
 
 
 def solve(arrived, points):
-    slots, rows, members = arrived.shape
+    _, _, members = arrived.shape
     height = members // 2 + META
     vmem = pl.BlockSpec(memory_space=pltpu.VMEM)
     return pl.pallas_call(
@@ -409,7 +411,8 @@
 
 
 def apply_kernel(
-    top, own, east, next_own, next_east, north, corner, anomalies, flux, out, mean, weights
+    top, own, east, next_own, next_east, far_own, far_east, north, corner, anomalies, flux,
+    out, mean, bases, changes, ready_bases, ready_changes,
 ):
     members = anomalies.shape[3]
     cols = anomalies.shape[2]
@@ -418,7 +421,9 @@
     now = lax.rem(step, 2)
     later = 1 - now
     from_north = (step == TILES_LAT - 1) & (top[0] == 0)
+    far_north = (step == TILES_LAT - 2) & (top[0] == 0)
     half = (FINE + 1) // 2
+
     def here(col):
         return own[col] if col < TILES_LON else east[0]
 
@@ -426,6 +431,11 @@
         inner = next_own[col] if col < TILES_LON else next_east[0]
         outer = north[col] if col < TILES_LON else corner[0]
         return jnp.where(from_north, outer, inner)
+
+    def beyond(col):
+        inner = far_own[col] if col < TILES_LON else far_east[0]
+        outer = north[col] if col < TILES_LON else corner[0]
+        return jnp.where(far_north, outer, inner)
 
     def means_of(blocks):
         lines = [block[members // 2 :].astype(F32)[0:1] for block in blocks]
@@ -437,15 +447,22 @@
         axis=0,
     ).astype(BF16)
 
-    def put(place, col, folded):
-        factor = unfolded(folded)
-        weights[place, col * members : (col + 1) * members, 0:members] = factor.astype(BF16)
-        return factor
+    places = [slice(col * members, (col + 1) * members) for col in columns]
+
+    def prepare(col, folded, slot):
+        high = unfolded(folded)
+        low = bases[slot, places[col], :].astype(F32)
+        ready_bases[places[col], :] = high.astype(BF16)
+        ready_changes[places[col], :] = ((high - low) * (1.0 / FINE)).astype(BF16)
 
     @pl.when(step == 0)
     def _():
         for col in columns:
-            put(now, col, here(col))
+            bases[now, places[col], :] = unfolded(here(col)).astype(BF16)
+            prepare(col, above(col), now)
+
+    bases[later] = ready_bases[...]
+    changes[...] = ready_changes[...]
 
     corner_index = lax.broadcasted_iota(jnp.int32, (16, cols), 0)
     cell = lax.broadcasted_iota(jnp.int32, (16, cols), 1)
@@ -473,14 +490,6 @@
             place = pl.ds(tile_row * FINE + line, 1)
             mean[0, place, :] = flux[0, place, :] + shift
 
-    for col in columns:
-        high = put(later, col, above(col))
-        place = slice(col * members, (col + 1) * members)
-        low = weights[now, place, 0:members].astype(F32)
-        change = ((high - low) * (1.0 / FINE)).astype(BF16)
-        weights[0, place, members:] = change
-        weights[1, place, members:] = change
-
     width = 32
     offset = lax.broadcasted_iota(jnp.int32, (width, members), 0)
     for part, (start, stop) in enumerate(((0, half), (half, FINE))):
@@ -495,7 +504,10 @@
             scaled = field * number
             left = jnp.concatenate([field, scaled], axis=2).reshape(count * width, 2 * members)
             place = slice(col * members, (col + 2) * members)
-            both = dot(left, weights[later if part else now, place, :], NT).reshape(count, width, 2 * members)
+            right = jnp.concatenate(
+                [bases[later if part else now, place, :], changes[place, :]], axis=1
+            )
+            both = dot(left, right, NT).reshape(count, width, 2 * members)
             cell = offset - col
             inside = (cell >= 0) & (cell < FINE)
             right_weight = jnp.where(inside, cell.astype(F32) / FINE, 0.0)
@@ -510,6 +522,9 @@
             ).astype(BF16)
         out[0, start:stop, cols - 8 :, :] = carry.astype(BF16)
 
+    for col in columns:
+        prepare(col, beyond(col), later)
+
 
 def apply(top, own, east, north, corner, anomalies, flux):
     lags, rows, cols, members = anomalies.shape
@@ -518,6 +533,7 @@
     one = lambda at: pl.BlockSpec((1, height, members), lambda l, r: (at(r), 0, 0))
     same = lambda r: r
     above = lambda r: jnp.minimum(r + 1, TILES_LAT - 1)
+    beyond = lambda r: jnp.minimum(r + 2, TILES_LAT - 1)
     fixed = lambda r: 0
     strip = pl.BlockSpec((1, FINE, cols, members), lambda l, r: (l, r, 0, 0))
     plane = pl.BlockSpec((1, rows, cols), lambda l, r: (l, 0, 0))
@@ -534,6 +550,8 @@
             one(same),
             line(above),
             one(above),
+            line(beyond),
+            one(beyond),
             line(fixed),
             one(fixed),
             strip,
@@ -541,17 +559,20 @@
         ],
         out_specs=(strip, plane),
         scratch_shapes=[
-            pltpu.VMEM((2, (TILES_LON + 1) * members, 2 * members), BF16),
+            pltpu.VMEM((2, (TILES_LON + 1) * members, members), BF16),
+            pltpu.VMEM(((TILES_LON + 1) * members, members), BF16),
+            pltpu.VMEM(((TILES_LON + 1) * members, members), BF16),
+            pltpu.VMEM(((TILES_LON + 1) * members, members), BF16),
         ],
         name="apply",
-    )(top, own, east, own, east, north, corner, anomalies, flux)
+    )(top, own, east, own, east, own, east, north, corner, anomalies, flux)
 
 
 def shards(obs_pert, obs_dep, obs_prec, obs_count, owner_point, anomalies, flux_mean):
     lat_devices = lax.axis_size("lat")
     lon_devices = lax.axis_size("lon")
     devices = lat_devices * lon_devices
-    holding, locn, members = obs_pert.shape
+    holding, _, _ = obs_pert.shape
     capacity = max(1, (holding + devices - 1) // devices)
     columns = TILES_LON * lon_devices
     points = TILES_LAT * TILES_LON
@@ -574,9 +595,9 @@
     both_pairs = [
         (a * lon_devices + c, b * lon_devices + d) for a, b in lat_pairs for c, d in lon_pairs
     ]
-    east = lax.ppermute(east, "lon", lon_pairs)
     north = lax.ppermute(north, "lat", lat_pairs)
     corner = lax.ppermute(corner, ("lat", "lon"), both_pairs)
+    east = lax.ppermute(east, "lon", lon_pairs)
     top = (lax.axis_index("lat") == lat_devices - 1).astype(jnp.int32).reshape(1)
     return apply(top, own, east, north, corner, anomalies, flux_mean)
 

time: 79.5 us -> 79.5 us (level)
  no operation moved by 1% of the time
where the time goes in v7:
time: 79.5 us; the launch traced here: 78.8 us
  Pallas kernels  52.8 us (66%)
  starting transfers between devices  14.2 us (18%)
  waiting for transfers between devices  9.6 us (12%)
  local copies, waits for them, and re-layouts  1.52 us (2%)
    pallas_call x2, Pallas kernels, solve(): pl.pallas_call(solve_kernel, out_shape=jax.ShapeDtypeStruct((points, heig...  29.4 us
    pallas_call x1, Pallas kernels, apply(): pl.pallas_call(apply_kernel, grid=(lags, TILES_LAT), out_shape=(jax.Shape...  16.9 us
    all_to_all x1, starting transfers between devices, shards(): arrived = exchange(packed[0])  7.08 us
    ppermute x1, waiting for transfers between devices, shards(): corner = lax.ppermute(corner, ('lat', 'lon'), both_pairs)  5.94 us
    all_to_all x1, starting transfers between devices, shards(): folded = exchange(solve(packed[1], points // 2))  4 us
    pallas_call x1, Pallas kernels, merge(): pl.pallas_call(merge_kernel, out_shape=(shape(TILES_LAT * TILES_LON), sha...  3.45 us
    pallas_call x1, Pallas kernels, pack(): pl.pallas_call(functools.partial(pack_kernel, columns, lon_devices, capac...  3.06 us
    all_to_all x1, waiting for transfers between devices, shards(): arrived = exchange(packed[0])  1.84 us
  transfers between devices with their start and end apart: 5, of which 3 were waited for; matrix products, arithmetic and copies ran while one was open for 0% of the time, Pallas kernels for 37%

profile of v7, /device:TPU:1, one launch (start us, length us, event | category | flops | bytes accessed | tf_op | source)
XLA Modules:
  0.0 78.8 jit_solution(8796950182040075706)
XLA Ops:
  0.6 3.1 %pack.1 = (bf16[32,72,128]{2,1,0:T(8,128)(2,1)}, bf16[32,72,128]{2,1,0:T(8,128)(2,1)}) custom-call(s32[64]{0:T(128)} %owner.1, s32[64]{0:T(128)} %count.1, bf16[64,64,128]{2,1,0:T(8,128)(2,1)} %pert.1, bf16[64,64]{1,0:T(8,128)(2,1)} %prec.1, bf16[64,64]{1,0:T(8,128)(2,1)} %dep.1), custom_call_target="tpu_custom_call" | custom-call | tf_op jit(solution)/shard_map/pack/pallas_call | solution.py:100
  3.7 7.1 %all-to-all-start = ((bf16[32,72,128]{2,1,0:T(8,128)(2,1)}), bf16[32,72,128]{2,1,0:T(8,128)(2,1)S(1)}, u32[]{:S(2)}, u32[]{:S(2)}) async-start(bf16[32,72,128]{2,1,0:T(8,128)(2,1)} %get-tuple-element.8), calls=%async_computation | async-start | bytes 1179648 | tf_op jit(solution)/shard_map/all_to_all | solution.py:587
  10.8 14.7 %solve.3 = bf16[32,72,128]{2,1,0:T(8,128)(2,1)} custom-call(bf16[32,72,128]{2,1,0:T(8,128)(2,1)} %get-tuple-element.9.arrived), custom_call_target="tpu_custom_call" | custom-call | flops 1920000000 | bytes 1920000 | tf_op jit(solution)/shard_map/solve/pallas_call | solution.py:342
  25.5 1.8 %all-to-all-done.arrived = bf16[32,72,128]{2,1,0:T(8,128)(2,1)S(1)} async-done(((bf16[32,72,128]{2,1,0:T(8,128)(2,1)}), bf16[32,72,128]{2,1,0:T(8,128)(2,1)S(1)}, u32[]{:S(2)}, u32[]{:S(2)}) %all-to-all-start) | async-done | bytes 589856 | tf_op jit(solution)/shard_map/all_to_all | solution.py:587
  27.3 0.0 copy-start.2
  27.3 4.0 %all-to-all-start.1 = ((bf16[32,72,128]{2,1,0:T(8,128)(2,1)}), bf16[32,72,128]{2,1,0:T(8,128)(2,1)S(1)}, u32[]{:S(2)}, u32[]{:S(2)}) async-start(bf16[32,72,128]{2,1,0:T(8,128)(2,1)} %solve.3), calls=%async_computation.1 | async-start | bytes 1179648 | tf_op jit(solution)/shard_map/all_to_all | solution.py:589
  31.3 0.0 copy-done.2
  31.3 14.7 %solve.2.refs_0_ = bf16[32,72,128]{2,1,0:T(8,128)(2,1)} custom-call(bf16[32,72,128]{2,1,0:T(8,128)(2,1)} %copy-done.2), custom_call_target="tpu_custom_call" | custom-call | flops 1920000000 | bytes 1920000 | tf_op jit(solution)/shard_map/solve/pallas_call | solution.py:342
  46.0 1.8 %all-to-all-done.1.refs_1_ = bf16[32,72,128]{2,1,0:T(8,128)(2,1)S(1)} async-done(((bf16[32,72,128]{2,1,0:T(8,128)(2,1)}), bf16[32,72,128]{2,1,0:T(8,128)(2,1)S(1)}, u32[]{:S(2)}, u32[]{:S(2)}) %all-to-all-start.1) | async-done | bytes 589856 | tf_op jit(solution)/shard_map/all_to_all | solution.py:589
  47.9 0.0 copy-start
  47.9 0.8 %copy-done = bf16[32,72,128]{2,1,0:T(8,128)(2,1)} copy-done((bf16[32,72,128]{2,1,0:T(8,128)(2,1)}, bf16[32,72,128]{2,1,0:T(8,128)(2,1)S(1)}, u32[]{:S(2)}) %copy-start) | copy-done | bytes 589848
  48.7 3.4 %merge.1 = (bf16[64,72,128]{2,1,0:T(8,128)(2,1)}, bf16[8,72,128]{2,1,0:T(8,128)(2,1)}, bf16[8,72,128]{2,1,0:T(8,128)(2,1)}, bf16[1,72,128]{2,1,0:T(8,128)(2,1)}) custom-call(bf16[32,72,128]{2,1,0:T(8,128)(2,1)} %solve.2.refs_0_, bf16[32,72,128]{2,1,0:T(8,128)(2,1)} %copy-done), custom_call_target="tpu_custom_call" | custom-call | tf_op jit(solution)/shard_map/merge/pallas_call | solution.py:385
  52.1 0.5 collective-permute-start
  52.6 1.3 %collective-permute-start.1 = (bf16[8,72,128]{2,1,0:T(8,128)(2,1)}, bf16[8,72,128]{2,1,0:T(8,128)(2,1)S(1)}, u32[]{:S(2)}, u32[]{:S(2)}) collective-permute-start(bf16[8,72,128]{2,1,0:T(8,128)(2,1)} %get-tuple-element.12), channel_id=1, source_target_pairs={{8,0},{16,8},{24,16},{9,1},{17,9},{25,17},{10,2},{18,10},{26,18},{... | collective-permute-start | bytes 442376 | tf_op jit(solution)/shard_map/ppermute | solution.py:598
  53.9 1.3 %collective-permute-start.2 = (bf16[1,72,128]{2,1,0:T(8,128)(2,1)}, bf16[1,72,128]{2,1,0:T(8,128)(2,1)S(1)}, u32[]{:S(2)}, u32[]{:S(2)}) collective-permute-start(bf16[1,72,128]{2,1,0:T(8,128)(2,1)} %get-tuple-element.13), channel_id=1, source_target_pairs={{8,7},{9,0},{10,1},{11,2},{12,3},{13,4},{14,5},{15,6},{16,15},{17,... | collective-permute-start | bytes 55304 | tf_op jit(solution)/shard_map/ppermute | solution.py:599
  55.2 5.9 %collective-permute-done.2.corner = bf16[1,72,128]{2,1,0:T(8,128)(2,1)S(1)} collective-permute-done((bf16[1,72,128]{2,1,0:T(8,128)(2,1)}, bf16[1,72,128]{2,1,0:T(8,128)(2,1)S(1)}, u32[]{:S(2)}, u32[]{:S(2)}) %collective-permute-start.2) | collective-permute-done | bytes 18464 | tf_op jit(solution)/shard_map/ppermute | solution.py:599
  61.2 0.0 copy-start.4
  61.2 0.0 collective-permute-done.east.next_east.far_east
  61.2 0.0 copy-start.1
  61.2 0.0 collective-permute-done.1.north
  61.2 0.0 copy-start.3
  61.2 0.6 copy-done.4
  61.8 0.1 copy-done.1
  61.9 0.0 copy-done.3
  61.9 16.9 %apply.1 = (bf16[1,200,200,128]{3,2,1,0:T(8,128)(2,1)}, f32[1,200,200]{2,1,0:T(8,128)}) custom-call(s32[1]{0:T(128)} %bitcast.top, bf16[64,72,128]{2,1,0:T(8,128)(2,1)} %get-tuple-element.10.own.next_own.far_own, bf16[8,72,128]{2,1,0:T(8,128)(2,1)} %copy-done.1, bf16[64,72,128]{2,1,0:T(8,128)(2,1)} %get-tuple-element.10.own.next_own.far_own, ...), custom_call_target="tpu_custom_call" | custom-call | tf_op jit(solution)/shard_map/apply/pallas_call | solution.py:540
Async XLA Ops:
  3.7 23.6 %all-to-all-start = ((bf16[32,72,128]{2,1,0:T(8,128)(2,1)}), bf16[32,72,128]{2,1,0:T(8,128)(2,1)S(1)}, u32[]{:S(2)}, u32[]{:S(2)}) async-start(bf16[32,72,128]{2,1,0:T(8,128)(2,1)} %get-tuple-element.8), calls=%async_computation | async-start | bytes 1179648 | tf_op jit(solution)/shard_map/all_to_all | solution.py:587
  27.3 4.0 %copy-start.2 = (bf16[32,72,128]{2,1,0:T(8,128)(2,1)}, bf16[32,72,128]{2,1,0:T(8,128)(2,1)S(1)}, u32[]{:S(2)}) copy-start(bf16[32,72,128]{2,1,0:T(8,128)(2,1)S(1)} %all-to-all-done.arrived) | copy-start | bytes 1769476
  27.3 20.5 %all-to-all-start.1 = ((bf16[32,72,128]{2,1,0:T(8,128)(2,1)}), bf16[32,72,128]{2,1,0:T(8,128)(2,1)S(1)}, u32[]{:S(2)}, u32[]{:S(2)}) async-start(bf16[32,72,128]{2,1,0:T(8,128)(2,1)} %solve.3), calls=%async_computation.1 | async-start | bytes 1179648 | tf_op jit(solution)/shard_map/all_to_all | solution.py:589
  47.9 0.8 %copy-start = (bf16[32,72,128]{2,1,0:T(8,128)(2,1)}, bf16[32,72,128]{2,1,0:T(8,128)(2,1)S(1)}, u32[]{:S(2)}) copy-start(bf16[32,72,128]{2,1,0:T(8,128)(2,1)S(1)} %all-to-all-done.1.refs_1_) | copy-start | bytes 1769476
  52.1 9.1 %collective-permute-start = (bf16[8,72,128]{2,1,0:T(8,128)(2,1)}, bf16[8,72,128]{2,1,0:T(8,128)(2,1)S(1)}, u32[]{:S(2)}, u32[]{:S(2)}) collective-permute-start(bf16[8,72,128]{2,1,0:T(8,128)(2,1)} %get-tuple-element.11), channel_id=1, source_target_pairs={{0,7},{1,0},{2,1},{3,2},{4,3},{5,4},{6,5},{7,6},{8,15},{9,8},{10,9... | collective-permute-start | bytes 442376 | tf_op jit(solution)/shard_map/ppermute | solution.py:600
  52.6 8.5 %collective-permute-start.1 = (bf16[8,72,128]{2,1,0:T(8,128)(2,1)}, bf16[8,72,128]{2,1,0:T(8,128)(2,1)S(1)}, u32[]{:S(2)}, u32[]{:S(2)}) collective-permute-start(bf16[8,72,128]{2,1,0:T(8,128)(2,1)} %get-tuple-element.12), channel_id=1, source_target_pairs={{8,0},{16,8},{24,16},{9,1},{17,9},{25,17},{10,2},{18,10},{26,18},{... | collective-permute-start | bytes 442376 | tf_op jit(solution)/shard_map/ppermute | solution.py:598
  53.9 7.3 %collective-permute-start.2 = (bf16[1,72,128]{2,1,0:T(8,128)(2,1)}, bf16[1,72,128]{2,1,0:T(8,128)(2,1)S(1)}, u32[]{:S(2)}, u32[]{:S(2)}) collective-permute-start(bf16[1,72,128]{2,1,0:T(8,128)(2,1)} %get-tuple-element.13), channel_id=1, source_target_pairs={{8,7},{9,0},{10,1},{11,2},{12,3},{13,4},{14,5},{15,6},{16,15},{17,... | collective-permute-start | bytes 55304 | tf_op jit(solution)/shard_map/ppermute | solution.py:599
  61.2 0.6 copy-start.4
  61.2 0.7 copy-start.1
  61.2 0.7 copy-start.3

commit v8 on v7

--- a/solution.py
+++ b/solution.py
@@ -450,15 +450,15 @@
     places = [slice(col * members, (col + 1) * members) for col in columns]
 
     def prepare(col, folded, slot):
-        high = unfolded(folded)
-        low = bases[slot, places[col], :].astype(F32)
-        ready_bases[places[col], :] = high.astype(BF16)
-        ready_changes[places[col], :] = ((high - low) * (1.0 / FINE)).astype(BF16)
+        high = unfolded(folded).T
+        low = bases[slot, :, places[col]].astype(F32)
+        ready_bases[:, places[col]] = high.astype(BF16)
+        ready_changes[:, places[col]] = ((high - low) * (1.0 / FINE)).astype(BF16)
 
     @pl.when(step == 0)
     def _():
         for col in columns:
-            bases[now, places[col], :] = unfolded(here(col)).astype(BF16)
+            bases[now, :, places[col]] = unfolded(here(col)).T.astype(BF16)
             prepare(col, above(col), now)
 
     bases[later] = ready_bases[...]
@@ -505,9 +505,9 @@
             left = jnp.concatenate([field, scaled], axis=2).reshape(count * width, 2 * members)
             place = slice(col * members, (col + 2) * members)
             right = jnp.concatenate(
-                [bases[later if part else now, place, :], changes[place, :]], axis=1
+                [bases[later if part else now, :, place], changes[:, place]], axis=0
             )
-            both = dot(left, right, NT).reshape(count, width, 2 * members)
+            both = dot(left, right).reshape(count, width, 2 * members)
             cell = offset - col
             inside = (cell >= 0) & (cell < FINE)
             right_weight = jnp.where(inside, cell.astype(F32) / FINE, 0.0)
@@ -559,10 +559,10 @@
         ],
         out_specs=(strip, plane),
         scratch_shapes=[
-            pltpu.VMEM((2, (TILES_LON + 1) * members, members), BF16),
-            pltpu.VMEM(((TILES_LON + 1) * members, members), BF16),
-            pltpu.VMEM(((TILES_LON + 1) * members, members), BF16),
-            pltpu.VMEM(((TILES_LON + 1) * members, members), BF16),
+            pltpu.VMEM((2, members, (TILES_LON + 1) * members), BF16),
+            pltpu.VMEM((members, (TILES_LON + 1) * members), BF16),
+            pltpu.VMEM((members, (TILES_LON + 1) * members), BF16),
+            pltpu.VMEM((members, (TILES_LON + 1) * members), BF16),
         ],
         name="apply",
     )(top, own, east, own, east, own, east, north, corner, anomalies, flux)

time: 79.5 us -> 80.3 us (1.010)
  no operation moved by 1% of the time
where the time goes in v8:
time: 80.3 us; the launch traced here: 79.5 us
  Pallas kernels  53.5 us (67%)
  starting transfers between devices  14.2 us (18%)
  waiting for transfers between devices  9.6 us (12%)
  local copies, waits for them, and re-layouts  1.52 us (2%)
    pallas_call x2, Pallas kernels, solve(): pl.pallas_call(solve_kernel, out_shape=jax.ShapeDtypeStruct((points, heig...  29.4 us
    pallas_call x1, Pallas kernels, apply(): pl.pallas_call(apply_kernel, grid=(lags, TILES_LAT), out_shape=(jax.Shape...  17.6 us
    all_to_all x1, starting transfers between devices, shards(): arrived = exchange(packed[0])  7.08 us
    ppermute x1, waiting for transfers between devices, shards(): corner = lax.ppermute(corner, ('lat', 'lon'), both_pairs)  5.94 us
    all_to_all x1, starting transfers between devices, shards(): folded = exchange(solve(packed[1], points // 2))  4 us
    pallas_call x1, Pallas kernels, merge(): pl.pallas_call(merge_kernel, out_shape=(shape(TILES_LAT * TILES_LON), sha...  3.45 us
    pallas_call x1, Pallas kernels, pack(): pl.pallas_call(functools.partial(pack_kernel, columns, lon_devices, capac...  3.06 us
    all_to_all x1, waiting for transfers between devices, shards(): arrived = exchange(packed[0])  1.84 us
  transfers between devices with their start and end apart: 5, of which 3 were waited for; matrix products, arithmetic and copies ran while one was open for 0% of the time, Pallas kernels for 37%

profile of v8, /device:TPU:1, one launch (start us, length us, event | category | flops | bytes accessed | tf_op | source)
XLA Modules:
  0.0 79.5 jit_solution(6198871822831483204)
XLA Ops:
  0.6 3.1 %pack.1 = (bf16[32,72,128]{2,1,0:T(8,128)(2,1)}, bf16[32,72,128]{2,1,0:T(8,128)(2,1)}) custom-call(s32[64]{0:T(128)} %owner.1, s32[64]{0:T(128)} %count.1, bf16[64,64,128]{2,1,0:T(8,128)(2,1)} %pert.1, bf16[64,64]{1,0:T(8,128)(2,1)} %prec.1, bf16[64,64]{1,0:T(8,128)(2,1)} %dep.1), custom_call_target="tpu_custom_call" | custom-call | tf_op jit(solution)/shard_map/pack/pallas_call | solution.py:100
  3.7 7.1 %all-to-all-start = ((bf16[32,72,128]{2,1,0:T(8,128)(2,1)}), bf16[32,72,128]{2,1,0:T(8,128)(2,1)S(1)}, u32[]{:S(2)}, u32[]{:S(2)}) async-start(bf16[32,72,128]{2,1,0:T(8,128)(2,1)} %get-tuple-element.8), calls=%async_computation | async-start | bytes 1179648 | tf_op jit(solution)/shard_map/all_to_all | solution.py:587
  10.8 14.7 %solve.3 = bf16[32,72,128]{2,1,0:T(8,128)(2,1)} custom-call(bf16[32,72,128]{2,1,0:T(8,128)(2,1)} %get-tuple-element.9.arrived), custom_call_target="tpu_custom_call" | custom-call | flops 1920000000 | bytes 1920000 | tf_op jit(solution)/shard_map/solve/pallas_call | solution.py:342
  25.5 1.8 %all-to-all-done.arrived = bf16[32,72,128]{2,1,0:T(8,128)(2,1)S(1)} async-done(((bf16[32,72,128]{2,1,0:T(8,128)(2,1)}), bf16[32,72,128]{2,1,0:T(8,128)(2,1)S(1)}, u32[]{:S(2)}, u32[]{:S(2)}) %all-to-all-start) | async-done | bytes 589856 | tf_op jit(solution)/shard_map/all_to_all | solution.py:587
  27.3 0.0 copy-start.2
  27.3 4.0 %all-to-all-start.1 = ((bf16[32,72,128]{2,1,0:T(8,128)(2,1)}), bf16[32,72,128]{2,1,0:T(8,128)(2,1)S(1)}, u32[]{:S(2)}, u32[]{:S(2)}) async-start(bf16[32,72,128]{2,1,0:T(8,128)(2,1)} %solve.3), calls=%async_computation.1 | async-start | bytes 1179648 | tf_op jit(solution)/shard_map/all_to_all | solution.py:589
  31.3 0.0 copy-done.2
  31.3 14.7 %solve.2.refs_0_ = bf16[32,72,128]{2,1,0:T(8,128)(2,1)} custom-call(bf16[32,72,128]{2,1,0:T(8,128)(2,1)} %copy-done.2), custom_call_target="tpu_custom_call" | custom-call | flops 1920000000 | bytes 1920000 | tf_op jit(solution)/shard_map/solve/pallas_call | solution.py:342
  46.0 1.8 %all-to-all-done.1.refs_1_ = bf16[32,72,128]{2,1,0:T(8,128)(2,1)S(1)} async-done(((bf16[32,72,128]{2,1,0:T(8,128)(2,1)}), bf16[32,72,128]{2,1,0:T(8,128)(2,1)S(1)}, u32[]{:S(2)}, u32[]{:S(2)}) %all-to-all-start.1) | async-done | bytes 589856 | tf_op jit(solution)/shard_map/all_to_all | solution.py:589
  47.9 0.0 copy-start
  47.9 0.8 %copy-done = bf16[32,72,128]{2,1,0:T(8,128)(2,1)} copy-done((bf16[32,72,128]{2,1,0:T(8,128)(2,1)}, bf16[32,72,128]{2,1,0:T(8,128)(2,1)S(1)}, u32[]{:S(2)}) %copy-start) | copy-done | bytes 589848
  48.7 3.4 %merge.1 = (bf16[64,72,128]{2,1,0:T(8,128)(2,1)}, bf16[8,72,128]{2,1,0:T(8,128)(2,1)}, bf16[8,72,128]{2,1,0:T(8,128)(2,1)}, bf16[1,72,128]{2,1,0:T(8,128)(2,1)}) custom-call(bf16[32,72,128]{2,1,0:T(8,128)(2,1)} %solve.2.refs_0_, bf16[32,72,128]{2,1,0:T(8,128)(2,1)} %copy-done), custom_call_target="tpu_custom_call" | custom-call | tf_op jit(solution)/shard_map/merge/pallas_call | solution.py:385
  52.1 0.5 collective-permute-start
  52.6 1.3 %collective-permute-start.1 = (bf16[8,72,128]{2,1,0:T(8,128)(2,1)}, bf16[8,72,128]{2,1,0:T(8,128)(2,1)S(1)}, u32[]{:S(2)}, u32[]{:S(2)}) collective-permute-start(bf16[8,72,128]{2,1,0:T(8,128)(2,1)} %get-tuple-element.12), channel_id=1, source_target_pairs={{8,0},{16,8},{24,16},{9,1},{17,9},{25,17},{10,2},{18,10},{26,18},{... | collective-permute-start | bytes 442376 | tf_op jit(solution)/shard_map/ppermute | solution.py:598
  53.9 1.3 %collective-permute-start.2 = (bf16[1,72,128]{2,1,0:T(8,128)(2,1)}, bf16[1,72,128]{2,1,0:T(8,128)(2,1)S(1)}, u32[]{:S(2)}, u32[]{:S(2)}) collective-permute-start(bf16[1,72,128]{2,1,0:T(8,128)(2,1)} %get-tuple-element.13), channel_id=1, source_target_pairs={{8,7},{9,0},{10,1},{11,2},{12,3},{13,4},{14,5},{15,6},{16,15},{17,... | collective-permute-start | bytes 55304 | tf_op jit(solution)/shard_map/ppermute | solution.py:599
  55.2 5.9 %collective-permute-done.2.corner = bf16[1,72,128]{2,1,0:T(8,128)(2,1)S(1)} collective-permute-done((bf16[1,72,128]{2,1,0:T(8,128)(2,1)}, bf16[1,72,128]{2,1,0:T(8,128)(2,1)S(1)}, u32[]{:S(2)}, u32[]{:S(2)}) %collective-permute-start.2) | collective-permute-done | bytes 18464 | tf_op jit(solution)/shard_map/ppermute | solution.py:599
  61.2 0.0 copy-start.4
  61.2 0.0 collective-permute-done.east.next_east.far_east
  61.2 0.0 copy-start.1
  61.2 0.0 collective-permute-done.1.north
  61.2 0.0 copy-start.3
  61.2 0.6 copy-done.4
  61.8 0.1 copy-done.1
  61.9 0.0 copy-done.3
  61.9 17.6 %apply.1 = (bf16[1,200,200,128]{3,2,1,0:T(8,128)(2,1)}, f32[1,200,200]{2,1,0:T(8,128)}) custom-call(s32[1]{0:T(128)} %bitcast.top, bf16[64,72,128]{2,1,0:T(8,128)(2,1)} %get-tuple-element.10.own.next_own.far_own, bf16[8,72,128]{2,1,0:T(8,128)(2,1)} %copy-done.1, bf16[64,72,128]{2,1,0:T(8,128)(2,1)} %get-tuple-element.10.own.next_own.far_own, ...), custom_call_target="tpu_custom_call" | custom-call | tf_op jit(solution)/shard_map/apply/pallas_call | solution.py:540
Async XLA Ops:
  3.7 23.6 %all-to-all-start = ((bf16[32,72,128]{2,1,0:T(8,128)(2,1)}), bf16[32,72,128]{2,1,0:T(8,128)(2,1)S(1)}, u32[]{:S(2)}, u32[]{:S(2)}) async-start(bf16[32,72,128]{2,1,0:T(8,128)(2,1)} %get-tuple-element.8), calls=%async_computation | async-start | bytes 1179648 | tf_op jit(solution)/shard_map/all_to_all | solution.py:587
  27.3 4.0 %copy-start.2 = (bf16[32,72,128]{2,1,0:T(8,128)(2,1)}, bf16[32,72,128]{2,1,0:T(8,128)(2,1)S(1)}, u32[]{:S(2)}) copy-start(bf16[32,72,128]{2,1,0:T(8,128)(2,1)S(1)} %all-to-all-done.arrived) | copy-start | bytes 1769476
  27.3 20.5 %all-to-all-start.1 = ((bf16[32,72,128]{2,1,0:T(8,128)(2,1)}), bf16[32,72,128]{2,1,0:T(8,128)(2,1)S(1)}, u32[]{:S(2)}, u32[]{:S(2)}) async-start(bf16[32,72,128]{2,1,0:T(8,128)(2,1)} %solve.3), calls=%async_computation.1 | async-start | bytes 1179648 | tf_op jit(solution)/shard_map/all_to_all | solution.py:589
  47.9 0.8 %copy-start = (bf16[32,72,128]{2,1,0:T(8,128)(2,1)}, bf16[32,72,128]{2,1,0:T(8,128)(2,1)S(1)}, u32[]{:S(2)}) copy-start(bf16[32,72,128]{2,1,0:T(8,128)(2,1)S(1)} %all-to-all-done.1.refs_1_) | copy-start | bytes 1769476
  52.1 9.1 %collective-permute-start = (bf16[8,72,128]{2,1,0:T(8,128)(2,1)}, bf16[8,72,128]{2,1,0:T(8,128)(2,1)S(1)}, u32[]{:S(2)}, u32[]{:S(2)}) collective-permute-start(bf16[8,72,128]{2,1,0:T(8,128)(2,1)} %get-tuple-element.11), channel_id=1, source_target_pairs={{0,7},{1,0},{2,1},{3,2},{4,3},{5,4},{6,5},{7,6},{8,15},{9,8},{10,9... | collective-permute-start | bytes 442376 | tf_op jit(solution)/shard_map/ppermute | solution.py:600
  52.6 8.5 %collective-permute-start.1 = (bf16[8,72,128]{2,1,0:T(8,128)(2,1)}, bf16[8,72,128]{2,1,0:T(8,128)(2,1)S(1)}, u32[]{:S(2)}, u32[]{:S(2)}) collective-permute-start(bf16[8,72,128]{2,1,0:T(8,128)(2,1)} %get-tuple-element.12), channel_id=1, source_target_pairs={{8,0},{16,8},{24,16},{9,1},{17,9},{25,17},{10,2},{18,10},{26,18},{... | collective-permute-start | bytes 442376 | tf_op jit(solution)/shard_map/ppermute | solution.py:598
  53.9 7.3 %collective-permute-start.2 = (bf16[1,72,128]{2,1,0:T(8,128)(2,1)}, bf16[1,72,128]{2,1,0:T(8,128)(2,1)S(1)}, u32[]{:S(2)}, u32[]{:S(2)}) collective-permute-start(bf16[1,72,128]{2,1,0:T(8,128)(2,1)} %get-tuple-element.13), channel_id=1, source_target_pairs={{8,7},{9,0},{10,1},{11,2},{12,3},{13,4},{14,5},{15,6},{16,15},{17,... | collective-permute-start | bytes 55304 | tf_op jit(solution)/shard_map/ppermute | solution.py:599
  61.2 0.6 copy-start.4
  61.2 0.7 copy-start.1
  61.2 0.7 copy-start.3
